TPU v7x, 256 devices: a whole 4x4x8 slice. The times are simulated.
256 devices in a mesh: case: 4 (over x), tile: 64 (over z, y, core).
Axes of the slice: x: 4, y: 4, z: 8, core: 2. Of those that a mesh axis runs over, the one named last changes fastest.
Arguments:
- forcing: bfloat16 [4, 1024, 512, 128], P('case', 'tile'), may hold values from -6 to 6
- permeability: float32 [4, 1024, 512], P('case', 'tile'), may hold values from 0.05 to 1
- merge_weights: int32 [4], P('case'), may hold values from 4 to 6
- start_codes: int32 [2, 256, 128], replicated, may hold values from -7 to 7
Outputs:
- basis: bfloat16 [4, 524288, 128], P('case', 'tile')
All inputs are finite; a program needn't handle non-finite values.
Results may differ from a plain program's by a relative error of at most 0.018.
Values may be sent and summed in bfloat16 or wider, within the bound.
No kernel may reach another device: no remote copies, remote signals or barrier semaphores. Data moves between devices by JAX's collectives and lax.ppermute only.
A program may use at most 64 MiB of HBM per device.

v0:
```python
import functools
import math

import jax
import jax.numpy as jnp
from jax import lax
from jax.experimental import pallas as pl
from jax.experimental.pallas import tpu as pltpu
from jax.sharding import PartitionSpec as P

STEPS = 3


def at(z, y, core):
    return (z * 4 + y) * 2 + core


PLANES = [[at(z, y, core) for z in range(8) for y in range(4)] for core in range(2)]


def case_swap(value, apart):
    return lax.ppermute(value, "case", [(source, source ^ apart) for source in range(4)])


def core_swap(value):
    return lax.ppermute(value, "tile", [(source, source ^ 1) for source in range(64)])


def plane_exchange(value):
    return lax.all_to_all(value, "tile", 0, 0, axis_index_groups=PLANES)


def edges(cells, width):
    head, tail = cells[:width], cells[cells.shape[0] - width :]
    up = [(i, i + 1) for i in range(63)]
    down = [(i + 1, i) for i in range(63)]
    return lax.ppermute(tail, "tile", up), lax.ppermute(head, "tile", down)


AB = (((1,), (0,)), ((), ()))
ATB = (((0,), (0,)), ((), ()))
ABT = (((1,), (1,)), ((), ()))


def parts_of(x, exact=False):
    high = x.astype(jnp.bfloat16)
    if exact:
        return (high,)
    rest = x - high.astype(jnp.float32)
    mid = rest.astype(jnp.bfloat16)
    low = (rest - mid.astype(jnp.float32)).astype(jnp.bfloat16)
    return (high, mid, low)


def product(a, b, dims=AB):
    out = None
    for i in range(len(a) - 1, -1, -1):
        for j in range(len(b) - 1, -1, -1):
            if i + j < 3:
                term = lax.dot_general(a[i], b[j], dims, preferred_element_type=jnp.float32)
                out = term if out is None else out + term
    return out


def spread(x, axis, index, size):
    piece = lax.slice_in_dim(x, index, index + 1, axis=axis)
    shape = (size, x.shape[1]) if axis == 0 else (x.shape[0], size)
    return jnp.broadcast_to(piece, shape)


def inverse_factors(mats):
    lane = lax.broadcasted_iota(jnp.int32, (8, 128), 1)
    sub = lax.broadcasted_iota(jnp.int32, (8, 128), 0)
    tiles = [[m[8 * b : 8 * b + 8] for b in range(16)] for m in mats]
    for k in range(16):
        first = 8 * k
        block = (lane >= first) & (lane < first + 8)
        for a in tiles:
            rows = [spread(a[k], 0, r, 8) for r in range(8)]
            piv = [
                [spread(rows[r], 1, first + s, 128) if s >= r else None for s in range(8)]
                for r in range(8)
            ]
            inv = [None] * 8
            mul = [[None] * 8 for _ in range(8)]
            for r in range(8):
                inv[r] = 1.0 / piv[r][r]
                for s in range(r + 1, 8):
                    mul[r][s] = piv[r][s] * inv[r]
                for s in range(r + 1, 8):
                    for t in range(s, 8):
                        piv[s][t] = piv[s][t] - mul[r][s] * piv[r][t]
            for s in range(8):
                rows[s] = jnp.where(block, jnp.where(lane == first + s, 1.0, 0.0), rows[s])
            for s in range(8):
                for r in range(s):
                    rows[s] = rows[s] - mul[r][s] * rows[r]
            scaled = [rows[r] * inv[r] for r in range(8)]
            for b in range(k + 1, 16):
                col = [spread(a[b], 1, first + r, 128) for r in range(8)]
                for r in range(8):
                    for s in range(r + 1, 8):
                        col[s] = col[s] - col[r] * mul[r][s]
                new = jnp.where(block, 0.0, a[b])
                for r in range(8):
                    new = new - col[r] * scaled[r]
                a[b] = new
            done = jnp.zeros((8, 128), jnp.float32)
            for r in range(8):
                done = jnp.where(sub == r, rows[r] * lax.rsqrt(piv[r][r]), done)
            a[k] = jnp.where(lane < first + 8, done, 0.0)
    return [jnp.concatenate(a, 0) for a in tiles]


def mixing(cells, me_ref, core_ref, own_ref, other_ref, start_ref, high_ref, low_ref, gram_ref):
    me, core = me_ref[0], core_ref[0]
    for side in (0, 1):

        @pl.when(core == side)
        def _(side=side):
            for half, ref in enumerate((own_ref, other_ref) if side == 0 else (other_ref, own_ref)):
                rows = ref[:, 0:16].reshape(4, 128, 128)
                for i in range(4):
                    gram_ref[5 * half + i] = rows[i]
                for k in range(32):
                    gram_ref[5 * half + 4, 4 * k : 4 * k + 4] = ref[k, 16:20]

    odd = lax.rem(me, 2) == 1
    upper = me // 2

    def side(index, flip):
        x = gram_ref[index]
        return jnp.where(flip, x.T, x)

    def merged(coeff_parts, gram_parts):
        t = product(gram_parts, coeff_parts)
        return product(coeff_parts, parts_of(t), ATB)

    start = parts_of(start_ref[0].astype(jnp.float32), True)
    coeffs, inners = [], []
    for half in (0, 1):
        a, b = me ^ (2 * half), me ^ (2 * half + 1)
        near = side(4 + (upper ^ half), odd)
        gram = jnp.concatenate(
            [jnp.concatenate([gram_ref[a], near], 1), jnp.concatenate([near.T, gram_ref[b]], 1)], 0
        )
        gram = parts_of(gram)
        first = product(gram, start) / cells
        second = product(gram, parts_of(first)) / cells
        coeff = (second.astype(jnp.bfloat16),)
        coeffs.append(coeff)
        inners.append(merged(coeff, gram))
    inverse = inverse_factors(inners)
    scale = math.sqrt(cells)
    maps = [scale * product(c, parts_of(v), ABT) for c, v in zip(coeffs, inverse)]
    maps = [parts_of(m) for m in maps]
    low_group = upper == 0
    rows = []
    for e in (0, 1):
        line = []
        for f in (2, 3):
            a, b = me ^ e, me ^ f
            index = jnp.where(low_group, 6 + 2 * a + (b - 2), 6 + 2 * b + (a - 2))
            line.append(side(index, upper == 1))
        rows.append(jnp.concatenate(line, 1))
    across = parts_of(jnp.concatenate(rows, 0))
    cross = product(maps[0], parts_of(product(across, maps[1])), ATB)
    cross = parts_of(cross / cells)
    start = start_ref[1].astype(jnp.float32)
    top, bottom = start[:128], start[128:]
    exact = True
    for _ in range(2):
        top, bottom = (
            top + product(cross, parts_of(bottom, exact)),
            bottom + product(cross, parts_of(top, exact), ATB),
        )
        exact = False
    top, bottom = (top.astype(jnp.bfloat16),), (bottom.astype(jnp.bfloat16),)
    mixed = product(top, parts_of(product(cross, bottom)), ATB)
    inner = product(top, top, ATB) + product(bottom, bottom, ATB) + mixed + mixed.T
    (last,) = inverse_factors([inner])
    last = parts_of(last)
    for half, coeff in enumerate((top, bottom)):
        step = product(coeff, last, ABT)
        final = product(maps[half], parts_of(step))
        high = final.astype(jnp.bfloat16)
        high_ref[pl.ds(256 * half, 256), :] = high
        low_ref[pl.ds(256 * half, 256), :] = (final - high.astype(jnp.float32)).astype(jnp.bfloat16)


NY, LANES, PAD = 512, 128, 8
HALO = 3
EXT = 16 + 2 * HALO
GROUP = 128


def diffuse(me_ref, tile_ref, scale_ref, own_ref, low_ref, high_ref, kp_ref, kp_low_ref, kp_high_ref, *rest):
    outs, (first, second, east, north, perm_ref) = rest[:6], rest[6:]
    me, tile = me_ref[0], tile_ref[0]
    zero_pad = jnp.zeros((PAD, LANES), jnp.float32)

    def fill(source, base, count):
        def one(i, _):
            first[base + i, PAD : PAD + NY] = source[i].astype(jnp.float32)
            return 0

        lax.fori_loop(0, count, one, 0)

    def clear(i, _):
        for buf in (first, second):
            buf[i, 0:PAD] = zero_pad
            buf[i, PAD + NY : PAD + NY + PAD] = zero_pad
        return 0

    lax.fori_loop(0, EXT, clear, 0)
    fill(low_ref, 0, HALO)
    fill(own_ref, HALO, 16)
    fill(high_ref, HALO + 16, HALO)

    rows = jnp.concatenate(
        [kp_low_ref[...], kp_ref[...], kp_high_ref[...], jnp.zeros((LANES - EXT, NY), jnp.float32)], 0
    )
    perm_ref[0:PAD] = zero_pad
    perm_ref[PAD : PAD + NY] = rows.T
    perm_ref[PAD + NY : PAD + NY + PAD] = zero_pad

    def spread_rows(g, _):
        at0 = pl.multiple_of(g * 8, 8)
        here = perm_ref[pl.ds(at0, 8)]
        after = perm_ref[pl.ds(at0 + 8, 8)]
        sub = lax.broadcasted_iota(jnp.int32, (8, LANES), 0)
        shifted = pltpu.roll(jnp.where(sub == 0, after, here), 7, axis=0)
        e = 0.12 * (here + shifted)
        n = 0.12 * (here + pltpu.roll(here, LANES - 1, axis=1))
        for i in range(EXT):
            if 1 <= i < EXT - 1:
                east[i, pl.ds(at0, 8)] = jnp.broadcast_to(e[:, i : i + 1], (8, LANES))
            if i < EXT - 1:
                north[i, pl.ds(at0, 8)] = jnp.broadcast_to(n[:, i : i + 1], (8, LANES))
        return 0

    lax.fori_loop(0, (PAD + NY) // 8, spread_rows, 0, unroll=5)

    def sweep(source, begin, count, write):
        for g in range(NY // GROUP):
            c = PAD + g * GROUP
            here = pl.ds(c, GROUP)

            def one(i, carry):
                row = begin + i
                center, south = carry
                above = source[row + 1, c : c + GROUP]
                up = north[row, c : c + GROUP] * (above - center)
                flux = up - south
                flux = flux + east[row, c : c + GROUP] * (source[row, c + 1 : c + GROUP + 1] - center)
                flux = flux + east[row, c - 1 : c + GROUP - 1] * (source[row, c - 1 : c + GROUP - 1] - center)
                write(row, c, center + flux)
                return above, up

            center = source[begin, c : c + GROUP]
            south = north[begin - 1, c : c + GROUP] * (center - source[begin - 1, c : c + GROUP])
            lax.fori_loop(0, count, one, (center, south))

    def store_to(buf):
        def write(row, c, value):
            buf[row, c : c + GROUP] = value

        return write

    def blank(buf, rows):
        for row in rows:
            buf[row, PAD : PAD + NY] = jnp.zeros((NY, LANES), jnp.float32)

    sweep(first, 1, EXT - 2, store_to(second))

    @pl.when(tile == 0)
    def _():
        blank(second, (1, 2))

    @pl.when(tile == 63)
    def _():
        blank(second, (EXT - 3, EXT - 2))

    sweep(second, 2, EXT - 4, store_to(first))

    @pl.when(tile == 0)
    def _():
        blank(first, (2,))

    @pl.when(tile == 63)
    def _():
        blank(first, (EXT - 3,))

    scale = jnp.sqrt(scale_ref[0].astype(jnp.float32) * jnp.ones((8, LANES), jnp.float32))
    scale = jnp.broadcast_to(scale[0:1], (GROUP, LANES))
    for j in range(4):
        begin = HALO + 4 * (me ^ j)

        def write(row, c, value, j=j, begin=begin):
            at0 = pl.multiple_of((row - begin) * NY + (c - PAD), GROUP)
            value = (value * scale).astype(jnp.bfloat16)
            outs[j][pl.ds(at0, GROUP)] = value
            outs[4 + j // 2][pl.ds(at0 + (j % 2) * 4 * NY, GROUP)] = value

        sweep(first, begin, 4, write)


def diffuse_call(me, tile, weights, own, low, high, kp, kp_low, kp_high):
    vmem = pl.BlockSpec(memory_space=pltpu.VMEM)
    smem = pl.BlockSpec(memory_space=pltpu.SMEM)
    big = pltpu.VMEM((EXT, PAD + NY + PAD, LANES), jnp.float32)
    shapes = [jax.ShapeDtypeStruct((2048, LANES), jnp.bfloat16)] * 4
    shapes += [jax.ShapeDtypeStruct((4096, LANES), jnp.bfloat16)] * 2
    return pl.pallas_call(
        diffuse,
        out_shape=shapes,
        in_specs=[smem] * 3 + [vmem] * 6,
        out_specs=[vmem] * 6,
        scratch_shapes=[big, big, big, big, pltpu.VMEM((PAD + NY + PAD, LANES), jnp.float32)],
        compiler_params=pltpu.CompilerParams(vmem_limit_bytes=52 << 20),
        cost_estimate=pl.CostEstimate(flops=40 << 20, bytes_accessed=8 << 20, transcendentals=0),
    )(me, tile, weights, own, low, high, kp, kp_low, kp_high)


def grams(me_ref, core_ref, *refs):
    pieces, own_ref, other_ref, wide = refs[:4], refs[4], refs[5], refs[6]
    me, core = me_ref[0], core_ref[0]
    for e in range(4):
        lanes = pl.ds(pl.multiple_of((me ^ e) * 128, 128), 128)
        wide[:, lanes] = pieces[e][...]
    left, right = wide[:, :256], wide[:, 256:]
    near = lax.dot_general(left, left, ATB, preferred_element_type=jnp.float32)
    far = lax.dot_general(right, right, ATB, preferred_element_type=jnp.float32)
    cross = lax.dot_general(left, right, ATB, preferred_element_type=jnp.float32)
    blocks = [
        near[:128, :128], near[128:, 128:], far[:128, :128], far[128:, 128:], near[:128, 128:],
        far[:128, 128:], cross[:128, :128], cross[:128, 128:], cross[128:, :128], cross[128:, 128:],
    ]
    for side in (0, 1):

        @pl.when(core == side)
        def _(side=side):
            for half, ref in enumerate((own_ref, other_ref) if side == 0 else (other_ref, own_ref)):
                mine = blocks[5 * half : 5 * half + 5]
                ref[:, 0:16] = jnp.concatenate(mine[:4], 0).reshape(32, 16, 128)
                ref[:, 16:24] = jnp.zeros((32, 8, 128), jnp.float32)
                for k in range(32):
                    ref[k, 16:20] = mine[4][4 * k : 4 * k + 4]


def grams_call(me, core, pieces):
    vmem = pl.BlockSpec(memory_space=pltpu.VMEM)
    smem = pl.BlockSpec(memory_space=pltpu.SMEM)
    shape = jax.ShapeDtypeStruct((32, 24, 128), jnp.float32)
    return pl.pallas_call(
        grams,
        out_shape=(shape, shape),
        in_specs=[smem, smem] + [vmem] * 4,
        out_specs=(vmem, vmem),
        scratch_shapes=[pltpu.VMEM((2048, 512), jnp.bfloat16)],
        compiler_params=pltpu.CompilerParams(vmem_limit_bytes=24 << 20),
        cost_estimate=pl.CostEstimate(flops=2 * 2048 * 512 * 512, bytes_accessed=3 << 20, transcendentals=0),
    )(me, core, *pieces)


def mixing_call(cells, me, core, own, other, start_codes):
    shape = jax.ShapeDtypeStruct((512, 128), jnp.bfloat16)
    vmem = pl.BlockSpec(memory_space=pltpu.VMEM)
    smem = pl.BlockSpec(memory_space=pltpu.SMEM)
    return pl.pallas_call(
        functools.partial(mixing, cells),
        out_shape=(shape, shape),
        in_specs=[smem, smem, vmem, vmem, vmem],
        out_specs=(vmem, vmem),
        scratch_shapes=[pltpu.VMEM((10, 128, 128), jnp.float32)],
        cost_estimate=pl.CostEstimate(flops=1 << 30, bytes_accessed=1 << 20, transcendentals=0),
    )(me, core, own, other, start_codes)


def finish(where, me_ref, high_ref, low_ref, *refs):
    pieces, out_ref = refs[:-5], refs[-5]
    wide, done, in_sem, out_sem = refs[-4:]
    me = me_ref[0]
    loads = []
    for j in range(4):
        for e in range(4):
            index, begin = where[4 * j + e]
            copy = pltpu.make_async_copy(
                pieces[index].at[pl.ds(begin, 2048)],
                wide.at[j, :, pl.ds(128 * e, 128)],
                in_sem.at[4 * j + e],
            )
            copy.start()
            loads.append(copy)
    mix = jnp.concatenate([high_ref[...], low_ref[...]], 1)
    stores = []
    for j in range(4):
        for e in range(4):
            loads[4 * j + e].wait()
        for r in range(0, 2048, 512):
            both = jnp.dot(wide[j, r : r + 512], mix, preferred_element_type=jnp.float32)
            done[j, r : r + 512] = (both[:, :128] + both[:, 128:]).astype(jnp.bfloat16)
        target = pl.multiple_of((me ^ j) * 2048, 2048)
        copy = pltpu.make_async_copy(done.at[j], out_ref.at[pl.ds(target, 2048)], out_sem.at[j])
        copy.start()
        stores.append(copy)
    for copy in stores:
        copy.wait()


def finish_call(me, high, low, pieces, where):
    vmem = pl.BlockSpec(memory_space=pltpu.VMEM)
    anywhere = pl.BlockSpec(memory_space=pl.ANY)
    return pl.pallas_call(
        functools.partial(finish, where),
        out_shape=jax.ShapeDtypeStruct((8192, 128), jnp.bfloat16),
        in_specs=[pl.BlockSpec(memory_space=pltpu.SMEM), vmem, vmem] + [anywhere] * len(pieces),
        out_specs=anywhere,
        scratch_shapes=[
            pltpu.VMEM((4, 2048, 512), jnp.bfloat16),
            pltpu.VMEM((4, 2048, 128), jnp.bfloat16),
            pltpu.SemaphoreType.DMA((16,)),
            pltpu.SemaphoreType.DMA((4,)),
        ],
        compiler_params=pltpu.CompilerParams(vmem_limit_bytes=24 << 20),
        cost_estimate=pl.CostEstimate(flops=2 * 8192 * 512 * 256, bytes_accessed=10 << 20, transcendentals=0),
    )(me, high, low, *pieces)


def merged_bases(forcing, permeability, merge_weights, start_codes):
    me = lax.axis_index("case").astype(jnp.int32).reshape(1)
    tile = lax.axis_index("tile").astype(jnp.int32).reshape(1)
    core = tile % 2
    cells = forcing.shape[1] * lax.axis_size("tile") * forcing.shape[2]
    low, high = edges(forcing[0], STEPS)
    kp_low, kp_high = edges(permeability[0], STEPS)
    *snap, front, back = diffuse_call(
        me, tile, merge_weights, forcing[0], low, high, permeability[0], kp_low, kp_high
    )
    met = [snap[0]] + [case_swap(snap[e], e) for e in (1, 2, 3)]
    next_piece = {e: case_swap(snap[e ^ 1], e) for e in (1, 2, 3)}
    own, other = grams_call(me, core, met)
    part = own + core_swap(other)
    part = plane_exchange(part).sum(0)
    part = part + case_swap(part, 1) + case_swap(part, 2) + case_swap(part, 3)
    last_pieces = {1: case_swap(back, 1), 2: case_swap(front, 2), 3: case_swap(front, 3)}
    own = plane_exchange(jnp.broadcast_to(part, (32,) + part.shape))
    other = core_swap(own)
    high, low = mixing_call(cells, me, core, own, other, start_codes)
    pieces = snap + met[1:] + [next_piece[e] for e in (1, 2, 3)] + [last_pieces[e] for e in (1, 2, 3)]
    where = []
    for j in range(4):
        for e in range(4):
            if e == 0:
                where.append((j, 0))
            elif j == 0:
                where.append((3 + e, 0))
            elif j == 1:
                where.append((6 + e, 0))
            else:
                where.append((9 + e, ((e ^ j) % 2) * 2048))
    return finish_call(me, high, low, pieces, tuple(where))[None]


def solution(mesh):
    placed = (P("case", "tile", None, None), P("case", "tile", None), P("case"), P())
    return jax.shard_map(
        merged_bases, mesh=mesh, in_specs=placed, out_specs=P("case", "tile", None), check_vma=False
    )
```

profile of v0, /device:TPU:8, one launch (start us, length us, event | category | flops | bytes accessed | tf_op | source)
XLA Modules:
  0.0 193.5 jit_solution(17960719972600973134)
XLA Ops:
  0.0 1.2 slice_bitcast_fusion
  1.2 1.9 collective-permute-start.1
  3.1 2.4 %collective-permute-start = (bf16[3,512,128]{2,1,0:T(8,128)(2,1)S(1)}, bf16[3,512,128]{2,1,0:T(8,128)(2,1)S(1)}, u32[]{:S(2)}, u32[]{:S(2)}) collective-permute-start(bf16[3,512,128]{2,1,0:T(8,128)(2,1)S(1)} %get-tuple-element.26), channel_id=1, source_target_pairs={{0,1},{1,2},{2,3},{3,4},{4,5},{5,6},{6,7},{7,8},{8,9},{9,10},{10,1... | collective-permute-start | bytes 1179656 | tf_op jit(solution)/shard_map/ppermute | solution.py:37
  6.3 3.7 %collective-permute-start.3 = (f32[3,512]{1,0:T(4,128)S(1)}, f32[3,512]{1,0:T(4,128)S(1)}, u32[]{:S(2)}, u32[]{:S(2)}) collective-permute-start(f32[3,512]{1,0:T(4,128)S(1)} %get-tuple-element.27), channel_id=1, source_target_pairs={{1,0},{2,1},{3,2},{4,3},{5,4},{6,5},{7,6},{8,7},{9,8},{10,9},{11,1... | collective-permute-start | bytes 18440 | tf_op jit(solution)/shard_map/ppermute | solution.py:37
  9.9 1.9 collective-permute-start.2
  12.5 2.4 %collective-permute-done.2.kp_low_ref = f32[3,512]{1,0:T(4,128)S(1)} collective-permute-done((f32[3,512]{1,0:T(4,128)S(1)}, f32[3,512]{1,0:T(4,128)S(1)}, u32[]{:S(2)}, u32[]{:S(2)}) %collective-permute-start.2) | collective-permute-done | bytes 6176 | tf_op jit(solution)/shard_map/ppermute | solution.py:37
  15.7 20.2 %shard_map.46 = (bf16[2048,128]{1,0:T(8,128)(2,1)}, bf16[2048,128]{1,0:T(8,128)(2,1)S(1)}, bf16[2048,128]{1,0:T(8,128)(2,1)}, bf16[2048,128]{1,0:T(8,128)(2,1)},...) custom-call(s32[1]{0:T(128)} %bitcast.me_ref, s32[1]{0:T(128)} %bitcast.1.tile_ref, s32[1]{0:T(128)S(6)} %copy.5.scale_ref, ...), custom_call_target="tpu_custom_call" | custom-call | flops 41943040 | bytes 8388608 | tf_op jit(solution)/shard_map/pallas_call | solution.py:314
  36.8 2.7 %collective-permute-start.5 = (bf16[2048,128]{1,0:T(8,128)(2,1)}, bf16[2048,128]{1,0:T(8,128)(2,1)S(1)}, u32[]{:S(2)}, u32[]{:S(2)}) collective-permute-start(bf16[2048,128]{1,0:T(8,128)(2,1)} %get-tuple-element.17.refs_2_), channel_id=1, source_target_pairs={{0,128},{64,192},{128,0},{192,64},{1,129},{65,193},{129,1},{193,65... | collective-permute-start | bytes 1572872 | tf_op jit(solution)/shard_map/ppermute | solution.py:22
  40.6 10.1 %collective-permute-done.4.refs_1_.refs_4_ = bf16[2048,128]{1,0:T(8,128)(2,1)S(1)} collective-permute-done((bf16[2048,128]{1,0:T(8,128)(2,1)S(1)}, bf16[2048,128]{1,0:T(8,128)(2,1)S(1)}, u32[]{:S(2)}, u32[]{:S(2)}) %collective-permute-start.4) | collective-permute-done | bytes 524320 | tf_op jit(solution)/shard_map/ppermute | solution.py:22
  50.7 11.4 %collective-permute-done.5.refs_2_.refs_5_ = bf16[2048,128]{1,0:T(8,128)(2,1)S(1)} collective-permute-done((bf16[2048,128]{1,0:T(8,128)(2,1)}, bf16[2048,128]{1,0:T(8,128)(2,1)S(1)}, u32[]{:S(2)}, u32[]{:S(2)}) %collective-permute-start.5) | collective-permute-done | bytes 524320 | tf_op jit(solution)/shard_map/ppermute | solution.py:22
  62.1 2.8 %collective-permute-done.6.refs_3_.refs_6_ = bf16[2048,128]{1,0:T(8,128)(2,1)S(1)} collective-permute-done((bf16[2048,128]{1,0:T(8,128)(2,1)}, bf16[2048,128]{1,0:T(8,128)(2,1)S(1)}, u32[]{:S(2)}, u32[]{:S(2)}) %collective-permute-start.6) | collective-permute-done | bytes 524320 | tf_op jit(solution)/shard_map/ppermute | solution.py:22
  64.9 2.8 %shard_map.47 = (f32[32,24,128]{2,1,0:T(8,128)S(1)}, f32[32,24,128]{2,1,0:T(8,128)S(1)}) custom-call(s32[1]{0:T(128)} %bitcast.me_ref, s32[1]{0:T(128)S(6)} %select_n.7.core_ref, bf16[2048,128]{1,0:T(8,128)(2,1)} %get-tuple-element.15.refs_0_, bf16[2048,128]{1,0:T(8,128)(2,1)S(1)} %collective-permute-done.4.refs_1_.refs_4_, ...), custom_call_target="tpu_custom_call" | custom-call | flops 1073741824 | bytes 3145728 | tf_op jit(solution)/shard_map/pallas_call | solution.py:355
  67.8 1.7 collective-permute-done.7
  69.6 27.6 %all_to_all.10 = f32[32,24,128]{2,1,0:T(8,128)S(1)} all-to-all(f32[32,24,128]{2,1,0:T(8,128)S(1)} %add.19), channel_id=1, replica_groups={{0,2,4,6,8,10,12,14,16,18,20,22,24,26,28,30,32,34,36,38,40,42,44,46,48,..., dimensions={0} | all-to-all | bytes 786432 | tf_op jit(solution)/shard_map/all_to_all | solution.py:30
  98.4 3.0 %collective-permute-start.8 = (f32[24,128]{1,0:T(8,128)S(1)}, f32[24,128]{1,0:T(8,128)S(1)}, u32[]{:S(2)}, u32[]{:S(2)}) collective-permute-start(f32[24,128]{1,0:T(8,128)S(1)} %reduce_sum.9), channel_id=1, source_target_pairs={{0,64},{64,0},{128,192},{192,128},{1,65},{65,1},{129,193},{193,129... | collective-permute-start | bytes 36872 | tf_op jit(solution)/shard_map/ppermute | solution.py:22
  104.0 5.6 %all-to-all-start.1 = ((f32[32,24,128]{2,1,0:T(8,128)}), f32[32,24,128]{2,1,0:T(8,128)S(1)}, u32[]{:S(2)}, u32[]{:S(2)}) async-start(f32[32,24,128]{2,1,0:T(8,128)} %broadcast_in_dim.6), calls=%async_computation.1 | async-start | bytes 786432 | tf_op jit(solution)/shard_map/all_to_all | solution.py:30
  109.6 2.0 %collective-permute-start.12 = (bf16[2048,128]{1,0:T(8,128)(2,1)}, bf16[2048,128]{1,0:T(8,128)(2,1)}, u32[]{:S(2)}, u32[]{:S(2)}) collective-permute-start(bf16[2048,128]{1,0:T(8,128)(2,1)} %get-tuple-element.15.refs_0_), channel_id=1, source_target_pairs={{0,64},{64,0},{128,192},{192,128},{1,65},{65,1},{129,193},{193,129... | collective-permute-start | bytes 1572872 | tf_op jit(solution)/shard_map/ppermute | solution.py:22
  111.7 2.5 %collective-permute-start.17 = (bf16[4096,128]{1,0:T(8,128)(2,1)}, bf16[4096,128]{1,0:T(8,128)(2,1)S(1)}, u32[]{:S(2)}, u32[]{:S(2)}) collective-permute-start(bf16[4096,128]{1,0:T(8,128)(2,1)} %get-tuple-element.24), channel_id=1, source_target_pairs={{0,192},{64,128},{128,64},{192,0},{1,193},{65,129},{129,65},{193,1... | collective-permute-start | bytes 3145736 | tf_op jit(solution)/shard_map/ppermute | solution.py:22
  114.3 1.4 collective-permute-start.16
  115.7 6.1 %all-to-all-done.1.own_ref = f32[32,24,128]{2,1,0:T(8,128)S(1)} async-done(((f32[32,24,128]{2,1,0:T(8,128)}), f32[32,24,128]{2,1,0:T(8,128)S(1)}, u32[]{:S(2)}, u32[]{:S(2)}) %all-to-all-start.1) | async-done | bytes 393248 | tf_op jit(solution)/shard_map/all_to_all | solution.py:30
  121.8 3.0 %collective-permute-done.12.refs_7_ = bf16[2048,128]{1,0:T(8,128)(2,1)} collective-permute-done((bf16[2048,128]{1,0:T(8,128)(2,1)}, bf16[2048,128]{1,0:T(8,128)(2,1)}, u32[]{:S(2)}, u32[]{:S(2)}) %collective-permute-start.12) | collective-permute-done | bytes 524320 | tf_op jit(solution)/shard_map/ppermute | solution.py:22
  124.8 2.5 %collective-permute-start.14 = (bf16[2048,128]{1,0:T(8,128)(2,1)}, bf16[2048,128]{1,0:T(8,128)(2,1)}, u32[]{:S(2)}, u32[]{:S(2)}) collective-permute-start(bf16[2048,128]{1,0:T(8,128)(2,1)} %get-tuple-element.17.refs_2_), channel_id=1, source_target_pairs={{0,192},{64,128},{128,64},{192,0},{1,193},{65,129},{129,65},{193,1... | collective-permute-start | bytes 1572872 | tf_op jit(solution)/shard_map/ppermute | solution.py:22
  128.1 1.4 collective-permute-start.13
  129.6 16.5 %shard_map.48 = (bf16[512,128]{1,0:T(8,128)(2,1)}, bf16[512,128]{1,0:T(8,128)(2,1)}) custom-call(s32[1]{0:T(128)} %bitcast.me_ref, s32[1]{0:T(128)S(6)} %select_n.7.core_ref, f32[32,24,128]{2,1,0:T(8,128)} %copy-done.13, f32[32,24,128]{2,1,0:T(8,128)} %copy-done.14, s32[2,256,128]{2,1,0:T(8,128)} %start_ref.1), custom_call_target="tpu_custom_call" | custom-call | flops 1073741824 | bytes 1048576 | tf_op jit(solution)/shard_map/pallas_call | solution.py:370
  146.0 34.1 %collective-permute-done.14.refs_9_ = bf16[2048,128]{1,0:T(8,128)(2,1)} collective-permute-done((bf16[2048,128]{1,0:T(8,128)(2,1)}, bf16[2048,128]{1,0:T(8,128)(2,1)}, u32[]{:S(2)}, u32[]{:S(2)}) %collective-permute-start.14) | collective-permute-done | bytes 524320 | tf_op jit(solution)/shard_map/ppermute | solution.py:22
  180.1 1.0 copy-done.1
  181.2 1.0 copy-done.2
  182.2 1.0 copy-done.3
  183.3 1.0 copy-done.5
  184.3 1.0 copy-done.7
  185.4 1.0 copy-done.9
  188.2 5.2 %shard_map.49 = bf16[8192,128]{1,0:T(8,128)(2,1)} custom-call(s32[1]{0:T(128)} %bitcast.me_ref, bf16[512,128]{1,0:T(8,128)(2,1)S(1)} %copy-done.10, bf16[512,128]{1,0:T(8,128)(2,1)S(1)} %copy-done.11, bf16[2048,128]{1,0:T(8,128)(2,1)} %get-tuple-element.15.refs_0_, bf16[2048,128]{1,0:T(8,128)(2,1)S(1)} %copy-done.1, bf16[2048,128]{1,0:T(8,128)(2,1)S(1)} %copy-done.2, ...), custom_call_target="tpu_custom_call" | custom-call | flops 2147483648 | bytes 10485760 | tf_op jit(solution)/shard_map/pallas_call | solution.py:414
  (47 shorter events, 10.2 us)
Async XLA Ops:
  1.2 13.7 %collective-permute-start.1 = (bf16[3,512,128]{2,1,0:T(8,128)(2,1)S(1)}, bf16[3,512,128]{2,1,0:T(8,128)(2,1)S(1)}, u32[]{:S(2)}, u32[]{:S(2)}) collective-permute-start(bf16[3,512,128]{2,1,0:T(8,128)(2,1)S(1)} %get-tuple-element.25), channel_id=1, source_target_pairs={{1,0},{2,1},{3,2},{4,3},{5,4},{6,5},{7,6},{8,7},{9,8},{10,9},{11,1... | collective-permute-start | bytes 1179656 | tf_op jit(solution)/shard_map/ppermute | solution.py:37
  3.1 11.8 %collective-permute-start = (bf16[3,512,128]{2,1,0:T(8,128)(2,1)S(1)}, bf16[3,512,128]{2,1,0:T(8,128)(2,1)S(1)}, u32[]{:S(2)}, u32[]{:S(2)}) collective-permute-start(bf16[3,512,128]{2,1,0:T(8,128)(2,1)S(1)} %get-tuple-element.26), channel_id=1, source_target_pairs={{0,1},{1,2},{2,3},{3,4},{4,5},{5,6},{6,7},{7,8},{8,9},{9,10},{10,1... | collective-permute-start | bytes 1179656 | tf_op jit(solution)/shard_map/ppermute | solution.py:37
  6.3 6.3 %collective-permute-start.3 = (f32[3,512]{1,0:T(4,128)S(1)}, f32[3,512]{1,0:T(4,128)S(1)}, u32[]{:S(2)}, u32[]{:S(2)}) collective-permute-start(f32[3,512]{1,0:T(4,128)S(1)} %get-tuple-element.27), channel_id=1, source_target_pairs={{1,0},{2,1},{3,2},{4,3},{5,4},{6,5},{7,6},{8,7},{9,8},{10,9},{11,1... | collective-permute-start | bytes 18440 | tf_op jit(solution)/shard_map/ppermute | solution.py:37
  9.9 5.0 %collective-permute-start.2 = (f32[3,512]{1,0:T(4,128)S(1)}, f32[3,512]{1,0:T(4,128)S(1)}, u32[]{:S(2)}, u32[]{:S(2)}) collective-permute-start(f32[3,512]{1,0:T(4,128)S(1)} %get-tuple-element.28), channel_id=1, source_target_pairs={{0,1},{1,2},{2,3},{3,4},{4,5},{5,6},{6,7},{7,8},{8,9},{9,10},{10,1... | collective-permute-start | bytes 18440 | tf_op jit(solution)/shard_map/ppermute | solution.py:37
  35.9 33.7 %copy-start = (bf16[2048,128]{1,0:T(8,128)(2,1)}, bf16[2048,128]{1,0:T(8,128)(2,1)S(1)}, u32[]{:S(2)}) copy-start(bf16[2048,128]{1,0:T(8,128)(2,1)S(1)} %get-tuple-element.16.refs_1_) | copy-start | bytes 1572868
  35.9 14.8 %collective-permute-start.4 = (bf16[2048,128]{1,0:T(8,128)(2,1)S(1)}, bf16[2048,128]{1,0:T(8,128)(2,1)S(1)}, u32[]{:S(2)}, u32[]{:S(2)}) collective-permute-start(bf16[2048,128]{1,0:T(8,128)(2,1)S(1)} %get-tuple-element.16.refs_1_), channel_id=1, source_target_pairs={{0,64},{64,0},{128,192},{192,128},{1,65},{65,1},{129,193},{193,129... | collective-permute-start | bytes 1572872 | tf_op jit(solution)/shard_map/ppermute | solution.py:22
  36.8 25.3 %collective-permute-start.5 = (bf16[2048,128]{1,0:T(8,128)(2,1)}, bf16[2048,128]{1,0:T(8,128)(2,1)S(1)}, u32[]{:S(2)}, u32[]{:S(2)}) collective-permute-start(bf16[2048,128]{1,0:T(8,128)(2,1)} %get-tuple-element.17.refs_2_), channel_id=1, source_target_pairs={{0,128},{64,192},{128,0},{192,64},{1,129},{65,193},{129,1},{193,65... | collective-permute-start | bytes 1572872 | tf_op jit(solution)/shard_map/ppermute | solution.py:22
  39.6 25.3 %collective-permute-start.6 = (bf16[2048,128]{1,0:T(8,128)(2,1)}, bf16[2048,128]{1,0:T(8,128)(2,1)S(1)}, u32[]{:S(2)}, u32[]{:S(2)}) collective-permute-start(bf16[2048,128]{1,0:T(8,128)(2,1)} %get-tuple-element.18.refs_3_), channel_id=1, source_target_pairs={{0,192},{64,128},{128,64},{192,0},{1,193},{65,129},{129,65},{193,1... | collective-permute-start | bytes 1572872 | tf_op jit(solution)/shard_map/ppermute | solution.py:22
  50.7 18.9 %copy-start.4 = (bf16[2048,128]{1,0:T(8,128)(2,1)}, bf16[2048,128]{1,0:T(8,128)(2,1)S(1)}, u32[]{:S(2)}) copy-start(bf16[2048,128]{1,0:T(8,128)(2,1)S(1)} %collective-permute-done.4.refs_1_.refs_4_) | copy-start | bytes 1572868
  62.1 7.5 %copy-start.6 = (bf16[2048,128]{1,0:T(8,128)(2,1)}, bf16[2048,128]{1,0:T(8,128)(2,1)S(1)}, u32[]{:S(2)}) copy-start(bf16[2048,128]{1,0:T(8,128)(2,1)S(1)} %collective-permute-done.5.refs_2_.refs_5_) | copy-start | bytes 1572868
  64.9 4.7 %copy-start.8 = (bf16[2048,128]{1,0:T(8,128)(2,1)}, bf16[2048,128]{1,0:T(8,128)(2,1)S(1)}, u32[]{:S(2)}) copy-start(bf16[2048,128]{1,0:T(8,128)(2,1)S(1)} %collective-permute-done.6.refs_3_.refs_6_) | copy-start | bytes 1572868
  67.7 1.8 collective-permute-start.7
  97.3 5.0 %collective-permute-start.10 = (f32[24,128]{1,0:T(8,128)S(1)}, f32[24,128]{1,0:T(8,128)S(1)}, u32[]{:S(2)}, u32[]{:S(2)}) collective-permute-start(f32[24,128]{1,0:T(8,128)S(1)} %reduce_sum.9), channel_id=1, source_target_pairs={{0,192},{64,128},{128,64},{192,0},{1,193},{65,129},{129,65},{193,1... | collective-permute-start | bytes 36872 | tf_op jit(solution)/shard_map/ppermute | solution.py:22
  97.8 5.2 %collective-permute-start.9 = (f32[24,128]{1,0:T(8,128)S(1)}, f32[24,128]{1,0:T(8,128)S(1)}, u32[]{:S(2)}, u32[]{:S(2)}) collective-permute-start(f32[24,128]{1,0:T(8,128)S(1)} %reduce_sum.9), channel_id=1, source_target_pairs={{0,128},{64,192},{128,0},{192,64},{1,129},{65,193},{129,1},{193,65... | collective-permute-start | bytes 36872 | tf_op jit(solution)/shard_map/ppermute | solution.py:22
  98.4 4.8 %collective-permute-start.8 = (f32[24,128]{1,0:T(8,128)S(1)}, f32[24,128]{1,0:T(8,128)S(1)}, u32[]{:S(2)}, u32[]{:S(2)}) collective-permute-start(f32[24,128]{1,0:T(8,128)S(1)} %reduce_sum.9), channel_id=1, source_target_pairs={{0,64},{64,0},{128,192},{192,128},{1,65},{65,1},{129,193},{193,129... | collective-permute-start | bytes 36872 | tf_op jit(solution)/shard_map/ppermute | solution.py:22
  104.0 17.7 %all-to-all-start.1 = ((f32[32,24,128]{2,1,0:T(8,128)}), f32[32,24,128]{2,1,0:T(8,128)S(1)}, u32[]{:S(2)}, u32[]{:S(2)}) async-start(f32[32,24,128]{2,1,0:T(8,128)} %broadcast_in_dim.6), calls=%async_computation.1 | async-start | bytes 786432 | tf_op jit(solution)/shard_map/all_to_all | solution.py:30
  109.6 15.2 %collective-permute-start.12 = (bf16[2048,128]{1,0:T(8,128)(2,1)}, bf16[2048,128]{1,0:T(8,128)(2,1)}, u32[]{:S(2)}, u32[]{:S(2)}) collective-permute-start(bf16[2048,128]{1,0:T(8,128)(2,1)} %get-tuple-element.15.refs_0_), channel_id=1, source_target_pairs={{0,64},{64,0},{128,192},{192,128},{1,65},{65,1},{129,193},{193,129... | collective-permute-start | bytes 1572872 | tf_op jit(solution)/shard_map/ppermute | solution.py:22
  111.6 68.5 %collective-permute-start.15 = (bf16[4096,128]{1,0:T(8,128)(2,1)}, bf16[4096,128]{1,0:T(8,128)(2,1)S(1)}, u32[]{:S(2)}, u32[]{:S(2)}) collective-permute-start(bf16[4096,128]{1,0:T(8,128)(2,1)} %get-tuple-element.23), channel_id=1, source_target_pairs={{0,64},{64,0},{128,192},{192,128},{1,65},{65,1},{129,193},{193,129... | collective-permute-start | bytes 3145736 | tf_op jit(solution)/shard_map/ppermute | solution.py:22
  111.7 68.4 %collective-permute-start.17 = (bf16[4096,128]{1,0:T(8,128)(2,1)}, bf16[4096,128]{1,0:T(8,128)(2,1)S(1)}, u32[]{:S(2)}, u32[]{:S(2)}) collective-permute-start(bf16[4096,128]{1,0:T(8,128)(2,1)} %get-tuple-element.24), channel_id=1, source_target_pairs={{0,192},{64,128},{128,64},{192,0},{1,193},{65,129},{129,65},{193,1... | collective-permute-start | bytes 3145736 | tf_op jit(solution)/shard_map/ppermute | solution.py:22
  114.3 65.9 %collective-permute-start.16 = (bf16[4096,128]{1,0:T(8,128)(2,1)}, bf16[4096,128]{1,0:T(8,128)(2,1)S(1)}, u32[]{:S(2)}, u32[]{:S(2)}) collective-permute-start(bf16[4096,128]{1,0:T(8,128)(2,1)} %get-tuple-element.24), channel_id=1, source_target_pairs={{0,128},{64,192},{128,0},{192,64},{1,129},{65,193},{129,1},{193,65... | collective-permute-start | bytes 3145736 | tf_op jit(solution)/shard_map/ppermute | solution.py:22
  121.8 7.8 %copy-start.13 = (f32[32,24,128]{2,1,0:T(8,128)}, f32[32,24,128]{2,1,0:T(8,128)S(1)}, u32[]{:S(2)}) copy-start(f32[32,24,128]{2,1,0:T(8,128)S(1)} %all-to-all-done.1.own_ref) | copy-start | bytes 1179652
  121.8 5.6 %collective-permute-start.11 = (f32[32,24,128]{2,1,0:T(8,128)S(1)}, f32[32,24,128]{2,1,0:T(8,128)S(1)}, u32[]{:S(2)}, u32[]{:S(2)}) collective-permute-start(f32[32,24,128]{2,1,0:T(8,128)S(1)} %all-to-all-done.1.own_ref), channel_id=1, source_target_pairs={{0,1},{1,0},{2,3},{3,2},{4,5},{5,4},{6,7},{7,6},{8,9},{9,8},{10,11... | collective-permute-start | bytes 1179656 | tf_op jit(solution)/shard_map/ppermute | solution.py:26
  124.8 55.3 %collective-permute-start.14 = (bf16[2048,128]{1,0:T(8,128)(2,1)}, bf16[2048,128]{1,0:T(8,128)(2,1)}, u32[]{:S(2)}, u32[]{:S(2)}) collective-permute-start(bf16[2048,128]{1,0:T(8,128)(2,1)} %get-tuple-element.17.refs_2_), channel_id=1, source_target_pairs={{0,192},{64,128},{128,64},{192,0},{1,193},{65,129},{129,65},{193,1... | collective-permute-start | bytes 1572872 | tf_op jit(solution)/shard_map/ppermute | solution.py:22
  128.1 52.0 %collective-permute-start.13 = (bf16[2048,128]{1,0:T(8,128)(2,1)}, bf16[2048,128]{1,0:T(8,128)(2,1)}, u32[]{:S(2)}, u32[]{:S(2)}) collective-permute-start(bf16[2048,128]{1,0:T(8,128)(2,1)} %get-tuple-element.18.refs_3_), channel_id=1, source_target_pairs={{0,128},{64,192},{128,0},{192,64},{1,129},{65,193},{129,1},{193,65... | collective-permute-start | bytes 1572872 | tf_op jit(solution)/shard_map/ppermute | solution.py:22
  180.1 1.0 copy-start.1
  181.2 1.0 copy-start.2
  182.2 1.0 copy-start.3
  183.3 1.0 copy-start.5
  184.3 1.0 copy-start.7
  185.3 1.0 copy-start.9
  186.4 0.9 copy-start.10
  187.3 0.9 copy-start.11
  (2 other events, 1.5 us)
where the time goes:
time: 194 us
  waiting for transfers between devices  73.4 us (38%)
  Pallas kernels  44.6 us (23%)
  starting transfers between devices  34.5 us (18%)
  blocking collectives  27.6 us (14%)
  local copies, waits for them, and re-layouts  12.3 us (6%)
    ppermute x12, waiting for transfers between devices, case_swap(): lax.ppermute(value, 'case', [(source, source ^ apart) for source in range...  63.2 us
    all_to_all x1, blocking collectives, plane_exchange(): return lax.all_to_all(value, 'tile', 0, 0, axis_index_groups=PLANES)  27.6 us
    pallas_call x1, Pallas kernels, diffuse_call(): pl.pallas_call(diffuse, out_shape=shapes, in_specs=[smem] * 3 + [vmem] *...  20.2 us
    ppermute x12, starting transfers between devices, case_swap(): lax.ppermute(value, 'case', [(source, source ^ apart) for source in range...  18.9 us
    pallas_call x1, Pallas kernels, mixing_call(): pl.pallas_call(functools.partial(mixing, cells), out_shape=(shape, shape)...  16.5 us
    ppermute x4, starting transfers between devices, edges(): return (lax.ppermute(tail, 'tile', up), lax.ppermute(head, 'tile', down))  9.92 us
    unnamed x30, local copies, waits for them, and re-layouts  9.58 us
    all_to_all x1, waiting for transfers between devices, plane_exchange(): return lax.all_to_all(value, 'tile', 0, 0, axis_index_groups=PLANES)  6.08 us
  transfers between devices with their start and end apart: 19, of which 11 were waited for; matrix products, arithmetic and copies ran while one was open for 0% of the time, Pallas kernels for 9%

commit v1 on v0

v1 whole, which is shorter than its diff:
```python
import functools
import math

import jax
import jax.numpy as jnp
from jax import lax
from jax.experimental import pallas as pl
from jax.experimental.pallas import tpu as pltpu
from jax.sharding import PartitionSpec as P

STEPS = 3


def at(z, y, core):
    return (z * 4 + y) * 2 + core


PLANES = [[at(z, y, core) for z in range(8) for y in range(4)] for core in range(2)]


def case_swap(value, apart):
    return lax.ppermute(value, "case", [(source, source ^ apart) for source in range(4)])


def core_swap(value):
    return lax.ppermute(value, "tile", [(source, source ^ 1) for source in range(64)])


def plane_exchange(value):
    return lax.all_to_all(value, "tile", 0, 0, axis_index_groups=PLANES)


AB = (((1,), (0,)), ((), ()))
ATB = (((0,), (0,)), ((), ()))
ABT = (((1,), (1,)), ((), ()))


def parts_of(x, exact=False):
    high = x.astype(jnp.bfloat16)
    if exact:
        return (high,)
    rest = x - high.astype(jnp.float32)
    mid = rest.astype(jnp.bfloat16)
    low = (rest - mid.astype(jnp.float32)).astype(jnp.bfloat16)
    return (high, mid, low)


def product(a, b, dims=AB):
    out = None
    for i in range(len(a) - 1, -1, -1):
        for j in range(len(b) - 1, -1, -1):
            if i + j < 3:
                term = lax.dot_general(a[i], b[j], dims, preferred_element_type=jnp.float32)
                out = term if out is None else out + term
    return out


def spread(x, axis, index, size):
    piece = lax.slice_in_dim(x, index, index + 1, axis=axis)
    shape = (size, x.shape[1]) if axis == 0 else (x.shape[0], size)
    return jnp.broadcast_to(piece, shape)


def inverse_factors(mats):
    lane = lax.broadcasted_iota(jnp.int32, (8, 128), 1)
    sub = lax.broadcasted_iota(jnp.int32, (8, 128), 0)
    tiles = [[m[8 * b : 8 * b + 8] for b in range(16)] for m in mats]
    for k in range(16):
        first = 8 * k
        block = (lane >= first) & (lane < first + 8)
        for a in tiles:
            rows = [spread(a[k], 0, r, 8) for r in range(8)]
            piv = [
                [spread(rows[r], 1, first + s, 128) if s >= r else None for s in range(8)]
                for r in range(8)
            ]
            inv = [None] * 8
            mul = [[None] * 8 for _ in range(8)]
            for r in range(8):
                inv[r] = 1.0 / piv[r][r]
                for s in range(r + 1, 8):
                    mul[r][s] = piv[r][s] * inv[r]
                for s in range(r + 1, 8):
                    for t in range(s, 8):
                        piv[s][t] = piv[s][t] - mul[r][s] * piv[r][t]
            for s in range(8):
                rows[s] = jnp.where(block, jnp.where(lane == first + s, 1.0, 0.0), rows[s])
            for s in range(8):
                for r in range(s):
                    rows[s] = rows[s] - mul[r][s] * rows[r]
            scaled = [rows[r] * inv[r] for r in range(8)]
            for b in range(k + 1, 16):
                col = [spread(a[b], 1, first + r, 128) for r in range(8)]
                for r in range(8):
                    for s in range(r + 1, 8):
                        col[s] = col[s] - col[r] * mul[r][s]
                new = jnp.where(block, 0.0, a[b])
                for r in range(8):
                    new = new - col[r] * scaled[r]
                a[b] = new
            done = jnp.zeros((8, 128), jnp.float32)
            for r in range(8):
                done = jnp.where(sub == r, rows[r] * lax.rsqrt(piv[r][r]), done)
            a[k] = jnp.where(lane < first + 8, done, 0.0)
    return [jnp.concatenate(a, 0) for a in tiles]


def mixing(cells, me_ref, core_ref, own_hbm, other_hbm, start_ref, high_ref, low_ref, *scratch):
    gram_ref, own_ref, other_ref, sems = scratch
    me, core = me_ref[0], core_ref[0]
    loads = [
        pltpu.make_async_copy(own_hbm, own_ref, sems.at[0]),
        pltpu.make_async_copy(other_hbm, other_ref, sems.at[1]),
    ]
    for copy in loads:
        copy.start()
    for copy in loads:
        copy.wait()
    for side in (0, 1):

        @pl.when(core == side)
        def _(side=side):
            for half, ref in enumerate((own_ref, other_ref) if side == 0 else (other_ref, own_ref)):
                rows = ref[:, 0:16].reshape(4, 128, 128)
                for i in range(4):
                    gram_ref[5 * half + i] = rows[i]
                for k in range(32):
                    gram_ref[5 * half + 4, 4 * k : 4 * k + 4] = ref[k, 16:20]

    odd = lax.rem(me, 2) == 1
    upper = me // 2

    def side(index, flip):
        x = gram_ref[index]
        return jnp.where(flip, x.T, x)

    def merged(coeff_parts, gram_parts):
        t = product(gram_parts, coeff_parts)
        return product(coeff_parts, parts_of(t), ATB)

    start = parts_of(start_ref[0].astype(jnp.float32), True)
    coeffs, inners = [], []
    for half in (0, 1):
        a, b = me ^ (2 * half), me ^ (2 * half + 1)
        near = side(4 + (upper ^ half), odd)
        gram = jnp.concatenate(
            [jnp.concatenate([gram_ref[a], near], 1), jnp.concatenate([near.T, gram_ref[b]], 1)], 0
        )
        gram = parts_of(gram)
        first = product(gram, start) / cells
        second = product(gram, parts_of(first)) / cells
        coeff = (second.astype(jnp.bfloat16),)
        coeffs.append(coeff)
        inners.append(merged(coeff, gram))
    inverse = inverse_factors(inners)
    scale = math.sqrt(cells)
    maps = [scale * product(c, parts_of(v), ABT) for c, v in zip(coeffs, inverse)]
    maps = [parts_of(m) for m in maps]
    low_group = upper == 0
    rows = []
    for e in (0, 1):
        line = []
        for f in (2, 3):
            a, b = me ^ e, me ^ f
            index = jnp.where(low_group, 6 + 2 * a + (b - 2), 6 + 2 * b + (a - 2))
            line.append(side(index, upper == 1))
        rows.append(jnp.concatenate(line, 1))
    across = parts_of(jnp.concatenate(rows, 0))
    cross = product(maps[0], parts_of(product(across, maps[1])), ATB)
    cross = parts_of(cross / cells)
    start = start_ref[1].astype(jnp.float32)
    top, bottom = start[:128], start[128:]
    exact = True
    for _ in range(2):
        top, bottom = (
            top + product(cross, parts_of(bottom, exact)),
            bottom + product(cross, parts_of(top, exact), ATB),
        )
        exact = False
    top, bottom = (top.astype(jnp.bfloat16),), (bottom.astype(jnp.bfloat16),)
    mixed = product(top, parts_of(product(cross, bottom)), ATB)
    inner = product(top, top, ATB) + product(bottom, bottom, ATB) + mixed + mixed.T
    (last,) = inverse_factors([inner])
    last = parts_of(last)
    for half, coeff in enumerate((top, bottom)):
        step = product(coeff, last, ABT)
        final = product(maps[half], parts_of(step))
        high = final.astype(jnp.bfloat16)
        high_ref[pl.ds(256 * half, 256), :] = high
        low_ref[pl.ds(256 * half, 256), :] = (final - high.astype(jnp.float32)).astype(jnp.bfloat16)


NY, LANES, PAD = 512, 128, 8
WIDE = PAD + NY + PAD
GROUP = 128
INNER, OUTER = 10 * GROUP, 6 * GROUP
PIECE = INNER + OUTER


def spread_faces(perm_ref, east, north, count):
    def one(g, _):
        at0 = pl.multiple_of(g * 8, 8)
        here = perm_ref[pl.ds(at0, 8)]
        after = perm_ref[pl.ds(at0 + 8, 8)]
        sub = lax.broadcasted_iota(jnp.int32, (8, LANES), 0)
        shifted = pltpu.roll(jnp.where(sub == 0, after, here), 7, axis=0)
        e = 0.12 * (here + shifted)
        n = 0.12 * (here + pltpu.roll(here, LANES - 1, axis=1))
        for i in range(count):
            east[i, pl.ds(at0, 8)] = jnp.broadcast_to(e[:, i : i + 1], (8, LANES))
            north[i, pl.ds(at0, 8)] = jnp.broadcast_to(n[:, i : i + 1], (8, LANES))
        return 0

    lax.fori_loop(0, (PAD + NY) // 8, one, 0, unroll=5)


def set_perm(perm_ref, rows):
    count = rows.shape[0]
    rows = jnp.concatenate([rows, jnp.zeros((LANES - count, NY), jnp.float32)], 0)
    perm_ref[0:PAD] = jnp.zeros((PAD, LANES), jnp.float32)
    perm_ref[PAD : PAD + NY] = rows.T
    perm_ref[PAD + NY : WIDE] = jnp.zeros((PAD, LANES), jnp.float32)


def clear_pads(buf, count):
    def one(i, _):
        buf[i, 0:PAD] = jnp.zeros((PAD, LANES), jnp.float32)
        buf[i, PAD + NY : WIDE] = jnp.zeros((PAD, LANES), jnp.float32)
        return 0

    lax.fori_loop(0, count, one, 0)


def sweep(source, east, north, begin, face, count, write):
    for g in range(NY // GROUP):
        c = PAD + g * GROUP

        def one(i, carry, c=c, g=g):
            row, plane = begin + i, face + i
            center, south = carry
            above = source[row + 1, c : c + GROUP]
            up = north[plane, c : c + GROUP] * (above - center)
            flux = up - south
            flux = flux + east[plane, c : c + GROUP] * (source[row, c + 1 : c + GROUP + 1] - center)
            flux = flux + east[plane, c - 1 : c + GROUP - 1] * (source[row, c - 1 : c + GROUP - 1] - center)
            write(i, g, center + flux)
            return above, up

        center = source[begin, c : c + GROUP]
        south = north[face - 1, c : c + GROUP] * (center - source[begin - 1, c : c + GROUP])
        lax.fori_loop(0, count, one, (center, south))


def into(buf, base):
    def write(i, g, value):
        buf[base + i, PAD + g * GROUP : PAD + g * GROUP + GROUP] = value

    return write


def into_snap(snap, base, scale_ref):
    scale = jnp.sqrt(jnp.full((8, LANES), scale_ref[0].astype(jnp.float32)))
    scale = jnp.broadcast_to(scale[0:1], (GROUP, LANES))

    def write(i, g, value):
        at0 = pl.multiple_of((base + i) * GROUP, GROUP)
        snap[g, pl.ds(at0, GROUP)] = (value * scale).astype(jnp.bfloat16)

    return write


def send_out(me, snap, singles, stacks, begin, size, sems):
    copies = []
    for e in (1, 2, 3):
        copies.append(pltpu.make_async_copy(snap.at[me ^ e], singles[e - 1], sems.at[len(copies)]))
        for j in (1, 2, 3):
            target = stacks[e - 1].at[pl.ds(PIECE * (j - 1) + begin, size)]
            copies.append(pltpu.make_async_copy(snap.at[me ^ e ^ j], target, sems.at[len(copies)]))
    for copy in copies:
        copy.start()
    return copies


def inner_rows(me_ref, scale_ref, own_ref, kp_ref, *refs):
    singles, stacks, edge_one, edge_two = refs[:3], refs[3:6], refs[6], refs[7]
    first, second, east, north, perm_ref, snap, held, sems, edge_sems = refs[8:]
    me = me_ref[0]
    load = pltpu.make_async_copy(own_ref, held, sems.at[0])
    load.start()
    clear_pads(first, 16)
    clear_pads(second, 16)

    def fill(i, _):
        first[i, PAD : PAD + NY] = held[i].astype(jnp.float32)
        return 0

    set_perm(perm_ref, kp_ref[...])
    spread_faces(perm_ref, east, north, 15)
    load.wait()
    lax.fori_loop(0, 16, fill, 0)
    sweep(first, east, north, 1, 1, 14, into(second, 1))
    sweep(second, east, north, 2, 2, 12, into(first, 2))
    edges_out = [
        pltpu.make_async_copy(second.at[pl.ds(1, 2)], edge_one.at[pl.ds(0, 2)], edge_sems.at[0]),
        pltpu.make_async_copy(second.at[pl.ds(13, 2)], edge_one.at[pl.ds(2, 2)], edge_sems.at[1]),
        pltpu.make_async_copy(first.at[pl.ds(2, 2)], edge_two.at[pl.ds(0, 2)], edge_sems.at[2]),
        pltpu.make_async_copy(first.at[pl.ds(12, 2)], edge_two.at[pl.ds(2, 2)], edge_sems.at[3]),
    ]
    for copy in edges_out:
        copy.start()
    sweep(first, east, north, 3, 3, 10, into_snap(snap, 0, scale_ref))
    for copy in edges_out + send_out(me, snap, singles, stacks, 0, INNER, sems):
        copy.wait()


def outer_rows(me_ref, tile_ref, scale_ref, own_hbm, kp_ref, low_hbm, high_hbm, edge_one, edge_two, *refs):
    singles, stacks = refs[3:6], refs[6:9]
    low0, low1, low2, high0, high1, high2, east, north, perm_ref, snap = refs[9:19]
    low_ref, high_ref, own_ref, sems, edge_sems = refs[19:]
    me, tile = me_ref[0], tile_ref[0]
    loads = [
        pltpu.make_async_copy(low_hbm, low_ref, sems.at[0]),
        pltpu.make_async_copy(high_hbm, high_ref, sems.at[1]),
        pltpu.make_async_copy(own_hbm.at[pl.ds(0, 2)], own_ref.at[pl.ds(0, 2)], sems.at[2]),
        pltpu.make_async_copy(own_hbm.at[pl.ds(14, 2)], own_ref.at[pl.ds(2, 2)], sems.at[3]),
    ]
    for copy in loads:
        copy.start()
    edges_in = [
        pltpu.make_async_copy(edge_one.at[pl.ds(0, 2)], low1.at[pl.ds(3, 2)], edge_sems.at[0]),
        pltpu.make_async_copy(edge_one.at[pl.ds(2, 2)], high1.at[pl.ds(0, 2)], edge_sems.at[1]),
        pltpu.make_async_copy(edge_two.at[pl.ds(0, 2)], low2.at[pl.ds(3, 2)], edge_sems.at[2]),
        pltpu.make_async_copy(edge_two.at[pl.ds(2, 2)], high2.at[pl.ds(0, 2)], edge_sems.at[3]),
    ]
    for copy in edges_in:
        copy.start()
    for buf in (low0, high0):
        clear_pads(buf, 5)
    for buf in (low1, low2):
        clear_pads(buf, 3)
    for buf in (high1, high2):
        clear_pads(buf.at[pl.ds(2, 3)], 3)
    for copy in loads:
        copy.wait()
    for i in range(3):
        low0[i, PAD : PAD + NY] = low_ref[NY * i : NY * i + NY].astype(jnp.float32)
        high0[2 + i, PAD : PAD + NY] = high_ref[NY * i : NY * i + NY].astype(jnp.float32)
    for i in range(2):
        low0[3 + i, PAD : PAD + NY] = own_ref[i].astype(jnp.float32)
        high0[i, PAD : PAD + NY] = own_ref[2 + i].astype(jnp.float32)

    def far_perm(ref):
        both = ref[3 * NY : 3 * NY + 32].astype(jnp.float32)
        packed = both[0:12] + both[12:24]
        return [
            jnp.concatenate([packed[4 * i + q : 4 * i + q + 1] for q in range(4)], 1) for i in range(3)
        ]

    kp = kp_ref[...]
    set_perm(perm_ref, jnp.concatenate(far_perm(low_ref) + [kp[0:4], kp[12:16]] + far_perm(high_ref), 0))
    spread_faces(perm_ref, east, north, 13)
    sweep(low0, east, north, 1, 1, 3, into(low1, 0))
    sweep(high0, east, north, 1, 10, 3, into(high1, 2))
    blank = jnp.zeros((NY, LANES), jnp.float32)

    @pl.when(tile == 0)
    def _():
        low1[0, PAD : PAD + NY] = blank
        low1[1, PAD : PAD + NY] = blank

    @pl.when(tile == 63)
    def _():
        high1[3, PAD : PAD + NY] = blank
        high1[4, PAD : PAD + NY] = blank

    for copy in edges_in:
        copy.wait()
    sweep(low1, east, north, 1, 2, 3, into(low2, 0))
    sweep(high1, east, north, 1, 9, 3, into(high2, 2))

    @pl.when(tile == 0)
    def _():
        low2[0, PAD : PAD + NY] = blank

    @pl.when(tile == 63)
    def _():
        high2[4, PAD : PAD + NY] = blank

    sweep(low2, east, north, 1, 3, 3, into_snap(snap, 0, scale_ref))
    sweep(high2, east, north, 1, 8, 3, into_snap(snap, 3, scale_ref))
    for copy in send_out(me, snap, singles, stacks, INNER, OUTER, sems):
        copy.wait()


VM = pl.BlockSpec(memory_space=pltpu.VMEM)
SM = pl.BlockSpec(memory_space=pltpu.SMEM)
ANY = pl.BlockSpec(memory_space=pl.ANY)


def half(rows):
    return jax.ShapeDtypeStruct((rows, LANES), jnp.bfloat16)


def planes(count):
    return pltpu.VMEM((count, WIDE, LANES), jnp.float32)


def inner_call(me, weights, own, kp):
    edge = jax.ShapeDtypeStruct((4, WIDE, LANES), jnp.float32)
    return pl.pallas_call(
        inner_rows,
        out_shape=[half(INNER)] * 3 + [half(3 * PIECE)] * 3 + [edge] * 2,
        in_specs=[SM, SM, ANY, VM],
        out_specs=[ANY] * 8,
        scratch_shapes=[planes(16), planes(16), planes(15), planes(15)]
        + [pltpu.VMEM((WIDE, LANES), jnp.float32), pltpu.VMEM((4, INNER, LANES), jnp.bfloat16)]
        + [pltpu.VMEM((16, NY, LANES), jnp.bfloat16)]
        + [pltpu.SemaphoreType.DMA((12,)), pltpu.SemaphoreType.DMA((4,))],
        compiler_params=pltpu.CompilerParams(vmem_limit_bytes=63 << 20),
        cost_estimate=pl.CostEstimate(flops=400 << 20, bytes_accessed=9 << 20, transcendentals=0),
    )(me, weights, own, kp)


def outer_call(me, tile, weights, own, kp, low, high, edge_one, edge_two, stacks):
    return pl.pallas_call(
        outer_rows,
        out_shape=[half(OUTER)] * 3 + [half(3 * PIECE)] * 3,
        in_specs=[SM, SM, SM, ANY, VM] + [ANY] * 7,
        out_specs=[ANY] * 6,
        input_output_aliases={9: 3, 10: 4, 11: 5},
        scratch_shapes=[planes(5)] * 6
        + [planes(13), planes(13), pltpu.VMEM((WIDE, LANES), jnp.float32)]
        + [pltpu.VMEM((4, OUTER, LANES), jnp.bfloat16)]
        + [pltpu.VMEM((3 * NY + 32, LANES), jnp.bfloat16)] * 2
        + [pltpu.VMEM((4, NY, LANES), jnp.bfloat16)]
        + [pltpu.SemaphoreType.DMA((12,)), pltpu.SemaphoreType.DMA((4,))],
        compiler_params=pltpu.CompilerParams(vmem_limit_bytes=63 << 20),
        cost_estimate=pl.CostEstimate(flops=200 << 20, bytes_accessed=9 << 20, transcendentals=0),
    )(me, tile, weights, own, kp, low, high, edge_one, edge_two, *stacks)


def grams(me_ref, core_ref, *refs):
    pieces, own_ref, other_ref, wide, sems = refs[:7], refs[7], refs[8], refs[9], refs[10]
    me, core = me_ref[0], core_ref[0]
    copies = []
    for e in range(4):
        lanes = pl.ds(pl.multiple_of((me ^ e) * 128, 128), 128)
        if e == 0:
            moves = [(pieces[0].at[pl.ds(0, PIECE)], 0, PIECE)]
        else:
            moves = [(pieces[e], 0, INNER), (pieces[3 + e], INNER, OUTER)]
        for source, begin, size in moves:
            target = wide.at[pl.ds(begin, size), lanes]
            copies.append(pltpu.make_async_copy(source, target, sems.at[len(copies)]))
    for copy in copies:
        copy.start()
    for copy in copies:
        copy.wait()
    left, right = wide[:, :256], wide[:, 256:]
    near = lax.dot_general(left, left, ATB, preferred_element_type=jnp.float32)
    far = lax.dot_general(right, right, ATB, preferred_element_type=jnp.float32)
    cross = lax.dot_general(left, right, ATB, preferred_element_type=jnp.float32)
    blocks = [
        near[:128, :128], near[128:, 128:], far[:128, :128], far[128:, 128:], near[:128, 128:],
        far[:128, 128:], cross[:128, :128], cross[:128, 128:], cross[128:, :128], cross[128:, 128:],
    ]
    for side in (0, 1):

        @pl.when(core == side)
        def _(side=side):
            for half, ref in enumerate((own_ref, other_ref) if side == 0 else (other_ref, own_ref)):
                mine = blocks[5 * half : 5 * half + 5]
                ref[:, 0:16] = jnp.concatenate(mine[:4], 0).reshape(32, 16, 128)
                ref[:, 16:24] = jnp.zeros((32, 8, 128), jnp.float32)
                for k in range(32):
                    ref[k, 16:20] = mine[4][4 * k : 4 * k + 4]


def grams_call(me, core, pieces):
    shape = jax.ShapeDtypeStruct((32, 24, 128), jnp.float32)
    return pl.pallas_call(
        grams,
        out_shape=(shape, shape),
        in_specs=[SM, SM] + [ANY] * 7,
        out_specs=(VM, VM),
        scratch_shapes=[pltpu.VMEM((PIECE, 512), jnp.bfloat16), pltpu.SemaphoreType.DMA((7,))],
        compiler_params=pltpu.CompilerParams(vmem_limit_bytes=63 << 20),
        cost_estimate=pl.CostEstimate(flops=2 * 2048 * 512 * 512, bytes_accessed=3 << 20, transcendentals=0),
    )(me, core, *pieces)


def mixing_call(cells, me, core, own, other, start_codes):
    shape = jax.ShapeDtypeStruct((512, 128), jnp.bfloat16)
    vmem = pl.BlockSpec(memory_space=pltpu.VMEM)
    smem = pl.BlockSpec(memory_space=pltpu.SMEM)
    return pl.pallas_call(
        functools.partial(mixing, cells),
        out_shape=(shape, shape),
        in_specs=[smem, smem, ANY, ANY, vmem],
        out_specs=(vmem, vmem),
        scratch_shapes=[pltpu.VMEM((10, 128, 128), jnp.float32)]
        + [pltpu.VMEM((32, 24, 128), jnp.float32)] * 2
        + [pltpu.SemaphoreType.DMA((2,))],
        compiler_params=pltpu.CompilerParams(vmem_limit_bytes=62 << 20),
        cost_estimate=pl.CostEstimate(flops=1 << 30, bytes_accessed=1 << 20, transcendentals=0),
    )(me, core, own, other, start_codes)


def finish(plan, me_ref, high_ref, low_ref, *refs):
    pieces, out_ref = refs[:-5], refs[-5]
    wide, done, in_sems, out_sems = refs[-4:]
    me = me_ref[0]
    loads = []
    for j in range(4):
        group = []
        for e in range(4):
            for index, source, target, size in plan[4 * j + e]:
                group.append(
                    pltpu.make_async_copy(
                        pieces[index].at[pl.ds(source, size)],
                        wide.at[j, pl.ds(target, size), pl.ds(128 * e, 128)],
                        in_sems.at[len(loads), len(group)],
                    )
                )
                group[-1].start()
        loads.append(group)
    mix = jnp.concatenate([high_ref[...], low_ref[...]], 1)
    stores = []
    for j in range(4):
        for copy in loads[j]:
            copy.wait()
        for r in range(16):
            both = jnp.dot(wide[j, 128 * r : 128 * r + 128], mix, preferred_element_type=jnp.float32)
            done[j, r] = (both[:, :128] + both[:, 128:]).astype(jnp.bfloat16)
        columns = pl.ds(pl.multiple_of((me ^ j) * GROUP, GROUP), GROUP)
        for n, (source, target, size) in enumerate(((0, 3, 10), (10, 0, 3), (13, 13, 3))):
            copy = pltpu.make_async_copy(
                done.at[j, pl.ds(source, size)], out_ref.at[pl.ds(target, size), columns], out_sems.at[j, n]
            )
            copy.start()
            stores.append(copy)
    for copy in stores:
        copy.wait()


def finish_call(me, high, low, pieces, plan):
    return pl.pallas_call(
        functools.partial(finish, plan),
        out_shape=jax.ShapeDtypeStruct((16, NY, LANES), jnp.bfloat16),
        in_specs=[SM, VM, VM] + [ANY] * len(pieces),
        out_specs=ANY,
        scratch_shapes=[
            pltpu.VMEM((4, PIECE, 512), jnp.bfloat16),
            pltpu.VMEM((4, 16, GROUP, LANES), jnp.bfloat16),
            pltpu.SemaphoreType.DMA((4, 8)),
            pltpu.SemaphoreType.DMA((4, 3)),
        ],
        compiler_params=pltpu.CompilerParams(vmem_limit_bytes=63 << 20),
        cost_estimate=pl.CostEstimate(flops=2 * 8192 * 512 * 256, bytes_accessed=10 << 20, transcendentals=0),
    )(me, high, low, *pieces)


def packed_edge(cells, perm):
    high = perm.astype(jnp.bfloat16)
    low = (perm - high.astype(jnp.float32)).astype(jnp.bfloat16)
    parts = [cells.reshape(-1, LANES), high.reshape(-1, LANES), low.reshape(-1, LANES)]
    return jnp.concatenate(parts + [jnp.zeros((8, LANES), jnp.bfloat16)], 0)


def merged_bases(forcing, permeability, merge_weights, start_codes):
    me = lax.axis_index("case").astype(jnp.int32).reshape(1)
    tile = lax.axis_index("tile").astype(jnp.int32).reshape(1)
    core = tile & 1
    cells = forcing.shape[1] * lax.axis_size("tile") * forcing.shape[2]
    own, kp = forcing[0], permeability[0]
    up = [(i, i + 1) for i in range(63)]
    down = [(i + 1, i) for i in range(63)]
    low = lax.ppermute(packed_edge(own[-STEPS:], kp[-STEPS:]), "tile", up)
    high = lax.ppermute(packed_edge(own[:STEPS], kp[:STEPS]), "tile", down)
    inner = inner_call(me, merge_weights, own, kp)
    met = [case_swap(inner[e - 1], e) for e in (1, 2, 3)]
    outer = outer_call(me, tile, merge_weights, own, kp, low, high, inner[6], inner[7], inner[3:6])
    stacks = outer[3:]
    met = met + [case_swap(outer[e - 1], e) for e in (1, 2, 3)]
    far = [case_swap(stacks[e - 1], e) for e in (1, 2, 3)]
    own_part, other_part = grams_call(me, core, [stacks[0]] + met)
    part = own_part + core_swap(other_part)
    part = plane_exchange(part).sum(0)
    part = part + case_swap(part, 1) + case_swap(part, 2) + case_swap(part, 3)
    mine = plane_exchange(jnp.broadcast_to(part, (32,) + part.shape))
    yours = core_swap(mine)
    high, low = mixing_call(cells, me, core, mine, yours, start_codes)
    own_at = {0: (0, 0), 3: (0, 1), 2: (0, 2), 1: (1, 2)}
    plan = []
    for j in range(4):
        for e in range(4):
            if e == 0:
                index, slot = own_at[j]
                plan.append(((index, PIECE * slot, 0, PIECE),))
            elif j == 0:
                plan.append(((1 + e, 0, 0, INNER), (4 + e, 0, INNER, OUTER)))
            else:
                plan.append(((7 + e, PIECE * (j - 1), 0, PIECE),))
    pieces = [stacks[0], stacks[1]] + met + far
    return finish_call(me, high, low, pieces, tuple(plan)).reshape(1, -1, LANES)


def solution(mesh):
    placed = (P("case", "tile", None, None), P("case", "tile", None), P("case"), P())
    return jax.shard_map(
        merged_bases, mesh=mesh, in_specs=placed, out_specs=P("case", "tile", None), check_vma=False
    )
```

time: 194 us -> 202 us (1.041)
  the two profiles are of different devices: /device:TPU:8 before, /device:TPU:1 now
where the time goes in v1:
time: 202 us
  waiting for transfers between devices  81.4 us (40%)
  Pallas kernels  55.9 us (28%)
  starting transfers between devices  37.7 us (19%)
  blocking collectives  20.4 us (10%)
  local copies, waits for them, and re-layouts  3.28 us (2%)
    ppermute x12, waiting for transfers between devices, case_swap(): lax.ppermute(value, 'case', [(source, source ^ apart) for source in range...  68.2 us
    all_to_all x1, blocking collectives, plane_exchange(): return lax.all_to_all(value, 'tile', 0, 0, axis_index_groups=PLANES)  20.4 us
    pallas_call x1, Pallas kernels, mixing_call(): pl.pallas_call(functools.partial(mixing, cells), out_shape=(shape, shape)...  17.6 us
    pallas_call x1, Pallas kernels, inner_call(): pl.pallas_call(inner_rows, out_shape=[half(INNER)] * 3 + [half(3 * PIECE)...  15.3 us
    pallas_call x1, Pallas kernels, outer_call(): pl.pallas_call(outer_rows, out_shape=[half(OUTER)] * 3 + [half(3 * PIECE)...  12.9 us
    ppermute x12, starting transfers between devices, case_swap(): lax.ppermute(value, 'case', [(source, source ^ apart) for source in range...  12.8 us
    all_to_all x1, starting transfers between devices, plane_exchange(): return lax.all_to_all(value, 'tile', 0, 0, axis_index_groups=PLANES)  11.7 us
    all_to_all x1, waiting for transfers between devices, plane_exchange(): return lax.all_to_all(value, 'tile', 0, 0, axis_index_groups=PLANES)  10.1 us
  transfers between devices with their start and end apart: 17, of which 9 were waited for; matrix products, arithmetic and copies ran while one was open for 0% of the time, Pallas kernels for 23%

profile of v1, /device:TPU:1, one launch (start us, length us, event | category | flops | bytes accessed | tf_op | source)
XLA Modules:
  0.0 201.5 jit_solution(12824865146033959474)
XLA Ops:
  0.0 0.7 fusion.1
  0.8 1.2 fusion
  2.2 5.1 %collective-permute-start.1 = (bf16[1568,128]{1,0:T(8,128)(2,1)S(1)}, bf16[1568,128]{1,0:T(8,128)(2,1)}, u32[]{:S(2)}, u32[]{:S(2)}) collective-permute-start(bf16[1568,128]{1,0:T(8,128)(2,1)S(1)} %concatenate.7), channel_id=1, source_target_pairs={{1,0},{2,1},{3,2},{4,3},{5,4},{6,5},{7,6},{8,7},{9,8},{10,9},{11,1... | collective-permute-start | bytes 1204232 | tf_op jit(solution)/shard_map/ppermute | solution.py:579
  7.7 1.9 collective-permute-start
  10.3 15.3 %shard_map.46 = (bf16[1280,128]{1,0:T(8,128)(2,1)}, bf16[1280,128]{1,0:T(8,128)(2,1)}, bf16[1280,128]{1,0:T(8,128)(2,1)}, bf16[6144,128]{1,0:T(8,128)(2,1)}, bf1...) custom-call(s32[1]{0:T(128)} %bitcast.me_ref, ...), custom_call_target="tpu_custom_call" | custom-call | flops 419430400 | bytes 9437184 | tf_op jit(solution)/shard_map/pallas_call | solution.py:410
  25.6 0.8 collective-permute-start.2
  26.4 2.5 %collective-permute-start.3 = (bf16[1280,128]{1,0:T(8,128)(2,1)}, bf16[1280,128]{1,0:T(8,128)(2,1)}, u32[]{:S(2)}, u32[]{:S(2)}) collective-permute-start(bf16[1280,128]{1,0:T(8,128)(2,1)} %get-tuple-element.30), channel_id=1, source_target_pairs={{0,128},{64,192},{128,0},{192,64},{1,129},{65,193},{129,1},{193,65... | collective-permute-start | bytes 983048 | tf_op jit(solution)/shard_map/ppermute | solution.py:22
  28.8 0.7 collective-permute-start.4
  29.6 12.9 %shard_map.47 = (bf16[768,128]{1,0:T(8,128)(2,1)}, bf16[768,128]{1,0:T(8,128)(2,1)}, bf16[768,128]{1,0:T(8,128)(2,1)}, bf16[6144,128]{1,0:T(8,128)(2,1)}, bf16[6...) custom-call(s32[1]{0:T(128)} %bitcast.me_ref, ...), custom_call_target="tpu_custom_call", output_to_operand_aliasing={{3}: (9, {}), {4}: (10, {}), {5}: (11, {})} | custom-call | flops 209715200 | bytes 9437184 | tf_op jit(solution)/shard_map/pallas_call | solution.py:425
  42.6 3.1 %collective-permute-start.6 = (bf16[768,128]{1,0:T(8,128)(2,1)}, bf16[768,128]{1,0:T(8,128)(2,1)S(1)}, u32[]{:S(2)}, u32[]{:S(2)}) collective-permute-start(bf16[768,128]{1,0:T(8,128)(2,1)} %get-tuple-element.33), channel_id=1, source_target_pairs={{0,128},{64,192},{128,0},{192,64},{1,129},{65,193},{129,1},{193,65... | collective-permute-start | bytes 589832 | tf_op jit(solution)/shard_map/ppermute | solution.py:22
  45.7 0.7 collective-permute-start.7
  46.5 0.9 collective-permute-done.5.refs_4_.refs_5_
  47.3 6.9 %collective-permute-done.6.refs_5_.refs_6_ = bf16[768,128]{1,0:T(8,128)(2,1)S(1)} collective-permute-done((bf16[768,128]{1,0:T(8,128)(2,1)}, bf16[768,128]{1,0:T(8,128)(2,1)S(1)}, u32[]{:S(2)}, u32[]{:S(2)}) %collective-permute-start.6) | collective-permute-done | bytes 196640 | tf_op jit(solution)/shard_map/ppermute | solution.py:22
  54.2 3.0 %collective-permute-done.7.refs_6_.refs_7_ = bf16[768,128]{1,0:T(8,128)(2,1)S(1)} collective-permute-done((bf16[768,128]{1,0:T(8,128)(2,1)}, bf16[768,128]{1,0:T(8,128)(2,1)S(1)}, u32[]{:S(2)}, u32[]{:S(2)}) %collective-permute-start.7) | collective-permute-done | bytes 196640 | tf_op jit(solution)/shard_map/ppermute | solution.py:22
  57.2 0.7 copy-done.4
  57.9 3.5 %shard_map.48 = (f32[32,24,128]{2,1,0:T(8,128)}, f32[32,24,128]{2,1,0:T(8,128)}) custom-call(s32[1]{0:T(128)} %bitcast.me_ref, s32[1]{0:T(128)S(6)} %and.5.core_ref, bf16[6144,128]{1,0:T(8,128)(2,1)} %get-tuple-element.28.refs_0_, bf16[1280,128]{1,0:T(8,128)(2,1)} %collective-permute-done.2.refs_1_.refs_2_, ...), custom_call_target="tpu_custom_call" | custom-call | flops 1073741824 | bytes 3145728 | tf_op jit(solution)/shard_map/pallas_call | solution.py:481
  61.5 1.5 collective-permute-start.8
  63.0 1.6 collective-permute-done.8
  64.6 1.8 add.12
  66.4 11.7 %all-to-all-start = ((f32[32,24,128]{2,1,0:T(8,128)}), f32[32,24,128]{2,1,0:T(8,128)S(1)}, u32[]{:S(2)}, u32[]{:S(2)}) async-start(f32[32,24,128]{2,1,0:T(8,128)} %add.12), calls=%async_computation | async-start | bytes 786432 | tf_op jit(solution)/shard_map/all_to_all | solution.py:30
  78.2 1.4 collective-permute-start.14
  79.6 2.5 %collective-permute-start.15 = (bf16[6144,128]{1,0:T(8,128)(2,1)}, bf16[6144,128]{1,0:T(8,128)(2,1)}, u32[]{:S(2)}, u32[]{:S(2)}) collective-permute-start(bf16[6144,128]{1,0:T(8,128)(2,1)} %get-tuple-element.40), channel_id=1, source_target_pairs={{0,192},{64,128},{128,64},{192,0},{1,193},{65,129},{129,65},{193,1... | collective-permute-start | bytes 4718600 | tf_op jit(solution)/shard_map/ppermute | solution.py:22
  82.1 10.1 %all-to-all-done = f32[32,24,128]{2,1,0:T(8,128)S(1)} async-done(((f32[32,24,128]{2,1,0:T(8,128)}), f32[32,24,128]{2,1,0:T(8,128)S(1)}, u32[]{:S(2)}, u32[]{:S(2)}) %all-to-all-start) | async-done | bytes 393248 | tf_op jit(solution)/shard_map/all_to_all | solution.py:30
  92.3 0.9 collective-permute-start.11
  93.2 54.4 %collective-permute-done.10 = f32[24,128]{1,0:T(8,128)S(1)} collective-permute-done((f32[24,128]{1,0:T(8,128)S(1)}, f32[24,128]{1,0:T(8,128)S(1)}, u32[]{:S(2)}, u32[]{:S(2)}) %collective-permute-start.10) | collective-permute-done | bytes 12320 | tf_op jit(solution)/shard_map/ppermute | solution.py:22
  147.6 2.5 %collective-permute-done.11 = f32[24,128]{1,0:T(8,128)S(1)} collective-permute-done((f32[24,128]{1,0:T(8,128)S(1)}, f32[24,128]{1,0:T(8,128)S(1)}, u32[]{:S(2)}, u32[]{:S(2)}) %collective-permute-start.11) | collective-permute-done | bytes 12320 | tf_op jit(solution)/shard_map/ppermute | solution.py:22
  150.2 0.4 collective-permute-done.9
  150.6 20.4 %all_to_all.10.own_hbm = f32[32,24,128]{2,1,0:T(8,128)S(1)} all-to-all(f32[32,24,128]{2,1,0:T(8,128)S(1)} %broadcast_in_dim.3), channel_id=1, replica_groups={{0,2,4,6,8,10,12,14,16,18,20,22,24,26,28,30,32,34,36,38,40,42,44,46,48,..., dimensions={0} | all-to-all | bytes 786432 | tf_op jit(solution)/shard_map/all_to_all | solution.py:30
  171.1 4.7 %collective-permute-start.12 = (f32[32,24,128]{2,1,0:T(8,128)S(1)}, f32[32,24,128]{2,1,0:T(8,128)}, u32[]{:S(2)}, u32[]{:S(2)}) collective-permute-start(f32[32,24,128]{2,1,0:T(8,128)S(1)} %all_to_all.10.own_hbm), channel_id=1, source_target_pairs={{0,1},{1,0},{2,3},{3,2},{4,5},{5,4},{6,7},{7,6},{8,9},{9,8},{10,11... | collective-permute-start | bytes 1179656 | tf_op jit(solution)/shard_map/ppermute | solution.py:26
  175.7 1.5 collective-permute-done.12.other_hbm
  177.2 17.6 %shard_map.49 = (bf16[512,128]{1,0:T(8,128)(2,1)}, bf16[512,128]{1,0:T(8,128)(2,1)}) custom-call(s32[1]{0:T(128)} %bitcast.me_ref, s32[1]{0:T(128)S(6)} %and.5.core_ref, f32[32,24,128]{2,1,0:T(8,128)} %copy-done.1, f32[32,24,128]{2,1,0:T(8,128)} %collective-permute-done.12.other_hbm, s32[2,256,128]{2,1,0:T(8,128)} %start_ref.1), custom_call_target="tpu_custom_call" | custom-call | flops 1073741824 | bytes 1048576 | tf_op jit(solution)/shard_map/pallas_call | solution.py:496
  194.8 6.5 %shard_map.50 = bf16[16,512,128]{2,1,0:T(8,128)(2,1)} custom-call(s32[1]{0:T(128)} %bitcast.me_ref, bf16[512,128]{1,0:T(8,128)(2,1)} %get-tuple-element.37.high_ref, bf16[512,128]{1,0:T(8,128)(2,1)} %get-tuple-element.38.low_ref, bf16[6144,128]{1,0:T(8,128)(2,1)} %get-tuple-element.28.refs_0_, bf16[6144,128]{1,0:T(8,128)(2,1)} %get-tuple-element.39.refs_1_, ...), custom_call_target="tpu_custom_call" | custom-call | flops 2147483648 | bytes 10485760 | tf_op jit(solution)/shard_map/pallas_call | solution.py:547
  (31 shorter events, 1.0 us)
Async XLA Ops:
  2.2 27.3 %collective-permute-start.1 = (bf16[1568,128]{1,0:T(8,128)(2,1)S(1)}, bf16[1568,128]{1,0:T(8,128)(2,1)}, u32[]{:S(2)}, u32[]{:S(2)}) collective-permute-start(bf16[1568,128]{1,0:T(8,128)(2,1)S(1)} %concatenate.7), channel_id=1, source_target_pairs={{1,0},{2,1},{3,2},{4,3},{5,4},{6,5},{7,6},{8,7},{9,8},{10,9},{11,1... | collective-permute-start | bytes 1204232 | tf_op jit(solution)/shard_map/ppermute | solution.py:579
  7.7 21.9 %collective-permute-start = (bf16[1568,128]{1,0:T(8,128)(2,1)S(1)}, bf16[1568,128]{1,0:T(8,128)(2,1)}, u32[]{:S(2)}, u32[]{:S(2)}) collective-permute-start(bf16[1568,128]{1,0:T(8,128)(2,1)S(1)} %concatenate.6), channel_id=1, source_target_pairs={{0,1},{1,2},{2,3},{3,4},{4,5},{5,6},{6,7},{7,8},{8,9},{9,10},{10,1... | collective-permute-start | bytes 1204232 | tf_op jit(solution)/shard_map/ppermute | solution.py:578
  25.6 20.1 %collective-permute-start.2 = (bf16[1280,128]{1,0:T(8,128)(2,1)}, bf16[1280,128]{1,0:T(8,128)(2,1)}, u32[]{:S(2)}, u32[]{:S(2)}) collective-permute-start(bf16[1280,128]{1,0:T(8,128)(2,1)} %get-tuple-element.29), channel_id=1, source_target_pairs={{0,64},{64,0},{128,192},{192,128},{1,65},{65,1},{129,193},{193,129... | collective-permute-start | bytes 983048 | tf_op jit(solution)/shard_map/ppermute | solution.py:22
  26.4 20.1 %collective-permute-start.3 = (bf16[1280,128]{1,0:T(8,128)(2,1)}, bf16[1280,128]{1,0:T(8,128)(2,1)}, u32[]{:S(2)}, u32[]{:S(2)}) collective-permute-start(bf16[1280,128]{1,0:T(8,128)(2,1)} %get-tuple-element.30), channel_id=1, source_target_pairs={{0,128},{64,192},{128,0},{192,64},{1,129},{65,193},{129,1},{193,65... | collective-permute-start | bytes 983048 | tf_op jit(solution)/shard_map/ppermute | solution.py:22
  28.8 17.6 %collective-permute-start.4 = (bf16[1280,128]{1,0:T(8,128)(2,1)}, bf16[1280,128]{1,0:T(8,128)(2,1)}, u32[]{:S(2)}, u32[]{:S(2)}) collective-permute-start(bf16[1280,128]{1,0:T(8,128)(2,1)} %get-tuple-element.31), channel_id=1, source_target_pairs={{0,192},{64,128},{128,64},{192,0},{1,193},{65,129},{129,65},{193,1... | collective-permute-start | bytes 983048 | tf_op jit(solution)/shard_map/ppermute | solution.py:22
  42.5 4.8 %collective-permute-start.5 = (bf16[768,128]{1,0:T(8,128)(2,1)}, bf16[768,128]{1,0:T(8,128)(2,1)S(1)}, u32[]{:S(2)}, u32[]{:S(2)}) collective-permute-start(bf16[768,128]{1,0:T(8,128)(2,1)} %get-tuple-element.32), channel_id=1, source_target_pairs={{0,64},{64,0},{128,192},{192,128},{1,65},{65,1},{129,193},{193,129... | collective-permute-start | bytes 589832 | tf_op jit(solution)/shard_map/ppermute | solution.py:22
  42.6 11.6 %collective-permute-start.6 = (bf16[768,128]{1,0:T(8,128)(2,1)}, bf16[768,128]{1,0:T(8,128)(2,1)S(1)}, u32[]{:S(2)}, u32[]{:S(2)}) collective-permute-start(bf16[768,128]{1,0:T(8,128)(2,1)} %get-tuple-element.33), channel_id=1, source_target_pairs={{0,128},{64,192},{128,0},{192,64},{1,129},{65,193},{129,1},{193,65... | collective-permute-start | bytes 589832 | tf_op jit(solution)/shard_map/ppermute | solution.py:22
  45.7 11.5 %collective-permute-start.7 = (bf16[768,128]{1,0:T(8,128)(2,1)}, bf16[768,128]{1,0:T(8,128)(2,1)S(1)}, u32[]{:S(2)}, u32[]{:S(2)}) collective-permute-start(bf16[768,128]{1,0:T(8,128)(2,1)} %get-tuple-element.34), channel_id=1, source_target_pairs={{0,192},{64,128},{128,64},{192,0},{1,193},{65,129},{129,65},{193,1... | collective-permute-start | bytes 589832 | tf_op jit(solution)/shard_map/ppermute | solution.py:22
  47.3 9.9 %copy-start.2 = (bf16[768,128]{1,0:T(8,128)(2,1)}, bf16[768,128]{1,0:T(8,128)(2,1)S(1)}, u32[]{:S(2)}) copy-start(bf16[768,128]{1,0:T(8,128)(2,1)S(1)} %collective-permute-done.5.refs_4_.refs_5_) | copy-start | bytes 589828
  54.2 3.0 %copy-start.3 = (bf16[768,128]{1,0:T(8,128)(2,1)}, bf16[768,128]{1,0:T(8,128)(2,1)S(1)}, u32[]{:S(2)}) copy-start(bf16[768,128]{1,0:T(8,128)(2,1)S(1)} %collective-permute-done.6.refs_5_.refs_6_) | copy-start | bytes 589828
  57.2 0.7 copy-start.4
  61.5 16.6 %copy-start = (bf16[6144,128]{1,0:T(8,128)(2,1)S(1)}, bf16[6144,128]{1,0:T(8,128)(2,1)}, u32[]{:S(2)}) copy-start(bf16[6144,128]{1,0:T(8,128)(2,1)} %get-tuple-element.28.refs_0_) | copy-start | bytes 4718596
  61.5 3.1 %collective-permute-start.8 = (f32[32,24,128]{2,1,0:T(8,128)}, f32[32,24,128]{2,1,0:T(8,128)S(1)}, u32[]{:S(2)}, u32[]{:S(2)}) collective-permute-start(f32[32,24,128]{2,1,0:T(8,128)} %get-tuple-element.36), channel_id=1, source_target_pairs={{0,1},{1,0},{2,3},{3,2},{4,5},{5,4},{6,7},{7,6},{8,9},{9,8},{10,11... | collective-permute-start | bytes 1179656 | tf_op jit(solution)/shard_map/ppermute | solution.py:26
  66.4 25.8 %all-to-all-start = ((f32[32,24,128]{2,1,0:T(8,128)}), f32[32,24,128]{2,1,0:T(8,128)S(1)}, u32[]{:S(2)}, u32[]{:S(2)}) async-start(f32[32,24,128]{2,1,0:T(8,128)} %add.12), calls=%async_computation | async-start | bytes 786432 | tf_op jit(solution)/shard_map/all_to_all | solution.py:30
  78.1 116.7 %collective-permute-start.13 = (bf16[6144,128]{1,0:T(8,128)(2,1)S(1)}, bf16[6144,128]{1,0:T(8,128)(2,1)}, u32[]{:S(2)}, u32[]{:S(2)}) collective-permute-start(bf16[6144,128]{1,0:T(8,128)(2,1)S(1)} %copy-done), channel_id=1, source_target_pairs={{0,64},{64,0},{128,192},{192,128},{1,65},{65,1},{129,193},{193,129... | collective-permute-start | bytes 4718600 | tf_op jit(solution)/shard_map/ppermute | solution.py:22
  78.2 116.6 %collective-permute-start.14 = (bf16[6144,128]{1,0:T(8,128)(2,1)}, bf16[6144,128]{1,0:T(8,128)(2,1)}, u32[]{:S(2)}, u32[]{:S(2)}) collective-permute-start(bf16[6144,128]{1,0:T(8,128)(2,1)} %get-tuple-element.39.refs_1_), channel_id=1, source_target_pairs={{0,128},{64,192},{128,0},{192,64},{1,129},{65,193},{129,1},{193,65... | collective-permute-start | bytes 4718600 | tf_op jit(solution)/shard_map/ppermute | solution.py:22
  79.6 115.3 %collective-permute-start.15 = (bf16[6144,128]{1,0:T(8,128)(2,1)}, bf16[6144,128]{1,0:T(8,128)(2,1)}, u32[]{:S(2)}, u32[]{:S(2)}) collective-permute-start(bf16[6144,128]{1,0:T(8,128)(2,1)} %get-tuple-element.40), channel_id=1, source_target_pairs={{0,192},{64,128},{128,64},{192,0},{1,193},{65,129},{129,65},{193,1... | collective-permute-start | bytes 4718600 | tf_op jit(solution)/shard_map/ppermute | solution.py:22
  92.2 55.4 %collective-permute-start.10 = (f32[24,128]{1,0:T(8,128)S(1)}, f32[24,128]{1,0:T(8,128)S(1)}, u32[]{:S(2)}, u32[]{:S(2)}) collective-permute-start(f32[24,128]{1,0:T(8,128)S(1)} %reduce_sum.9), channel_id=1, source_target_pairs={{0,128},{64,192},{128,0},{192,64},{1,129},{65,193},{129,1},{193,65... | collective-permute-start | bytes 36872 | tf_op jit(solution)/shard_map/ppermute | solution.py:22
  92.3 57.8 %collective-permute-start.11 = (f32[24,128]{1,0:T(8,128)S(1)}, f32[24,128]{1,0:T(8,128)S(1)}, u32[]{:S(2)}, u32[]{:S(2)}) collective-permute-start(f32[24,128]{1,0:T(8,128)S(1)} %reduce_sum.9), channel_id=1, source_target_pairs={{0,192},{64,128},{128,64},{192,0},{1,193},{65,129},{129,65},{193,1... | collective-permute-start | bytes 36872 | tf_op jit(solution)/shard_map/ppermute | solution.py:22
  147.6 2.9 %collective-permute-start.9 = (f32[24,128]{1,0:T(8,128)S(1)}, f32[24,128]{1,0:T(8,128)S(1)}, u32[]{:S(2)}, u32[]{:S(2)}) collective-permute-start(f32[24,128]{1,0:T(8,128)S(1)} %reduce_sum.9), channel_id=1, source_target_pairs={{0,64},{64,0},{128,192},{192,128},{1,65},{65,1},{129,193},{193,129... | collective-permute-start | bytes 36872 | tf_op jit(solution)/shard_map/ppermute | solution.py:22
  171.1 6.2 %copy-start.1 = (f32[32,24,128]{2,1,0:T(8,128)}, f32[32,24,128]{2,1,0:T(8,128)S(1)}, u32[]{:S(2)}) copy-start(f32[32,24,128]{2,1,0:T(8,128)S(1)} %all_to_all.10.own_hbm) | copy-start | bytes 1179652
  171.1 6.2 %collective-permute-start.12 = (f32[32,24,128]{2,1,0:T(8,128)S(1)}, f32[32,24,128]{2,1,0:T(8,128)}, u32[]{:S(2)}, u32[]{:S(2)}) collective-permute-start(f32[32,24,128]{2,1,0:T(8,128)S(1)} %all_to_all.10.own_hbm), channel_id=1, source_target_pairs={{0,1},{1,0},{2,3},{3,2},{4,5},{5,4},{6,7},{7,6},{8,9},{9,8},{10,11... | collective-permute-start | bytes 1179656 | tf_op jit(solution)/shard_map/ppermute | solution.py:26

commit v2 on v1

--- a/solution.py
+++ b/solution.py
@@ -240,10 +240,12 @@
             center, south = carry
             above = source[row + 1, c : c + GROUP]
             up = north[plane, c : c + GROUP] * (above - center)
-            flux = up - south
-            flux = flux + east[plane, c : c + GROUP] * (source[row, c + 1 : c + GROUP + 1] - center)
-            flux = flux + east[plane, c - 1 : c + GROUP - 1] * (source[row, c - 1 : c + GROUP - 1] - center)
-            write(i, g, center + flux)
+            east_here = east[plane, c : c + GROUP]
+            flux = east_here * (source[row, c + 1 : c + GROUP + 1] - center)
+            before = source[row, c - PAD : c]
+            edge = east[plane, c - PAD : c] * (source[row, c - PAD + 1 : c + 1] - before)
+            shifted = jnp.concatenate([edge, flux], 0)[PAD - 1 : PAD - 1 + GROUP]
+            write(i, g, center + ((up - south) + (flux - shifted)))
             return above, up
 
         center = source[begin, c : c + GROUP]
@@ -269,12 +271,12 @@
     return write
 
 
-def send_out(me, snap, singles, stacks, begin, size, sems):
+def send_out(me, snap, singles, moves, sems):
     copies = []
     for e in (1, 2, 3):
         copies.append(pltpu.make_async_copy(snap.at[me ^ e], singles[e - 1], sems.at[len(copies)]))
-        for j in (1, 2, 3):
-            target = stacks[e - 1].at[pl.ds(PIECE * (j - 1) + begin, size)]
+        for stacks, j, begin, size in moves:
+            target = stacks[e - 1].at[pl.ds(begin, size)]
             copies.append(pltpu.make_async_copy(snap.at[me ^ e ^ j], target, sems.at[len(copies)]))
     for copy in copies:
         copy.start()
@@ -282,8 +284,8 @@
 
 
 def inner_rows(me_ref, scale_ref, own_ref, kp_ref, *refs):
-    singles, stacks, edge_one, edge_two = refs[:3], refs[3:6], refs[6], refs[7]
-    first, second, east, north, perm_ref, snap, held, sems, edge_sems = refs[8:]
+    singles, near, late, edge_one, edge_two = refs[:3], refs[3:6], refs[6:9], refs[9], refs[10]
+    first, second, east, north, perm_ref, snap, held, sems, edge_sems = refs[11:]
     me = me_ref[0]
     load = pltpu.make_async_copy(own_ref, held, sems.at[0])
     load.start()
@@ -309,14 +311,15 @@
     for copy in edges_out:
         copy.start()
     sweep(first, east, north, 3, 3, 10, into_snap(snap, 0, scale_ref))
-    for copy in edges_out + send_out(me, snap, singles, stacks, 0, INNER, sems):
+    moves = ((near, 1, 0, INNER), (late, 3, 0, INNER), (late, 2, PIECE, INNER))
+    for copy in edges_out + send_out(me, snap, singles, moves, sems):
         copy.wait()
 
 
 def outer_rows(me_ref, tile_ref, scale_ref, own_hbm, kp_ref, low_hbm, high_hbm, edge_one, edge_two, *refs):
-    singles, stacks = refs[3:6], refs[6:9]
-    low0, low1, low2, high0, high1, high2, east, north, perm_ref, snap = refs[9:19]
-    low_ref, high_ref, own_ref, sems, edge_sems = refs[19:]
+    singles, near, late = refs[6:9], refs[9:12], refs[12:15]
+    low0, low1, low2, high0, high1, high2, east, north, perm_ref, snap = refs[15:25]
+    low_ref, high_ref, own_ref, sems, edge_sems = refs[25:]
     me, tile = me_ref[0], tile_ref[0]
     loads = [
         pltpu.make_async_copy(low_hbm, low_ref, sems.at[0]),
@@ -388,7 +391,8 @@
 
     sweep(low2, east, north, 1, 3, 3, into_snap(snap, 0, scale_ref))
     sweep(high2, east, north, 1, 8, 3, into_snap(snap, 3, scale_ref))
-    for copy in send_out(me, snap, singles, stacks, INNER, OUTER, sems):
+    moves = ((near, 1, INNER, OUTER), (near, 2, PIECE, OUTER), (late, 3, INNER, OUTER))
+    for copy in send_out(me, snap, singles, moves, sems):
         copy.wait()
 
 
@@ -409,9 +413,9 @@
     edge = jax.ShapeDtypeStruct((4, WIDE, LANES), jnp.float32)
     return pl.pallas_call(
         inner_rows,
-        out_shape=[half(INNER)] * 3 + [half(3 * PIECE)] * 3 + [edge] * 2,
+        out_shape=[half(INNER)] * 3 + [half(PIECE + OUTER)] * 3 + [half(PIECE + INNER)] * 3 + [edge] * 2,
         in_specs=[SM, SM, ANY, VM],
-        out_specs=[ANY] * 8,
+        out_specs=[ANY] * 11,
         scratch_shapes=[planes(16), planes(16), planes(15), planes(15)]
         + [pltpu.VMEM((WIDE, LANES), jnp.float32), pltpu.VMEM((4, INNER, LANES), jnp.bfloat16)]
         + [pltpu.VMEM((16, NY, LANES), jnp.bfloat16)]
@@ -424,10 +428,10 @@
 def outer_call(me, tile, weights, own, kp, low, high, edge_one, edge_two, stacks):
     return pl.pallas_call(
         outer_rows,
-        out_shape=[half(OUTER)] * 3 + [half(3 * PIECE)] * 3,
-        in_specs=[SM, SM, SM, ANY, VM] + [ANY] * 7,
-        out_specs=[ANY] * 6,
-        input_output_aliases={9: 3, 10: 4, 11: 5},
+        out_shape=[half(OUTER)] * 3 + [half(PIECE + OUTER)] * 3 + [half(PIECE + INNER)] * 3,
+        in_specs=[SM, SM, SM, ANY, VM] + [ANY] * 10,
+        out_specs=[ANY] * 9,
+        input_output_aliases={9 + n: 3 + n for n in range(6)},
         scratch_shapes=[planes(5)] * 6
         + [planes(13), planes(13), pltpu.VMEM((WIDE, LANES), jnp.float32)]
         + [pltpu.VMEM((4, OUTER, LANES), jnp.bfloat16)]
@@ -579,29 +583,30 @@
     high = lax.ppermute(packed_edge(own[:STEPS], kp[:STEPS]), "tile", down)
     inner = inner_call(me, merge_weights, own, kp)
     met = [case_swap(inner[e - 1], e) for e in (1, 2, 3)]
-    outer = outer_call(me, tile, merge_weights, own, kp, low, high, inner[6], inner[7], inner[3:6])
-    stacks = outer[3:]
+    outer = outer_call(me, tile, merge_weights, own, kp, low, high, inner[9], inner[10], inner[3:9])
+    near, late = outer[3:6], outer[6:9]
     met = met + [case_swap(outer[e - 1], e) for e in (1, 2, 3)]
-    far = [case_swap(stacks[e - 1], e) for e in (1, 2, 3)]
-    own_part, other_part = grams_call(me, core, [stacks[0]] + met)
+    far = [case_swap(near[e - 1], e) for e in (1, 2, 3)]
+    far = far + [case_swap(late[e - 1], e) for e in (1, 2, 3)]
+    own_part, other_part = grams_call(me, core, [near[0]] + met)
     part = own_part + core_swap(other_part)
     part = plane_exchange(part).sum(0)
     part = part + case_swap(part, 1) + case_swap(part, 2) + case_swap(part, 3)
     mine = plane_exchange(jnp.broadcast_to(part, (32,) + part.shape))
     yours = core_swap(mine)
     high, low = mixing_call(cells, me, core, mine, yours, start_codes)
-    own_at = {0: (0, 0), 3: (0, 1), 2: (0, 2), 1: (1, 2)}
     plan = []
     for j in range(4):
         for e in range(4):
             if e == 0:
-                index, slot = own_at[j]
-                plan.append(((index, PIECE * slot, 0, PIECE),))
+                plan.append((({0: 0, 3: 1, 2: 2, 1: 3}[j], 0, 0, PIECE),))
             elif j == 0:
-                plan.append(((1 + e, 0, 0, INNER), (4 + e, 0, INNER, OUTER)))
+                plan.append(((3 + e, 0, 0, INNER), (6 + e, 0, INNER, OUTER)))
+            elif j == 2:
+                plan.append(((12 + e, PIECE, 0, INNER), (9 + e, PIECE, INNER, OUTER)))
             else:
-                plan.append(((7 + e, PIECE * (j - 1), 0, PIECE),))
-    pieces = [stacks[0], stacks[1]] + met + far
+                plan.append(((9 + e if j == 1 else 12 + e, 0, 0, PIECE),))
+    pieces = [near[0], near[1], near[2], late[1]] + met + far
     return finish_call(me, high, low, pieces, tuple(plan)).reshape(1, -1, LANES)
 
 

time: 202 us -> 198 us (0.980)
  waiting for transfers between devices: 81.4 us -> 72.7 us
  blocking collectives: 20.4 us -> 25.6 us
    ppermute x12 -> x15, waiting for transfers between devices: 68.2 us -> 60.9 us  [case_swap(): lax.ppermute(value, 'case', [(source, source ^ apart) for source in range...]
    all_to_all x1, starting transfers between devices: 11.7 us -> 4.77 us  [plane_exchange(): return lax.all_to_all(value, 'tile', 0, 0, axis_index_groups=PLANES)]
    all_to_all x1, blocking collectives: 20.4 us -> 25.6 us  [plane_exchange(): return lax.all_to_all(value, 'tile', 0, 0, axis_index_groups=PLANES)]
    ppermute x12 -> x15, starting transfers between devices: 12.8 us -> 17.8 us  [case_swap(): lax.ppermute(value, 'case', [(source, source ^ apart) for source in range...]
  transfers between devices with their start and end apart: 17 -> 20, of which waited for: 9 -> 8; matrix products, arithmetic and copies ran while one was open for 0% -> 0% of each run, Pallas kernels for 23% -> 23%
where the time goes in v2:
time: 198 us; the launch traced here: 197 us
  waiting for transfers between devices  72.7 us (37%)
  Pallas kernels  55.4 us (28%)
  starting transfers between devices  36.3 us (18%)
  blocking collectives  25.6 us (13%)
  local copies, waits for them, and re-layouts  5.22 us (3%)
    ppermute x15, waiting for transfers between devices, case_swap(): lax.ppermute(value, 'case', [(source, source ^ apart) for source in range...  60.9 us
    all_to_all x1, blocking collectives, plane_exchange(): return lax.all_to_all(value, 'tile', 0, 0, axis_index_groups=PLANES)  25.6 us
    ppermute x15, starting transfers between devices, case_swap(): lax.ppermute(value, 'case', [(source, source ^ apart) for source in range...  17.8 us
    pallas_call x1, Pallas kernels, mixing_call(): pl.pallas_call(functools.partial(mixing, cells), out_shape=(shape, shape)...  17.6 us
    pallas_call x1, Pallas kernels, inner_call(): pl.pallas_call(inner_rows, out_shape=[half(INNER)] * 3 + [half(PIECE + OU...  15 us
    pallas_call x1, Pallas kernels, outer_call(): pl.pallas_call(outer_rows, out_shape=[half(OUTER)] * 3 + [half(PIECE + OU...  12.7 us
    all_to_all x1, waiting for transfers between devices, plane_exchange(): return lax.all_to_all(value, 'tile', 0, 0, axis_index_groups=PLANES)  10.2 us
    ppermute x2, starting transfers between devices, core_swap(): lax.ppermute(value, 'tile', [(source, source ^ 1) for source in range(64)])  6.73 us
  transfers between devices with their start and end apart: 20, of which 8 were waited for; matrix products, arithmetic and copies ran while one was open for 0% of the time, Pallas kernels for 23%

profile of v2, /device:TPU:1, one launch (start us, length us, event | category | flops | bytes accessed | tf_op | source)
XLA Modules:
  0.0 197.3 jit_solution(8941875320985059223)
XLA Ops:
  0.8 1.2 fusion
  2.2 5.1 %collective-permute-start.1 = (bf16[1568,128]{1,0:T(8,128)(2,1)S(1)}, bf16[1568,128]{1,0:T(8,128)(2,1)}, u32[]{:S(2)}, u32[]{:S(2)}) collective-permute-start(bf16[1568,128]{1,0:T(8,128)(2,1)S(1)} %concatenate.7), channel_id=1, source_target_pairs={{1,0},{2,1},{3,2},{4,3},{5,4},{6,5},{7,6},{8,7},{9,8},{10,9},{11,1... | collective-permute-start | bytes 1204232 | tf_op jit(solution)/shard_map/ppermute | solution.py:583
  7.7 1.9 collective-permute-start
  10.3 15.0 %shard_map.46 = (bf16[1280,128]{1,0:T(8,128)(2,1)}, bf16[1280,128]{1,0:T(8,128)(2,1)}, bf16[1280,128]{1,0:T(8,128)(2,1)}, bf16[2816,128]{1,0:T(8,128)(2,1)}, bf1...) custom-call(s32[1]{0:T(128)} %bitcast.me_ref, ...), custom_call_target="tpu_custom_call" | custom-call | flops 419430400 | bytes 9437184 | tf_op jit(solution)/shard_map/pallas_call | solution.py:414
  25.3 0.8 collective-permute-start.2
  26.1 2.5 %collective-permute-start.3 = (bf16[1280,128]{1,0:T(8,128)(2,1)}, bf16[1280,128]{1,0:T(8,128)(2,1)}, u32[]{:S(2)}, u32[]{:S(2)}) collective-permute-start(bf16[1280,128]{1,0:T(8,128)(2,1)} %get-tuple-element.39), channel_id=1, source_target_pairs={{0,128},{64,192},{128,0},{192,64},{1,129},{65,193},{129,1},{193,65... | collective-permute-start | bytes 983048 | tf_op jit(solution)/shard_map/ppermute | solution.py:22
  29.3 12.7 %shard_map.47 = (bf16[768,128]{1,0:T(8,128)(2,1)}, bf16[768,128]{1,0:T(8,128)(2,1)}, bf16[768,128]{1,0:T(8,128)(2,1)}, bf16[2816,128]{1,0:T(8,128)(2,1)}, bf16[2...) custom-call(s32[1]{0:T(128)} %bitcast.me_ref, ...), custom_call_target="tpu_custom_call", output_to_operand_aliasing={{3}: (9, {}), {4}: (10, {}), {5}: (11, {}), {6}: (12, {}), ... | custom-call | flops 209715200 | bytes 9437184 | tf_op jit(solution)/shard_map/pallas_call | solution.py:429
  42.1 3.1 %collective-permute-start.6 = (bf16[768,128]{1,0:T(8,128)(2,1)}, bf16[768,128]{1,0:T(8,128)(2,1)S(1)}, u32[]{:S(2)}, u32[]{:S(2)}) collective-permute-start(bf16[768,128]{1,0:T(8,128)(2,1)} %get-tuple-element.42), channel_id=1, source_target_pairs={{0,128},{64,192},{128,0},{192,64},{1,129},{65,193},{129,1},{193,65... | collective-permute-start | bytes 589832 | tf_op jit(solution)/shard_map/ppermute | solution.py:22
  46.0 0.9 collective-permute-done.5.refs_4_.refs_7_
  46.8 6.9 %collective-permute-done.6.refs_5_.refs_8_ = bf16[768,128]{1,0:T(8,128)(2,1)S(1)} collective-permute-done((bf16[768,128]{1,0:T(8,128)(2,1)}, bf16[768,128]{1,0:T(8,128)(2,1)S(1)}, u32[]{:S(2)}, u32[]{:S(2)}) %collective-permute-start.6) | collective-permute-done | bytes 196640 | tf_op jit(solution)/shard_map/ppermute | solution.py:22
  53.7 3.0 %collective-permute-done.7.refs_6_.refs_9_ = bf16[768,128]{1,0:T(8,128)(2,1)S(1)} collective-permute-done((bf16[768,128]{1,0:T(8,128)(2,1)}, bf16[768,128]{1,0:T(8,128)(2,1)S(1)}, u32[]{:S(2)}, u32[]{:S(2)}) %collective-permute-start.7) | collective-permute-done | bytes 196640 | tf_op jit(solution)/shard_map/ppermute | solution.py:22
  57.4 3.5 %shard_map.48 = (f32[32,24,128]{2,1,0:T(8,128)}, f32[32,24,128]{2,1,0:T(8,128)}) custom-call(s32[1]{0:T(128)} %bitcast.me_ref, s32[1]{0:T(128)S(6)} %and.5.core_ref, bf16[2816,128]{1,0:T(8,128)(2,1)} %get-tuple-element.37.refs_0_, bf16[1280,128]{1,0:T(8,128)(2,1)} %collective-permute-done.2.refs_1_.refs_4_, ...), custom_call_target="tpu_custom_call" | custom-call | flops 1073741824 | bytes 3145728 | tf_op jit(solution)/shard_map/pallas_call | solution.py:485
  61.0 1.5 collective-permute-start.8
  62.5 1.6 collective-permute-done.8
  64.1 1.0 add.12
  65.1 25.6 %all_to_all.10 = f32[32,24,128]{2,1,0:T(8,128)S(1)} all-to-all(f32[32,24,128]{2,1,0:T(8,128)S(1)} %add.12), channel_id=1, replica_groups={{0,2,4,6,8,10,12,14,16,18,20,22,24,26,28,30,32,34,36,38,40,42,44,46,48,..., dimensions={0} | all-to-all | bytes 786432 | tf_op jit(solution)/shard_map/all_to_all | solution.py:30
  90.8 0.9 collective-permute-start.11
  91.7 1.8 collective-permute-start.9
  93.5 1.4 collective-permute-done.10
  94.9 0.8 broadcast_in_dim.3
  95.7 4.8 %all-to-all-start.1 = ((f32[32,24,128]{2,1,0:T(8,128)}), f32[32,24,128]{2,1,0:T(8,128)S(1)}, u32[]{:S(2)}, u32[]{:S(2)}) async-start(f32[32,24,128]{2,1,0:T(8,128)} %broadcast_in_dim.3), calls=%async_computation.1 | async-start | bytes 786432 | tf_op jit(solution)/shard_map/all_to_all | solution.py:30
  100.5 1.3 collective-permute-start.13
  101.8 10.2 %all-to-all-done.1.own_hbm = f32[32,24,128]{2,1,0:T(8,128)S(1)} async-done(((f32[32,24,128]{2,1,0:T(8,128)}), f32[32,24,128]{2,1,0:T(8,128)S(1)}, u32[]{:S(2)}, u32[]{:S(2)}) %all-to-all-start.1) | async-done | bytes 393248 | tf_op jit(solution)/shard_map/all_to_all | solution.py:30
  112.0 5.2 %collective-permute-start.12 = (f32[32,24,128]{2,1,0:T(8,128)S(1)}, f32[32,24,128]{2,1,0:T(8,128)S(1)}, u32[]{:S(2)}, u32[]{:S(2)}) collective-permute-start(f32[32,24,128]{2,1,0:T(8,128)S(1)} %all-to-all-done.1.own_hbm), channel_id=1, source_target_pairs={{0,1},{1,0},{2,3},{3,2},{4,5},{5,4},{6,7},{7,6},{8,9},{9,8},{10,11... | collective-permute-start | bytes 1179656 | tf_op jit(solution)/shard_map/ppermute | solution.py:26
  117.2 1.2 collective-permute-start.16
  118.4 1.5 collective-permute-start.17
  120.0 1.1 collective-permute-start.18
  122.7 1.6 collective-permute-start.15
  124.3 17.6 %shard_map.49 = (bf16[512,128]{1,0:T(8,128)(2,1)}, bf16[512,128]{1,0:T(8,128)(2,1)}) custom-call(s32[1]{0:T(128)} %bitcast.me_ref, s32[1]{0:T(128)S(6)} %and.5.core_ref, f32[32,24,128]{2,1,0:T(8,128)} %copy-done.4, f32[32,24,128]{2,1,0:T(8,128)} %copy-done.8, s32[2,256,128]{2,1,0:T(8,128)} %start_ref.1), custom_call_target="tpu_custom_call" | custom-call | flops 1073741824 | bytes 1048576 | tf_op jit(solution)/shard_map/pallas_call | solution.py:500
  141.9 31.1 %collective-permute-done.14.refs_11_ = bf16[2816,128]{1,0:T(8,128)(2,1)} collective-permute-done((bf16[2816,128]{1,0:T(8,128)(2,1)S(1)}, bf16[2816,128]{1,0:T(8,128)(2,1)}, u32[]{:S(2)}, u32[]{:S(2)}) %collective-permute-start.14) | collective-permute-done | bytes 720928 | tf_op jit(solution)/shard_map/ppermute | solution.py:22
  173.0 17.5 %collective-permute-done.15.refs_12_ = bf16[2816,128]{1,0:T(8,128)(2,1)} collective-permute-done((bf16[2816,128]{1,0:T(8,128)(2,1)}, bf16[2816,128]{1,0:T(8,128)(2,1)}, u32[]{:S(2)}, u32[]{:S(2)}) %collective-permute-start.15) | collective-permute-done | bytes 720928 | tf_op jit(solution)/shard_map/ppermute | solution.py:22
  190.6 6.6 %shard_map.50 = bf16[16,512,128]{2,1,0:T(8,128)(2,1)} custom-call(s32[1]{0:T(128)} %bitcast.me_ref, bf16[512,128]{1,0:T(8,128)(2,1)} %get-tuple-element.46.high_ref, bf16[512,128]{1,0:T(8,128)(2,1)} %get-tuple-element.47.low_ref, bf16[2816,128]{1,0:T(8,128)(2,1)} %get-tuple-element.37.refs_0_, bf16[2816,128]{1,0:T(8,128)(2,1)} %get-tuple-element.48.refs_1_, ...), custom_call_target="tpu_custom_call" | custom-call | flops 2147483648 | bytes 10485760 | tf_op jit(solution)/shard_map/pallas_call | solution.py:551
  (45 shorter events, 5.4 us)
Async XLA Ops:
  2.2 27.0 %collective-permute-start.1 = (bf16[1568,128]{1,0:T(8,128)(2,1)S(1)}, bf16[1568,128]{1,0:T(8,128)(2,1)}, u32[]{:S(2)}, u32[]{:S(2)}) collective-permute-start(bf16[1568,128]{1,0:T(8,128)(2,1)S(1)} %concatenate.7), channel_id=1, source_target_pairs={{1,0},{2,1},{3,2},{4,3},{5,4},{6,5},{7,6},{8,7},{9,8},{10,9},{11,1... | collective-permute-start | bytes 1204232 | tf_op jit(solution)/shard_map/ppermute | solution.py:583
  7.7 21.6 %collective-permute-start = (bf16[1568,128]{1,0:T(8,128)(2,1)S(1)}, bf16[1568,128]{1,0:T(8,128)(2,1)}, u32[]{:S(2)}, u32[]{:S(2)}) collective-permute-start(bf16[1568,128]{1,0:T(8,128)(2,1)S(1)} %concatenate.6), channel_id=1, source_target_pairs={{0,1},{1,2},{2,3},{3,4},{4,5},{5,6},{6,7},{7,8},{8,9},{9,10},{10,1... | collective-permute-start | bytes 1204232 | tf_op jit(solution)/shard_map/ppermute | solution.py:582
  25.3 19.9 %collective-permute-start.2 = (bf16[1280,128]{1,0:T(8,128)(2,1)}, bf16[1280,128]{1,0:T(8,128)(2,1)}, u32[]{:S(2)}, u32[]{:S(2)}) collective-permute-start(bf16[1280,128]{1,0:T(8,128)(2,1)} %get-tuple-element.38), channel_id=1, source_target_pairs={{0,64},{64,0},{128,192},{192,128},{1,65},{65,1},{129,193},{193,129... | collective-permute-start | bytes 983048 | tf_op jit(solution)/shard_map/ppermute | solution.py:22
  26.1 19.9 %collective-permute-start.3 = (bf16[1280,128]{1,0:T(8,128)(2,1)}, bf16[1280,128]{1,0:T(8,128)(2,1)}, u32[]{:S(2)}, u32[]{:S(2)}) collective-permute-start(bf16[1280,128]{1,0:T(8,128)(2,1)} %get-tuple-element.39), channel_id=1, source_target_pairs={{0,128},{64,192},{128,0},{192,64},{1,129},{65,193},{129,1},{193,65... | collective-permute-start | bytes 983048 | tf_op jit(solution)/shard_map/ppermute | solution.py:22
  28.5 17.4 %collective-permute-start.4 = (bf16[1280,128]{1,0:T(8,128)(2,1)}, bf16[1280,128]{1,0:T(8,128)(2,1)}, u32[]{:S(2)}, u32[]{:S(2)}) collective-permute-start(bf16[1280,128]{1,0:T(8,128)(2,1)} %get-tuple-element.40), channel_id=1, source_target_pairs={{0,192},{64,128},{128,64},{192,0},{1,193},{65,129},{129,65},{193,1... | collective-permute-start | bytes 983048 | tf_op jit(solution)/shard_map/ppermute | solution.py:22
  42.0 4.8 %collective-permute-start.5 = (bf16[768,128]{1,0:T(8,128)(2,1)}, bf16[768,128]{1,0:T(8,128)(2,1)S(1)}, u32[]{:S(2)}, u32[]{:S(2)}) collective-permute-start(bf16[768,128]{1,0:T(8,128)(2,1)} %get-tuple-element.41), channel_id=1, source_target_pairs={{0,64},{64,0},{128,192},{192,128},{1,65},{65,1},{129,193},{193,129... | collective-permute-start | bytes 589832 | tf_op jit(solution)/shard_map/ppermute | solution.py:22
  42.1 11.6 %collective-permute-start.6 = (bf16[768,128]{1,0:T(8,128)(2,1)}, bf16[768,128]{1,0:T(8,128)(2,1)S(1)}, u32[]{:S(2)}, u32[]{:S(2)}) collective-permute-start(bf16[768,128]{1,0:T(8,128)(2,1)} %get-tuple-element.42), channel_id=1, source_target_pairs={{0,128},{64,192},{128,0},{192,64},{1,129},{65,193},{129,1},{193,65... | collective-permute-start | bytes 589832 | tf_op jit(solution)/shard_map/ppermute | solution.py:22
  45.2 11.5 %collective-permute-start.7 = (bf16[768,128]{1,0:T(8,128)(2,1)}, bf16[768,128]{1,0:T(8,128)(2,1)S(1)}, u32[]{:S(2)}, u32[]{:S(2)}) collective-permute-start(bf16[768,128]{1,0:T(8,128)(2,1)} %get-tuple-element.43), channel_id=1, source_target_pairs={{0,192},{64,128},{128,64},{192,0},{1,193},{65,129},{129,65},{193,1... | collective-permute-start | bytes 589832 | tf_op jit(solution)/shard_map/ppermute | solution.py:22
  46.8 9.9 %copy-start.5 = (bf16[768,128]{1,0:T(8,128)(2,1)}, bf16[768,128]{1,0:T(8,128)(2,1)S(1)}, u32[]{:S(2)}) copy-start(bf16[768,128]{1,0:T(8,128)(2,1)S(1)} %collective-permute-done.5.refs_4_.refs_7_) | copy-start | bytes 589828
  53.7 3.0 %copy-start.6 = (bf16[768,128]{1,0:T(8,128)(2,1)}, bf16[768,128]{1,0:T(8,128)(2,1)S(1)}, u32[]{:S(2)}) copy-start(bf16[768,128]{1,0:T(8,128)(2,1)S(1)} %collective-permute-done.6.refs_5_.refs_8_) | copy-start | bytes 589828
  56.7 0.7 copy-start.7
  61.0 39.5 %copy-start.1 = (bf16[2816,128]{1,0:T(8,128)(2,1)S(1)}, bf16[2816,128]{1,0:T(8,128)(2,1)}, u32[]{:S(2)}) copy-start(bf16[2816,128]{1,0:T(8,128)(2,1)} %get-tuple-element.37.refs_0_) | copy-start | bytes 2162692
  61.0 57.5 %copy-start = (bf16[3328,128]{1,0:T(8,128)(2,1)S(1)}, bf16[3328,128]{1,0:T(8,128)(2,1)}, u32[]{:S(2)}) copy-start(bf16[3328,128]{1,0:T(8,128)(2,1)} %get-tuple-element.50.refs_3_) | copy-start | bytes 2555908
  61.0 60.1 %copy-start.2 = (bf16[2816,128]{1,0:T(8,128)(2,1)S(1)}, bf16[2816,128]{1,0:T(8,128)(2,1)}, u32[]{:S(2)}) copy-start(bf16[2816,128]{1,0:T(8,128)(2,1)} %get-tuple-element.48.refs_1_) | copy-start | bytes 2162692
  61.0 3.1 %collective-permute-start.8 = (f32[32,24,128]{2,1,0:T(8,128)}, f32[32,24,128]{2,1,0:T(8,128)S(1)}, u32[]{:S(2)}, u32[]{:S(2)}) collective-permute-start(f32[32,24,128]{2,1,0:T(8,128)} %get-tuple-element.45), channel_id=1, source_target_pairs={{0,1},{1,0},{2,3},{3,2},{4,5},{5,4},{6,7},{7,6},{8,9},{9,8},{10,11... | collective-permute-start | bytes 1179656 | tf_op jit(solution)/shard_map/ppermute | solution.py:26
  90.7 4.1 %collective-permute-start.10 = (f32[24,128]{1,0:T(8,128)S(1)}, f32[24,128]{1,0:T(8,128)S(1)}, u32[]{:S(2)}, u32[]{:S(2)}) collective-permute-start(f32[24,128]{1,0:T(8,128)S(1)} %reduce_sum.9), channel_id=1, source_target_pairs={{0,128},{64,192},{128,0},{192,64},{1,129},{65,193},{129,1},{193,65... | collective-permute-start | bytes 36872 | tf_op jit(solution)/shard_map/ppermute | solution.py:22
  90.8 4.0 %collective-permute-start.11 = (f32[24,128]{1,0:T(8,128)S(1)}, f32[24,128]{1,0:T(8,128)S(1)}, u32[]{:S(2)}, u32[]{:S(2)}) collective-permute-start(f32[24,128]{1,0:T(8,128)S(1)} %reduce_sum.9), channel_id=1, source_target_pairs={{0,192},{64,128},{128,64},{192,0},{1,193},{65,129},{129,65},{193,1... | collective-permute-start | bytes 36872 | tf_op jit(solution)/shard_map/ppermute | solution.py:22
  91.7 3.2 %collective-permute-start.9 = (f32[24,128]{1,0:T(8,128)S(1)}, f32[24,128]{1,0:T(8,128)S(1)}, u32[]{:S(2)}, u32[]{:S(2)}) collective-permute-start(f32[24,128]{1,0:T(8,128)S(1)} %reduce_sum.9), channel_id=1, source_target_pairs={{0,64},{64,0},{128,192},{192,128},{1,65},{65,1},{129,193},{193,129... | collective-permute-start | bytes 36872 | tf_op jit(solution)/shard_map/ppermute | solution.py:22
  95.7 16.3 %all-to-all-start.1 = ((f32[32,24,128]{2,1,0:T(8,128)}), f32[32,24,128]{2,1,0:T(8,128)S(1)}, u32[]{:S(2)}, u32[]{:S(2)}) async-start(f32[32,24,128]{2,1,0:T(8,128)} %broadcast_in_dim.3), calls=%async_computation.1 | async-start | bytes 786432 | tf_op jit(solution)/shard_map/all_to_all | solution.py:30
  100.5 20.6 %collective-permute-start.13 = (bf16[2816,128]{1,0:T(8,128)(2,1)S(1)}, bf16[2816,128]{1,0:T(8,128)(2,1)S(1)}, u32[]{:S(2)}, u32[]{:S(2)}) collective-permute-start(bf16[2816,128]{1,0:T(8,128)(2,1)S(1)} %copy-done.1), channel_id=1, source_target_pairs={{0,64},{64,0},{128,192},{192,128},{1,65},{65,1},{129,193},{193,129... | collective-permute-start | bytes 2162696 | tf_op jit(solution)/shard_map/ppermute | solution.py:22
  112.0 12.3 %copy-start.4 = (f32[32,24,128]{2,1,0:T(8,128)}, f32[32,24,128]{2,1,0:T(8,128)S(1)}, u32[]{:S(2)}) copy-start(f32[32,24,128]{2,1,0:T(8,128)S(1)} %all-to-all-done.1.own_hbm) | copy-start | bytes 1179652
  112.0 10.0 %collective-permute-start.12 = (f32[32,24,128]{2,1,0:T(8,128)S(1)}, f32[32,24,128]{2,1,0:T(8,128)S(1)}, u32[]{:S(2)}, u32[]{:S(2)}) collective-permute-start(f32[32,24,128]{2,1,0:T(8,128)S(1)} %all-to-all-done.1.own_hbm), channel_id=1, source_target_pairs={{0,1},{1,0},{2,3},{3,2},{4,5},{5,4},{6,7},{7,6},{8,9},{9,8},{10,11... | collective-permute-start | bytes 1179656 | tf_op jit(solution)/shard_map/ppermute | solution.py:26
  117.2 73.4 %collective-permute-start.16 = (bf16[3328,128]{1,0:T(8,128)(2,1)}, bf16[3328,128]{1,0:T(8,128)(2,1)}, u32[]{:S(2)}, u32[]{:S(2)}) collective-permute-start(bf16[3328,128]{1,0:T(8,128)(2,1)} %get-tuple-element.51), channel_id=1, source_target_pairs={{0,64},{64,0},{128,192},{192,128},{1,65},{65,1},{129,193},{193,129... | collective-permute-start | bytes 2555912 | tf_op jit(solution)/shard_map/ppermute | solution.py:22
  118.4 72.1 %collective-permute-start.17 = (bf16[3328,128]{1,0:T(8,128)(2,1)S(1)}, bf16[3328,128]{1,0:T(8,128)(2,1)}, u32[]{:S(2)}, u32[]{:S(2)}) collective-permute-start(bf16[3328,128]{1,0:T(8,128)(2,1)S(1)} %copy-done), channel_id=1, source_target_pairs={{0,128},{64,192},{128,0},{192,64},{1,129},{65,193},{129,1},{193,65... | collective-permute-start | bytes 2555912 | tf_op jit(solution)/shard_map/ppermute | solution.py:22
  120.0 70.6 %collective-permute-start.18 = (bf16[3328,128]{1,0:T(8,128)(2,1)}, bf16[3328,128]{1,0:T(8,128)(2,1)}, u32[]{:S(2)}, u32[]{:S(2)}) collective-permute-start(bf16[3328,128]{1,0:T(8,128)(2,1)} %get-tuple-element.52), channel_id=1, source_target_pairs={{0,192},{64,128},{128,64},{192,0},{1,193},{65,129},{129,65},{193,1... | collective-permute-start | bytes 2555912 | tf_op jit(solution)/shard_map/ppermute | solution.py:22
  121.1 0.9 copy-start.3
  121.1 52.0 %collective-permute-start.14 = (bf16[2816,128]{1,0:T(8,128)(2,1)S(1)}, bf16[2816,128]{1,0:T(8,128)(2,1)}, u32[]{:S(2)}, u32[]{:S(2)}) collective-permute-start(bf16[2816,128]{1,0:T(8,128)(2,1)S(1)} %copy-done.2), channel_id=1, source_target_pairs={{0,128},{64,192},{128,0},{192,64},{1,129},{65,193},{129,1},{193,65... | collective-permute-start | bytes 2162696 | tf_op jit(solution)/shard_map/ppermute | solution.py:22
  122.0 0.8 copy-start.8
  122.7 67.9 %collective-permute-start.15 = (bf16[2816,128]{1,0:T(8,128)(2,1)}, bf16[2816,128]{1,0:T(8,128)(2,1)}, u32[]{:S(2)}, u32[]{:S(2)}) collective-permute-start(bf16[2816,128]{1,0:T(8,128)(2,1)} %get-tuple-element.49.refs_2_), channel_id=1, source_target_pairs={{0,192},{64,128},{128,64},{192,0},{1,193},{65,129},{129,65},{193,1... | collective-permute-start | bytes 2162696 | tf_op jit(solution)/shard_map/ppermute | solution.py:22

commit v3 on v2

--- a/solution.py
+++ b/solution.py
@@ -198,20 +198,22 @@
 
 
 def spread_faces(perm_ref, east, north, count):
-    def one(g, _):
-        at0 = pl.multiple_of(g * 8, 8)
-        here = perm_ref[pl.ds(at0, 8)]
-        after = perm_ref[pl.ds(at0 + 8, 8)]
-        sub = lax.broadcasted_iota(jnp.int32, (8, LANES), 0)
-        shifted = pltpu.roll(jnp.where(sub == 0, after, here), 7, axis=0)
-        e = 0.12 * (here + shifted)
-        n = 0.12 * (here + pltpu.roll(here, LANES - 1, axis=1))
-        for i in range(count):
-            east[i, pl.ds(at0, 8)] = jnp.broadcast_to(e[:, i : i + 1], (8, LANES))
-            north[i, pl.ds(at0, 8)] = jnp.broadcast_to(n[:, i : i + 1], (8, LANES))
-        return 0
-
-    lax.fori_loop(0, (PAD + NY) // 8, one, 0, unroll=5)
+    here = perm_ref[...]
+    after = jnp.concatenate([here[1:], here[:1]], 0)
+    row = lax.broadcasted_iota(jnp.int32, (256, 256), 0) & 127
+    second = lax.broadcasted_iota(jnp.int32, (256, 256), 1) >> 7
+    faces = []
+    for value in (0.12 * (here + after), 0.12 * (here + pltpu.roll(here, LANES - 1, axis=1))):
+        high = value.astype(jnp.bfloat16)
+        low = (value - high.astype(jnp.float32)).astype(jnp.bfloat16)
+        faces.append(jnp.concatenate([high, low], 1))
+    for i in range(0, count, 2):
+        pick = jnp.where(row == second + i, 1.0, 0.0).astype(jnp.bfloat16)
+        for face, out in zip(faces, (east, north)):
+            both = jnp.dot(face, pick, preferred_element_type=jnp.float32)
+            out[i] = both[:, :LANES]
+            if i + 1 < count:
+                out[i + 1] = both[:, LANES:]
 
 
 def set_perm(perm_ref, rows):

time: 198 us -> 189 us (0.955)
  Pallas kernels: 55.4 us -> 45.5 us
    pallas_call x1, Pallas kernels: 15 us -> 9.7 us  [inner_call(): pl.pallas_call(inner_rows, out_shape=[half(INNER)] * 3 + [half(PIECE + OU...]
    pallas_call x1, Pallas kernels: 12.7 us -> 8.31 us  [outer_call(): pl.pallas_call(outer_rows, out_shape=[half(OUTER)] * 3 + [half(PIECE + OU...]
  transfers between devices with their start and end apart: 20 -> 20, of which waited for: 8 -> 9; matrix products, arithmetic and copies ran while one was open for 0% -> 0% of each run, Pallas kernels for 23% -> 19%
where the time goes in v3:
time: 189 us
  waiting for transfers between devices  74.5 us (39%)
  Pallas kernels  45.5 us (24%)
  starting transfers between devices  36.7 us (19%)
  blocking collectives  24.8 us (13%)
  local copies, waits for them, and re-layouts  5.22 us (3%)
    ppermute x15, waiting for transfers between devices, case_swap(): lax.ppermute(value, 'case', [(source, source ^ apart) for source in range...  62.8 us
    all_to_all x1, blocking collectives, plane_exchange(): return lax.all_to_all(value, 'tile', 0, 0, axis_index_groups=PLANES)  24.8 us
    ppermute x15, starting transfers between devices, case_swap(): lax.ppermute(value, 'case', [(source, source ^ apart) for source in range...  17.8 us
    pallas_call x1, Pallas kernels, mixing_call(): pl.pallas_call(functools.partial(mixing, cells), out_shape=(shape, shape)...  17.4 us
    all_to_all x1, waiting for transfers between devices, plane_exchange(): return lax.all_to_all(value, 'tile', 0, 0, axis_index_groups=PLANES)  10.1 us
    pallas_call x1, Pallas kernels, inner_call(): pl.pallas_call(inner_rows, out_shape=[half(INNER)] * 3 + [half(PIECE + OU...  9.7 us
    pallas_call x1, Pallas kernels, outer_call(): pl.pallas_call(outer_rows, out_shape=[half(OUTER)] * 3 + [half(PIECE + OU...  8.31 us
    ppermute x2, starting transfers between devices, core_swap(): lax.ppermute(value, 'tile', [(source, source ^ 1) for source in range(64)])  6.86 us
  transfers between devices with their start and end apart: 20, of which 9 were waited for; matrix products, arithmetic and copies ran while one was open for 0% of the time, Pallas kernels for 19%

profile of v3, /device:TPU:1, one launch (start us, length us, event | category | flops | bytes accessed | tf_op | source)
XLA Modules:
  0.0 188.7 jit_solution(11877891667231184029)
XLA Ops:
  0.8 1.2 fusion
  2.2 5.1 %collective-permute-start.1 = (bf16[1568,128]{1,0:T(8,128)(2,1)S(1)}, bf16[1568,128]{1,0:T(8,128)(2,1)}, u32[]{:S(2)}, u32[]{:S(2)}) collective-permute-start(bf16[1568,128]{1,0:T(8,128)(2,1)S(1)} %concatenate.7), channel_id=1, source_target_pairs={{1,0},{2,1},{3,2},{4,3},{5,4},{6,5},{7,6},{8,7},{9,8},{10,9},{11,1... | collective-permute-start | bytes 1204232 | tf_op jit(solution)/shard_map/ppermute | solution.py:585
  7.7 1.9 %collective-permute-start = (bf16[1568,128]{1,0:T(8,128)(2,1)S(1)}, bf16[1568,128]{1,0:T(8,128)(2,1)}, u32[]{:S(2)}, u32[]{:S(2)}) collective-permute-start(bf16[1568,128]{1,0:T(8,128)(2,1)S(1)} %concatenate.6), channel_id=1, source_target_pairs={{0,1},{1,2},{2,3},{3,4},{4,5},{5,6},{6,7},{7,8},{8,9},{9,10},{10,1... | collective-permute-start | bytes 1204232 | tf_op jit(solution)/shard_map/ppermute | solution.py:584
  10.3 9.7 %shard_map.46 = (bf16[1280,128]{1,0:T(8,128)(2,1)}, bf16[1280,128]{1,0:T(8,128)(2,1)}, bf16[1280,128]{1,0:T(8,128)(2,1)}, bf16[2816,128]{1,0:T(8,128)(2,1)}, bf1...) custom-call(s32[1]{0:T(128)} %bitcast.me_ref, ...), custom_call_target="tpu_custom_call" | custom-call | flops 419430400 | bytes 9437184 | tf_op jit(solution)/shard_map/pallas_call | solution.py:416
  20.8 2.5 %collective-permute-start.3 = (bf16[1280,128]{1,0:T(8,128)(2,1)}, bf16[1280,128]{1,0:T(8,128)(2,1)}, u32[]{:S(2)}, u32[]{:S(2)}) collective-permute-start(bf16[1280,128]{1,0:T(8,128)(2,1)} %get-tuple-element.39), channel_id=1, source_target_pairs={{0,128},{64,192},{128,0},{192,64},{1,129},{65,193},{129,1},{193,65... | collective-permute-start | bytes 983048 | tf_op jit(solution)/shard_map/ppermute | solution.py:22
  23.9 8.3 %shard_map.47 = (bf16[768,128]{1,0:T(8,128)(2,1)}, bf16[768,128]{1,0:T(8,128)(2,1)}, bf16[768,128]{1,0:T(8,128)(2,1)}, bf16[2816,128]{1,0:T(8,128)(2,1)}, bf16[2...) custom-call(s32[1]{0:T(128)} %bitcast.me_ref, ...), custom_call_target="tpu_custom_call", output_to_operand_aliasing={{3}: (9, {}), {4}: (10, {}), {5}: (11, {}), {6}: (12, {}), ... | custom-call | flops 209715200 | bytes 9437184 | tf_op jit(solution)/shard_map/pallas_call | solution.py:431
  32.4 3.1 %collective-permute-start.6 = (bf16[768,128]{1,0:T(8,128)(2,1)}, bf16[768,128]{1,0:T(8,128)(2,1)S(1)}, u32[]{:S(2)}, u32[]{:S(2)}) collective-permute-start(bf16[768,128]{1,0:T(8,128)(2,1)} %get-tuple-element.42), channel_id=1, source_target_pairs={{0,128},{64,192},{128,0},{192,64},{1,129},{65,193},{129,1},{193,65... | collective-permute-start | bytes 589832 | tf_op jit(solution)/shard_map/ppermute | solution.py:22
  36.2 2.1 %collective-permute-done.3.refs_2_.refs_5_ = bf16[1280,128]{1,0:T(8,128)(2,1)} collective-permute-done((bf16[1280,128]{1,0:T(8,128)(2,1)}, bf16[1280,128]{1,0:T(8,128)(2,1)}, u32[]{:S(2)}, u32[]{:S(2)}) %collective-permute-start.3) | collective-permute-done | bytes 327712 | tf_op jit(solution)/shard_map/ppermute | solution.py:22
  38.3 2.1 %collective-permute-done.4.refs_3_.refs_6_ = bf16[1280,128]{1,0:T(8,128)(2,1)} collective-permute-done((bf16[1280,128]{1,0:T(8,128)(2,1)}, bf16[1280,128]{1,0:T(8,128)(2,1)}, u32[]{:S(2)}, u32[]{:S(2)}) %collective-permute-start.4) | collective-permute-done | bytes 327712 | tf_op jit(solution)/shard_map/ppermute | solution.py:22
  40.4 6.3 %collective-permute-done.6.refs_5_.refs_8_ = bf16[768,128]{1,0:T(8,128)(2,1)S(1)} collective-permute-done((bf16[768,128]{1,0:T(8,128)(2,1)}, bf16[768,128]{1,0:T(8,128)(2,1)S(1)}, u32[]{:S(2)}, u32[]{:S(2)}) %collective-permute-start.6) | collective-permute-done | bytes 196640 | tf_op jit(solution)/shard_map/ppermute | solution.py:22
  46.7 2.0 %collective-permute-done.7.refs_6_.refs_9_ = bf16[768,128]{1,0:T(8,128)(2,1)S(1)} collective-permute-done((bf16[768,128]{1,0:T(8,128)(2,1)}, bf16[768,128]{1,0:T(8,128)(2,1)S(1)}, u32[]{:S(2)}, u32[]{:S(2)}) %collective-permute-start.7) | collective-permute-done | bytes 196640 | tf_op jit(solution)/shard_map/ppermute | solution.py:22
  49.4 3.5 %shard_map.48 = (f32[32,24,128]{2,1,0:T(8,128)}, f32[32,24,128]{2,1,0:T(8,128)}) custom-call(s32[1]{0:T(128)} %bitcast.me_ref, s32[1]{0:T(128)S(6)} %and.5.core_ref, bf16[2816,128]{1,0:T(8,128)(2,1)} %get-tuple-element.37.refs_0_, bf16[1280,128]{1,0:T(8,128)(2,1)} %collective-permute-done.2.refs_1_.refs_4_, ...), custom_call_target="tpu_custom_call" | custom-call | flops 1073741824 | bytes 3145728 | tf_op jit(solution)/shard_map/pallas_call | solution.py:487
  53.0 1.6 collective-permute-start.8
  54.5 1.6 collective-permute-done.8
  56.1 1.0 add.12
  57.1 24.8 %all_to_all.10 = f32[32,24,128]{2,1,0:T(8,128)S(1)} all-to-all(f32[32,24,128]{2,1,0:T(8,128)S(1)} %add.12), channel_id=1, replica_groups={{0,2,4,6,8,10,12,14,16,18,20,22,24,26,28,30,32,34,36,38,40,42,44,46,48,..., dimensions={0} | all-to-all | bytes 786432 | tf_op jit(solution)/shard_map/all_to_all | solution.py:30
  82.0 1.1 collective-permute-start.11
  83.1 1.5 collective-permute-start.9
  84.7 1.4 collective-permute-done.10
  86.1 0.8 broadcast_in_dim.3
  86.9 5.0 %all-to-all-start.1 = ((f32[32,24,128]{2,1,0:T(8,128)}), f32[32,24,128]{2,1,0:T(8,128)S(1)}, u32[]{:S(2)}, u32[]{:S(2)}) async-start(f32[32,24,128]{2,1,0:T(8,128)} %broadcast_in_dim.3), calls=%async_computation.1 | async-start | bytes 786432 | tf_op jit(solution)/shard_map/all_to_all | solution.py:30
  91.9 1.3 collective-permute-start.13
  93.2 10.1 %all-to-all-done.1.own_hbm = f32[32,24,128]{2,1,0:T(8,128)S(1)} async-done(((f32[32,24,128]{2,1,0:T(8,128)}), f32[32,24,128]{2,1,0:T(8,128)S(1)}, u32[]{:S(2)}, u32[]{:S(2)}) %all-to-all-start.1) | async-done | bytes 393248 | tf_op jit(solution)/shard_map/all_to_all | solution.py:30
  103.3 5.3 %collective-permute-start.12 = (f32[32,24,128]{2,1,0:T(8,128)S(1)}, f32[32,24,128]{2,1,0:T(8,128)S(1)}, u32[]{:S(2)}, u32[]{:S(2)}) collective-permute-start(f32[32,24,128]{2,1,0:T(8,128)S(1)} %all-to-all-done.1.own_hbm), channel_id=1, source_target_pairs={{0,1},{1,0},{2,3},{3,2},{4,5},{5,4},{6,7},{7,6},{8,9},{9,8},{10,11... | collective-permute-start | bytes 1179656 | tf_op jit(solution)/shard_map/ppermute | solution.py:26
  108.6 1.2 collective-permute-start.16
  109.8 1.5 collective-permute-start.17
  111.3 1.1 collective-permute-start.18
  114.1 1.6 collective-permute-start.15
  115.7 17.4 %shard_map.49 = (bf16[512,128]{1,0:T(8,128)(2,1)}, bf16[512,128]{1,0:T(8,128)(2,1)}) custom-call(s32[1]{0:T(128)} %bitcast.me_ref, s32[1]{0:T(128)S(6)} %and.5.core_ref, f32[32,24,128]{2,1,0:T(8,128)} %copy-done.4, f32[32,24,128]{2,1,0:T(8,128)} %copy-done.8, s32[2,256,128]{2,1,0:T(8,128)} %start_ref.1), custom_call_target="tpu_custom_call" | custom-call | flops 1073741824 | bytes 1048576 | tf_op jit(solution)/shard_map/pallas_call | solution.py:502
  133.1 31.3 %collective-permute-done.14.refs_11_ = bf16[2816,128]{1,0:T(8,128)(2,1)} collective-permute-done((bf16[2816,128]{1,0:T(8,128)(2,1)S(1)}, bf16[2816,128]{1,0:T(8,128)(2,1)}, u32[]{:S(2)}, u32[]{:S(2)}) %collective-permute-start.14) | collective-permute-done | bytes 720928 | tf_op jit(solution)/shard_map/ppermute | solution.py:22
  164.4 17.5 %collective-permute-done.15.refs_12_ = bf16[2816,128]{1,0:T(8,128)(2,1)} collective-permute-done((bf16[2816,128]{1,0:T(8,128)(2,1)}, bf16[2816,128]{1,0:T(8,128)(2,1)}, u32[]{:S(2)}, u32[]{:S(2)}) %collective-permute-start.15) | collective-permute-done | bytes 720928 | tf_op jit(solution)/shard_map/ppermute | solution.py:22
  182.0 6.6 %shard_map.50 = bf16[16,512,128]{2,1,0:T(8,128)(2,1)} custom-call(s32[1]{0:T(128)} %bitcast.me_ref, bf16[512,128]{1,0:T(8,128)(2,1)} %get-tuple-element.46.high_ref, bf16[512,128]{1,0:T(8,128)(2,1)} %get-tuple-element.47.low_ref, bf16[2816,128]{1,0:T(8,128)(2,1)} %get-tuple-element.37.refs_0_, bf16[2816,128]{1,0:T(8,128)(2,1)} %get-tuple-element.48.refs_1_, ...), custom_call_target="tpu_custom_call" | custom-call | flops 2147483648 | bytes 10485760 | tf_op jit(solution)/shard_map/pallas_call | solution.py:553
  (45 shorter events, 6.2 us)
Async XLA Ops:
  2.2 21.7 %collective-permute-start.1 = (bf16[1568,128]{1,0:T(8,128)(2,1)S(1)}, bf16[1568,128]{1,0:T(8,128)(2,1)}, u32[]{:S(2)}, u32[]{:S(2)}) collective-permute-start(bf16[1568,128]{1,0:T(8,128)(2,1)S(1)} %concatenate.7), channel_id=1, source_target_pairs={{1,0},{2,1},{3,2},{4,3},{5,4},{6,5},{7,6},{8,7},{9,8},{10,9},{11,1... | collective-permute-start | bytes 1204232 | tf_op jit(solution)/shard_map/ppermute | solution.py:585
  7.7 16.2 %collective-permute-start = (bf16[1568,128]{1,0:T(8,128)(2,1)S(1)}, bf16[1568,128]{1,0:T(8,128)(2,1)}, u32[]{:S(2)}, u32[]{:S(2)}) collective-permute-start(bf16[1568,128]{1,0:T(8,128)(2,1)S(1)} %concatenate.6), channel_id=1, source_target_pairs={{0,1},{1,2},{2,3},{3,4},{4,5},{5,6},{6,7},{7,8},{8,9},{9,10},{10,1... | collective-permute-start | bytes 1204232 | tf_op jit(solution)/shard_map/ppermute | solution.py:584
  20.0 15.5 %collective-permute-start.2 = (bf16[1280,128]{1,0:T(8,128)(2,1)}, bf16[1280,128]{1,0:T(8,128)(2,1)}, u32[]{:S(2)}, u32[]{:S(2)}) collective-permute-start(bf16[1280,128]{1,0:T(8,128)(2,1)} %get-tuple-element.38), channel_id=1, source_target_pairs={{0,64},{64,0},{128,192},{192,128},{1,65},{65,1},{129,193},{193,129... | collective-permute-start | bytes 983048 | tf_op jit(solution)/shard_map/ppermute | solution.py:22
  20.8 17.6 %collective-permute-start.3 = (bf16[1280,128]{1,0:T(8,128)(2,1)}, bf16[1280,128]{1,0:T(8,128)(2,1)}, u32[]{:S(2)}, u32[]{:S(2)}) collective-permute-start(bf16[1280,128]{1,0:T(8,128)(2,1)} %get-tuple-element.39), channel_id=1, source_target_pairs={{0,128},{64,192},{128,0},{192,64},{1,129},{65,193},{129,1},{193,65... | collective-permute-start | bytes 983048 | tf_op jit(solution)/shard_map/ppermute | solution.py:22
  23.2 17.2 %collective-permute-start.4 = (bf16[1280,128]{1,0:T(8,128)(2,1)}, bf16[1280,128]{1,0:T(8,128)(2,1)}, u32[]{:S(2)}, u32[]{:S(2)}) collective-permute-start(bf16[1280,128]{1,0:T(8,128)(2,1)} %get-tuple-element.40), channel_id=1, source_target_pairs={{0,192},{64,128},{128,64},{192,0},{1,193},{65,129},{129,65},{193,1... | collective-permute-start | bytes 983048 | tf_op jit(solution)/shard_map/ppermute | solution.py:22
  32.3 8.1 %collective-permute-start.5 = (bf16[768,128]{1,0:T(8,128)(2,1)}, bf16[768,128]{1,0:T(8,128)(2,1)S(1)}, u32[]{:S(2)}, u32[]{:S(2)}) collective-permute-start(bf16[768,128]{1,0:T(8,128)(2,1)} %get-tuple-element.41), channel_id=1, source_target_pairs={{0,64},{64,0},{128,192},{192,128},{1,65},{65,1},{129,193},{193,129... | collective-permute-start | bytes 589832 | tf_op jit(solution)/shard_map/ppermute | solution.py:22
  32.4 14.3 %collective-permute-start.6 = (bf16[768,128]{1,0:T(8,128)(2,1)}, bf16[768,128]{1,0:T(8,128)(2,1)S(1)}, u32[]{:S(2)}, u32[]{:S(2)}) collective-permute-start(bf16[768,128]{1,0:T(8,128)(2,1)} %get-tuple-element.42), channel_id=1, source_target_pairs={{0,128},{64,192},{128,0},{192,64},{1,129},{65,193},{129,1},{193,65... | collective-permute-start | bytes 589832 | tf_op jit(solution)/shard_map/ppermute | solution.py:22
  35.5 13.2 %collective-permute-start.7 = (bf16[768,128]{1,0:T(8,128)(2,1)}, bf16[768,128]{1,0:T(8,128)(2,1)S(1)}, u32[]{:S(2)}, u32[]{:S(2)}) collective-permute-start(bf16[768,128]{1,0:T(8,128)(2,1)} %get-tuple-element.43), channel_id=1, source_target_pairs={{0,192},{64,128},{128,64},{192,0},{1,193},{65,129},{129,65},{193,1... | collective-permute-start | bytes 589832 | tf_op jit(solution)/shard_map/ppermute | solution.py:22
  40.4 8.3 %copy-start.5 = (bf16[768,128]{1,0:T(8,128)(2,1)}, bf16[768,128]{1,0:T(8,128)(2,1)S(1)}, u32[]{:S(2)}) copy-start(bf16[768,128]{1,0:T(8,128)(2,1)S(1)} %collective-permute-done.5.refs_4_.refs_7_) | copy-start | bytes 589828
  46.7 2.0 %copy-start.6 = (bf16[768,128]{1,0:T(8,128)(2,1)}, bf16[768,128]{1,0:T(8,128)(2,1)S(1)}, u32[]{:S(2)}) copy-start(bf16[768,128]{1,0:T(8,128)(2,1)S(1)} %collective-permute-done.6.refs_5_.refs_8_) | copy-start | bytes 589828
  48.7 0.7 copy-start.7
  52.9 38.9 %copy-start.1 = (bf16[2816,128]{1,0:T(8,128)(2,1)S(1)}, bf16[2816,128]{1,0:T(8,128)(2,1)}, u32[]{:S(2)}) copy-start(bf16[2816,128]{1,0:T(8,128)(2,1)} %get-tuple-element.37.refs_0_) | copy-start | bytes 2162692
  52.9 56.9 %copy-start = (bf16[3328,128]{1,0:T(8,128)(2,1)S(1)}, bf16[3328,128]{1,0:T(8,128)(2,1)}, u32[]{:S(2)}) copy-start(bf16[3328,128]{1,0:T(8,128)(2,1)} %get-tuple-element.50.refs_3_) | copy-start | bytes 2555908
  53.0 59.5 %copy-start.2 = (bf16[2816,128]{1,0:T(8,128)(2,1)S(1)}, bf16[2816,128]{1,0:T(8,128)(2,1)}, u32[]{:S(2)}) copy-start(bf16[2816,128]{1,0:T(8,128)(2,1)} %get-tuple-element.48.refs_1_) | copy-start | bytes 2162692
  53.0 3.1 %collective-permute-start.8 = (f32[32,24,128]{2,1,0:T(8,128)}, f32[32,24,128]{2,1,0:T(8,128)S(1)}, u32[]{:S(2)}, u32[]{:S(2)}) collective-permute-start(f32[32,24,128]{2,1,0:T(8,128)} %get-tuple-element.45), channel_id=1, source_target_pairs={{0,1},{1,0},{2,3},{3,2},{4,5},{5,4},{6,7},{7,6},{8,9},{9,8},{10,11... | collective-permute-start | bytes 1179656 | tf_op jit(solution)/shard_map/ppermute | solution.py:26
  81.9 4.1 %collective-permute-start.10 = (f32[24,128]{1,0:T(8,128)S(1)}, f32[24,128]{1,0:T(8,128)S(1)}, u32[]{:S(2)}, u32[]{:S(2)}) collective-permute-start(f32[24,128]{1,0:T(8,128)S(1)} %reduce_sum.9), channel_id=1, source_target_pairs={{0,128},{64,192},{128,0},{192,64},{1,129},{65,193},{129,1},{193,65... | collective-permute-start | bytes 36872 | tf_op jit(solution)/shard_map/ppermute | solution.py:22
  82.0 4.0 %collective-permute-start.11 = (f32[24,128]{1,0:T(8,128)S(1)}, f32[24,128]{1,0:T(8,128)S(1)}, u32[]{:S(2)}, u32[]{:S(2)}) collective-permute-start(f32[24,128]{1,0:T(8,128)S(1)} %reduce_sum.9), channel_id=1, source_target_pairs={{0,192},{64,128},{128,64},{192,0},{1,193},{65,129},{129,65},{193,1... | collective-permute-start | bytes 36872 | tf_op jit(solution)/shard_map/ppermute | solution.py:22
  83.1 2.9 %collective-permute-start.9 = (f32[24,128]{1,0:T(8,128)S(1)}, f32[24,128]{1,0:T(8,128)S(1)}, u32[]{:S(2)}, u32[]{:S(2)}) collective-permute-start(f32[24,128]{1,0:T(8,128)S(1)} %reduce_sum.9), channel_id=1, source_target_pairs={{0,64},{64,0},{128,192},{192,128},{1,65},{65,1},{129,193},{193,129... | collective-permute-start | bytes 36872 | tf_op jit(solution)/shard_map/ppermute | solution.py:22
  86.9 16.4 %all-to-all-start.1 = ((f32[32,24,128]{2,1,0:T(8,128)}), f32[32,24,128]{2,1,0:T(8,128)S(1)}, u32[]{:S(2)}, u32[]{:S(2)}) async-start(f32[32,24,128]{2,1,0:T(8,128)} %broadcast_in_dim.3), calls=%async_computation.1 | async-start | bytes 786432 | tf_op jit(solution)/shard_map/all_to_all | solution.py:30
  91.9 20.6 %collective-permute-start.13 = (bf16[2816,128]{1,0:T(8,128)(2,1)S(1)}, bf16[2816,128]{1,0:T(8,128)(2,1)S(1)}, u32[]{:S(2)}, u32[]{:S(2)}) collective-permute-start(bf16[2816,128]{1,0:T(8,128)(2,1)S(1)} %copy-done.1), channel_id=1, source_target_pairs={{0,64},{64,0},{128,192},{192,128},{1,65},{65,1},{129,193},{193,129... | collective-permute-start | bytes 2162696 | tf_op jit(solution)/shard_map/ppermute | solution.py:22
  103.3 12.4 %copy-start.4 = (f32[32,24,128]{2,1,0:T(8,128)}, f32[32,24,128]{2,1,0:T(8,128)S(1)}, u32[]{:S(2)}) copy-start(f32[32,24,128]{2,1,0:T(8,128)S(1)} %all-to-all-done.1.own_hbm) | copy-start | bytes 1179652
  103.3 10.0 %collective-permute-start.12 = (f32[32,24,128]{2,1,0:T(8,128)S(1)}, f32[32,24,128]{2,1,0:T(8,128)S(1)}, u32[]{:S(2)}, u32[]{:S(2)}) collective-permute-start(f32[32,24,128]{2,1,0:T(8,128)S(1)} %all-to-all-done.1.own_hbm), channel_id=1, source_target_pairs={{0,1},{1,0},{2,3},{3,2},{4,5},{5,4},{6,7},{7,6},{8,9},{9,8},{10,11... | collective-permute-start | bytes 1179656 | tf_op jit(solution)/shard_map/ppermute | solution.py:26
  108.6 73.4 %collective-permute-start.16 = (bf16[3328,128]{1,0:T(8,128)(2,1)}, bf16[3328,128]{1,0:T(8,128)(2,1)}, u32[]{:S(2)}, u32[]{:S(2)}) collective-permute-start(bf16[3328,128]{1,0:T(8,128)(2,1)} %get-tuple-element.51), channel_id=1, source_target_pairs={{0,64},{64,0},{128,192},{192,128},{1,65},{65,1},{129,193},{193,129... | collective-permute-start | bytes 2555912 | tf_op jit(solution)/shard_map/ppermute | solution.py:22
  109.8 72.1 %collective-permute-start.17 = (bf16[3328,128]{1,0:T(8,128)(2,1)S(1)}, bf16[3328,128]{1,0:T(8,128)(2,1)}, u32[]{:S(2)}, u32[]{:S(2)}) collective-permute-start(bf16[3328,128]{1,0:T(8,128)(2,1)S(1)} %copy-done), channel_id=1, source_target_pairs={{0,128},{64,192},{128,0},{192,64},{1,129},{65,193},{129,1},{193,65... | collective-permute-start | bytes 2555912 | tf_op jit(solution)/shard_map/ppermute | solution.py:22
  111.3 70.6 %collective-permute-start.18 = (bf16[3328,128]{1,0:T(8,128)(2,1)}, bf16[3328,128]{1,0:T(8,128)(2,1)}, u32[]{:S(2)}, u32[]{:S(2)}) collective-permute-start(bf16[3328,128]{1,0:T(8,128)(2,1)} %get-tuple-element.52), channel_id=1, source_target_pairs={{0,192},{64,128},{128,64},{192,0},{1,193},{65,129},{129,65},{193,1... | collective-permute-start | bytes 2555912 | tf_op jit(solution)/shard_map/ppermute | solution.py:22
  112.5 0.9 copy-start.3
  112.5 52.0 %collective-permute-start.14 = (bf16[2816,128]{1,0:T(8,128)(2,1)S(1)}, bf16[2816,128]{1,0:T(8,128)(2,1)}, u32[]{:S(2)}, u32[]{:S(2)}) collective-permute-start(bf16[2816,128]{1,0:T(8,128)(2,1)S(1)} %copy-done.2), channel_id=1, source_target_pairs={{0,128},{64,192},{128,0},{192,64},{1,129},{65,193},{129,1},{193,65... | collective-permute-start | bytes 2162696 | tf_op jit(solution)/shard_map/ppermute | solution.py:22
  113.4 0.8 copy-start.8
  114.1 67.9 %collective-permute-start.15 = (bf16[2816,128]{1,0:T(8,128)(2,1)}, bf16[2816,128]{1,0:T(8,128)(2,1)}, u32[]{:S(2)}, u32[]{:S(2)}) collective-permute-start(bf16[2816,128]{1,0:T(8,128)(2,1)} %get-tuple-element.49.refs_2_), channel_id=1, source_target_pairs={{0,192},{64,128},{128,64},{192,0},{1,193},{65,129},{129,65},{193,1... | collective-permute-start | bytes 2162696 | tf_op jit(solution)/shard_map/ppermute | solution.py:22

commit v4 on v3

--- a/solution.py
+++ b/solution.py
@@ -65,43 +65,60 @@
     lane = lax.broadcasted_iota(jnp.int32, (8, 128), 1)
     sub = lax.broadcasted_iota(jnp.int32, (8, 128), 0)
     tiles = [[m[8 * b : 8 * b + 8] for b in range(16)] for m in mats]
-    for k in range(16):
-        first = 8 * k
-        block = (lane >= first) & (lane < first + 8)
+    for big in range(4):
         for a in tiles:
-            rows = [spread(a[k], 0, r, 8) for r in range(8)]
-            piv = [
-                [spread(rows[r], 1, first + s, 128) if s >= r else None for s in range(8)]
-                for r in range(8)
-            ]
-            inv = [None] * 8
-            mul = [[None] * 8 for _ in range(8)]
-            for r in range(8):
-                inv[r] = 1.0 / piv[r][r]
-                for s in range(r + 1, 8):
-                    mul[r][s] = piv[r][s] * inv[r]
-                for s in range(r + 1, 8):
-                    for t in range(s, 8):
-                        piv[s][t] = piv[s][t] - mul[r][s] * piv[r][t]
-            for s in range(8):
-                rows[s] = jnp.where(block, jnp.where(lane == first + s, 1.0, 0.0), rows[s])
-            for s in range(8):
-                for r in range(s):
-                    rows[s] = rows[s] - mul[r][s] * rows[r]
-            scaled = [rows[r] * inv[r] for r in range(8)]
-            for b in range(k + 1, 16):
-                col = [spread(a[b], 1, first + r, 128) for r in range(8)]
+            left, right = [], []
+            for k in range(4 * big, 4 * big + 4):
+                first = 8 * k
+                block = (lane >= first) & (lane < first + 8)
+                rows = [spread(a[k], 0, r, 8) for r in range(8)]
+                piv = [
+                    [spread(rows[r], 1, first + s, 128) if s >= r else None for s in range(8)]
+                    for r in range(8)
+                ]
+                inv = [None] * 8
+                mul = [[None] * 8 for _ in range(8)]
                 for r in range(8):
+                    inv[r] = 1.0 / piv[r][r]
                     for s in range(r + 1, 8):
-                        col[s] = col[s] - col[r] * mul[r][s]
-                new = jnp.where(block, 0.0, a[b])
-                for r in range(8):
-                    new = new - col[r] * scaled[r]
-                a[b] = new
-            done = jnp.zeros((8, 128), jnp.float32)
-            for r in range(8):
-                done = jnp.where(sub == r, rows[r] * lax.rsqrt(piv[r][r]), done)
-            a[k] = jnp.where(lane < first + 8, done, 0.0)
+                        mul[r][s] = piv[r][s] * inv[r]
+                    for s in range(r + 1, 8):
+                        for t in range(s, 8):
+                            piv[s][t] = piv[s][t] - mul[r][s] * piv[r][t]
+                for s in range(8):
+                    rows[s] = jnp.where(block, jnp.where(lane == first + s, 1.0, 0.0), rows[s])
+                for s in range(8):
+                    for r in range(s):
+                        rows[s] = rows[s] - mul[r][s] * rows[r]
+                scaled = [rows[r] * inv[r] for r in range(8)]
+                for b in range(k + 1, 4 * big + 4):
+                    col = [spread(a[b], 1, first + r, 128) for r in range(8)]
+                    for r in range(8):
+                        for s in range(r + 1, 8):
+                            col[s] = col[s] - col[r] * mul[r][s]
+                    new = jnp.where(block, 0.0, a[b])
+                    for r in range(8):
+                        new = new - col[r] * scaled[r]
+                    a[b] = new
+                plain, pivots, inverse = rows[0], piv[0][0], inv[0]
+                for r in range(1, 8):
+                    plain = jnp.where(sub == r, rows[r], plain)
+                    pivots = jnp.where(sub == r, piv[r][r], pivots)
+                    inverse = jnp.where(sub == r, inv[r], inverse)
+                left.append(plain)
+                later = (lane >= first + 8) & (lane < 32 * (big + 1))
+                right.append(jnp.where(later, 0.0, plain * inverse))
+                a[k] = jnp.where(lane < first + 8, plain * lax.rsqrt(pivots), 0.0)
+            if big < 3:
+                after = 32 * (big + 1)
+                x = parts_of(jnp.concatenate(left, 0))
+                y = parts_of(jnp.concatenate(right, 0))
+                x = jnp.concatenate([x[0], x[0], x[1], x[0], x[2], x[1]], 0)
+                y = jnp.concatenate([y[0], y[1], y[0], y[2], y[0], y[1]], 0)
+                update = lax.dot_general(x, y, ATB, preferred_element_type=jnp.float32)
+                used = (lane >= 32 * big) & (lane < after)
+                for b in range(4 * big + 4, 16):
+                    a[b] = jnp.where(used, 0.0, a[b]) - update[8 * b : 8 * b + 8]
     return [jnp.concatenate(a, 0) for a in tiles]
 
 
@@ -313,7 +330,7 @@
     for copy in edges_out:
         copy.start()
     sweep(first, east, north, 3, 3, 10, into_snap(snap, 0, scale_ref))
-    moves = ((near, 1, 0, INNER), (late, 3, 0, INNER), (late, 2, PIECE, INNER))
+    moves = ((near, 1, 0, INNER), (near, 2, PIECE, INNER), (late, 3, 0, INNER))
     for copy in edges_out + send_out(me, snap, singles, moves, sems):
         copy.wait()
 
@@ -393,7 +410,7 @@
 
     sweep(low2, east, north, 1, 3, 3, into_snap(snap, 0, scale_ref))
     sweep(high2, east, north, 1, 8, 3, into_snap(snap, 3, scale_ref))
-    moves = ((near, 1, INNER, OUTER), (near, 2, PIECE, OUTER), (late, 3, INNER, OUTER))
+    moves = ((near, 1, INNER, OUTER), (late, 3, INNER, OUTER), (late, 2, PIECE, OUTER))
     for copy in send_out(me, snap, singles, moves, sems):
         copy.wait()
 
@@ -415,7 +432,7 @@
     edge = jax.ShapeDtypeStruct((4, WIDE, LANES), jnp.float32)
     return pl.pallas_call(
         inner_rows,
-        out_shape=[half(INNER)] * 3 + [half(PIECE + OUTER)] * 3 + [half(PIECE + INNER)] * 3 + [edge] * 2,
+        out_shape=[half(INNER)] * 3 + [half(PIECE + INNER)] * 3 + [half(PIECE + OUTER)] * 3 + [edge] * 2,
         in_specs=[SM, SM, ANY, VM],
         out_specs=[ANY] * 11,
         scratch_shapes=[planes(16), planes(16), planes(15), planes(15)]
@@ -430,7 +447,7 @@
 def outer_call(me, tile, weights, own, kp, low, high, edge_one, edge_two, stacks):
     return pl.pallas_call(
         outer_rows,
-        out_shape=[half(OUTER)] * 3 + [half(PIECE + OUTER)] * 3 + [half(PIECE + INNER)] * 3,
+        out_shape=[half(OUTER)] * 3 + [half(PIECE + INNER)] * 3 + [half(PIECE + OUTER)] * 3,
         in_specs=[SM, SM, SM, ANY, VM] + [ANY] * 10,
         out_specs=[ANY] * 9,
         input_output_aliases={9 + n: 3 + n for n in range(6)},
@@ -605,7 +622,7 @@
             elif j == 0:
                 plan.append(((3 + e, 0, 0, INNER), (6 + e, 0, INNER, OUTER)))
             elif j == 2:
-                plan.append(((12 + e, PIECE, 0, INNER), (9 + e, PIECE, INNER, OUTER)))
+                plan.append(((9 + e, PIECE, 0, INNER), (12 + e, PIECE, INNER, OUTER)))
             else:
                 plan.append(((9 + e if j == 1 else 12 + e, 0, 0, PIECE),))
     pieces = [near[0], near[1], near[2], late[1]] + met + far
@@ -614,6 +631,4 @@
 
 def solution(mesh):
     placed = (P("case", "tile", None, None), P("case", "tile", None), P("case"), P())
-    return jax.shard_map(
-        merged_bases, mesh=mesh, in_specs=placed, out_specs=P("case", "tile", None), check_vma=False
-    )
+    return jax.shard_map(merged_bases, mesh=mesh, in_specs=placed, out_specs=P("case", "tile", None), check_vma=False)

time: 189 us -> 189 us (level)
  transfers between devices with their start and end apart: 20 -> 20, of which waited for: 9 -> 9; matrix products, arithmetic and copies ran while one was open for 0% -> 0% of each run, Pallas kernels for 19% -> 18%
where the time goes in v4:
time: 189 us
  waiting for transfers between devices  75.5 us (40%)
  Pallas kernels  44.4 us (23%)
  starting transfers between devices  37.1 us (20%)
  blocking collectives  24.8 us (13%)
  local copies, waits for them, and re-layouts  4.77 us (3%)
    ppermute x15, waiting for transfers between devices, case_swap(): lax.ppermute(value, 'case', [(source, source ^ apart) for source in range...  63.8 us
    all_to_all x1, blocking collectives, plane_exchange(): return lax.all_to_all(value, 'tile', 0, 0, axis_index_groups=PLANES)  24.8 us
    ppermute x15, starting transfers between devices, case_swap(): lax.ppermute(value, 'case', [(source, source ^ apart) for source in range...  18.2 us
    pallas_call x1, Pallas kernels, mixing_call(): pl.pallas_call(functools.partial(mixing, cells), out_shape=(shape, shape)...  16.4 us
    all_to_all x1, waiting for transfers between devices, plane_exchange(): return lax.all_to_all(value, 'tile', 0, 0, axis_index_groups=PLANES)  10.1 us
    pallas_call x1, Pallas kernels, inner_call(): pl.pallas_call(inner_rows, out_shape=[half(INNER)] * 3 + [half(PIECE + IN...  9.66 us
    pallas_call x1, Pallas kernels, outer_call(): pl.pallas_call(outer_rows, out_shape=[half(OUTER)] * 3 + [half(PIECE + IN...  8.26 us
    ppermute x2, starting transfers between devices, core_swap(): lax.ppermute(value, 'tile', [(source, source ^ 1) for source in range(64)])  6.86 us
  transfers between devices with their start and end apart: 20, of which 9 were waited for; matrix products, arithmetic and copies ran while one was open for 0% of the time, Pallas kernels for 18%

profile of v4, /device:TPU:1, one launch (start us, length us, event | category | flops | bytes accessed | tf_op | source)
XLA Modules:
  0.0 188.6 jit_solution(5724714985873141214)
XLA Ops:
  0.8 1.2 fusion
  2.2 5.1 %collective-permute-start.1 = (bf16[1568,128]{1,0:T(8,128)(2,1)S(1)}, bf16[1568,128]{1,0:T(8,128)(2,1)}, u32[]{:S(2)}, u32[]{:S(2)}) collective-permute-start(bf16[1568,128]{1,0:T(8,128)(2,1)S(1)} %concatenate.7), channel_id=1, source_target_pairs={{1,0},{2,1},{3,2},{4,3},{5,4},{6,5},{7,6},{8,7},{9,8},{10,9},{11,1... | collective-permute-start | bytes 1204232 | tf_op jit(solution)/shard_map/ppermute | solution.py:602
  7.7 1.9 %collective-permute-start = (bf16[1568,128]{1,0:T(8,128)(2,1)S(1)}, bf16[1568,128]{1,0:T(8,128)(2,1)}, u32[]{:S(2)}, u32[]{:S(2)}) collective-permute-start(bf16[1568,128]{1,0:T(8,128)(2,1)S(1)} %concatenate.6), channel_id=1, source_target_pairs={{0,1},{1,2},{2,3},{3,4},{4,5},{5,6},{6,7},{7,8},{8,9},{9,10},{10,1... | collective-permute-start | bytes 1204232 | tf_op jit(solution)/shard_map/ppermute | solution.py:601
  10.3 9.7 %shard_map.46 = (bf16[1280,128]{1,0:T(8,128)(2,1)}, bf16[1280,128]{1,0:T(8,128)(2,1)}, bf16[1280,128]{1,0:T(8,128)(2,1)}, bf16[3328,128]{1,0:T(8,128)(2,1)}, bf1...) custom-call(s32[1]{0:T(128)} %bitcast.me_ref, ...), custom_call_target="tpu_custom_call" | custom-call | flops 419430400 | bytes 9437184 | tf_op jit(solution)/shard_map/pallas_call | solution.py:433
  20.7 2.5 %collective-permute-start.3 = (bf16[1280,128]{1,0:T(8,128)(2,1)}, bf16[1280,128]{1,0:T(8,128)(2,1)}, u32[]{:S(2)}, u32[]{:S(2)}) collective-permute-start(bf16[1280,128]{1,0:T(8,128)(2,1)} %get-tuple-element.39), channel_id=1, source_target_pairs={{0,128},{64,192},{128,0},{192,64},{1,129},{65,193},{129,1},{193,65... | collective-permute-start | bytes 983048 | tf_op jit(solution)/shard_map/ppermute | solution.py:22
  23.9 8.3 %shard_map.47 = (bf16[768,128]{1,0:T(8,128)(2,1)}, bf16[768,128]{1,0:T(8,128)(2,1)}, bf16[768,128]{1,0:T(8,128)(2,1)}, bf16[3328,128]{1,0:T(8,128)(2,1)}, bf16[3...) custom-call(s32[1]{0:T(128)} %bitcast.me_ref, ...), custom_call_target="tpu_custom_call", output_to_operand_aliasing={{3}: (9, {}), {4}: (10, {}), {5}: (11, {}), {6}: (12, {}), ... | custom-call | flops 209715200 | bytes 9437184 | tf_op jit(solution)/shard_map/pallas_call | solution.py:448
  32.3 3.1 %collective-permute-start.6 = (bf16[768,128]{1,0:T(8,128)(2,1)}, bf16[768,128]{1,0:T(8,128)(2,1)S(1)}, u32[]{:S(2)}, u32[]{:S(2)}) collective-permute-start(bf16[768,128]{1,0:T(8,128)(2,1)} %get-tuple-element.42), channel_id=1, source_target_pairs={{0,128},{64,192},{128,0},{192,64},{1,129},{65,193},{129,1},{193,65... | collective-permute-start | bytes 589832 | tf_op jit(solution)/shard_map/ppermute | solution.py:22
  36.1 2.2 %collective-permute-done.3.refs_2_.refs_5_ = bf16[1280,128]{1,0:T(8,128)(2,1)} collective-permute-done((bf16[1280,128]{1,0:T(8,128)(2,1)}, bf16[1280,128]{1,0:T(8,128)(2,1)}, u32[]{:S(2)}, u32[]{:S(2)}) %collective-permute-start.3) | collective-permute-done | bytes 327712 | tf_op jit(solution)/shard_map/ppermute | solution.py:22
  38.3 2.1 %collective-permute-done.4.refs_3_.refs_6_ = bf16[1280,128]{1,0:T(8,128)(2,1)} collective-permute-done((bf16[1280,128]{1,0:T(8,128)(2,1)}, bf16[1280,128]{1,0:T(8,128)(2,1)}, u32[]{:S(2)}, u32[]{:S(2)}) %collective-permute-start.4) | collective-permute-done | bytes 327712 | tf_op jit(solution)/shard_map/ppermute | solution.py:22
  40.4 6.3 %collective-permute-done.6.refs_5_.refs_8_ = bf16[768,128]{1,0:T(8,128)(2,1)S(1)} collective-permute-done((bf16[768,128]{1,0:T(8,128)(2,1)}, bf16[768,128]{1,0:T(8,128)(2,1)S(1)}, u32[]{:S(2)}, u32[]{:S(2)}) %collective-permute-start.6) | collective-permute-done | bytes 196640 | tf_op jit(solution)/shard_map/ppermute | solution.py:22
  46.6 2.0 %collective-permute-done.7.refs_6_.refs_9_ = bf16[768,128]{1,0:T(8,128)(2,1)S(1)} collective-permute-done((bf16[768,128]{1,0:T(8,128)(2,1)}, bf16[768,128]{1,0:T(8,128)(2,1)S(1)}, u32[]{:S(2)}, u32[]{:S(2)}) %collective-permute-start.7) | collective-permute-done | bytes 196640 | tf_op jit(solution)/shard_map/ppermute | solution.py:22
  49.3 3.5 %shard_map.48 = (f32[32,24,128]{2,1,0:T(8,128)}, f32[32,24,128]{2,1,0:T(8,128)}) custom-call(s32[1]{0:T(128)} %bitcast.me_ref, s32[1]{0:T(128)S(6)} %and.5.core_ref, bf16[3328,128]{1,0:T(8,128)(2,1)} %get-tuple-element.37.refs_0_, bf16[1280,128]{1,0:T(8,128)(2,1)} %collective-permute-done.2.refs_1_.refs_4_, ...), custom_call_target="tpu_custom_call" | custom-call | flops 1073741824 | bytes 3145728 | tf_op jit(solution)/shard_map/pallas_call | solution.py:504
  52.9 1.6 collective-permute-start.8
  54.5 1.6 collective-permute-done.8
  56.0 1.0 add.12
  57.1 24.8 %all_to_all.10 = f32[32,24,128]{2,1,0:T(8,128)S(1)} all-to-all(f32[32,24,128]{2,1,0:T(8,128)S(1)} %add.12), channel_id=1, replica_groups={{0,2,4,6,8,10,12,14,16,18,20,22,24,26,28,30,32,34,36,38,40,42,44,46,48,..., dimensions={0} | all-to-all | bytes 786432 | tf_op jit(solution)/shard_map/all_to_all | solution.py:30
  82.0 1.1 collective-permute-start.11
  83.1 1.5 collective-permute-start.9
  84.6 1.4 collective-permute-done.10
  86.0 0.8 broadcast_in_dim.3
  86.8 5.0 %all-to-all-start.1 = ((f32[32,24,128]{2,1,0:T(8,128)}), f32[32,24,128]{2,1,0:T(8,128)S(1)}, u32[]{:S(2)}, u32[]{:S(2)}) async-start(f32[32,24,128]{2,1,0:T(8,128)} %broadcast_in_dim.3), calls=%async_computation.1 | async-start | bytes 786432 | tf_op jit(solution)/shard_map/all_to_all | solution.py:30
  91.8 1.3 collective-permute-start.16
  93.1 10.1 %all-to-all-done.1.own_hbm = f32[32,24,128]{2,1,0:T(8,128)S(1)} async-done(((f32[32,24,128]{2,1,0:T(8,128)}), f32[32,24,128]{2,1,0:T(8,128)S(1)}, u32[]{:S(2)}, u32[]{:S(2)}) %all-to-all-start.1) | async-done | bytes 393248 | tf_op jit(solution)/shard_map/all_to_all | solution.py:30
  103.3 5.3 %collective-permute-start.12 = (f32[32,24,128]{2,1,0:T(8,128)S(1)}, f32[32,24,128]{2,1,0:T(8,128)S(1)}, u32[]{:S(2)}, u32[]{:S(2)}) collective-permute-start(f32[32,24,128]{2,1,0:T(8,128)S(1)} %all-to-all-done.1.own_hbm), channel_id=1, source_target_pairs={{0,1},{1,0},{2,3},{3,2},{4,5},{5,4},{6,7},{7,6},{8,9},{9,8},{10,11... | collective-permute-start | bytes 1179656 | tf_op jit(solution)/shard_map/ppermute | solution.py:26
  108.6 1.2 collective-permute-start.13
  109.8 1.5 collective-permute-start.14
  111.3 1.1 collective-permute-start.15
  113.6 2.0 %collective-permute-start.18 = (bf16[2816,128]{1,0:T(8,128)(2,1)}, bf16[2816,128]{1,0:T(8,128)(2,1)}, u32[]{:S(2)}, u32[]{:S(2)}) collective-permute-start(bf16[2816,128]{1,0:T(8,128)(2,1)} %get-tuple-element.52), channel_id=1, source_target_pairs={{0,192},{64,128},{128,64},{192,0},{1,193},{65,129},{129,65},{193,1... | collective-permute-start | bytes 2162696 | tf_op jit(solution)/shard_map/ppermute | solution.py:22
  115.6 16.4 %shard_map.49 = (bf16[512,128]{1,0:T(8,128)(2,1)}, bf16[512,128]{1,0:T(8,128)(2,1)}) custom-call(s32[1]{0:T(128)} %bitcast.me_ref, s32[1]{0:T(128)S(6)} %and.5.core_ref, f32[32,24,128]{2,1,0:T(8,128)} %copy-done.3, f32[32,24,128]{2,1,0:T(8,128)} %copy-done.7, s32[2,256,128]{2,1,0:T(8,128)} %start_ref.1), custom_call_target="tpu_custom_call" | custom-call | flops 1073741824 | bytes 1048576 | tf_op jit(solution)/shard_map/pallas_call | solution.py:519
  132.0 32.1 %collective-permute-done.17.refs_14_ = bf16[2816,128]{1,0:T(8,128)(2,1)} collective-permute-done((bf16[2816,128]{1,0:T(8,128)(2,1)}, bf16[2816,128]{1,0:T(8,128)(2,1)}, u32[]{:S(2)}, u32[]{:S(2)}) %collective-permute-start.17) | collective-permute-done | bytes 720928 | tf_op jit(solution)/shard_map/ppermute | solution.py:22
  164.1 17.7 %collective-permute-done.18.refs_15_ = bf16[2816,128]{1,0:T(8,128)(2,1)} collective-permute-done((bf16[2816,128]{1,0:T(8,128)(2,1)}, bf16[2816,128]{1,0:T(8,128)(2,1)}, u32[]{:S(2)}, u32[]{:S(2)}) %collective-permute-start.18) | collective-permute-done | bytes 720928 | tf_op jit(solution)/shard_map/ppermute | solution.py:22
  181.8 6.6 %shard_map.50 = bf16[16,512,128]{2,1,0:T(8,128)(2,1)} custom-call(s32[1]{0:T(128)} %bitcast.me_ref, bf16[512,128]{1,0:T(8,128)(2,1)} %get-tuple-element.46.high_ref, bf16[512,128]{1,0:T(8,128)(2,1)} %get-tuple-element.47.low_ref, bf16[3328,128]{1,0:T(8,128)(2,1)} %get-tuple-element.37.refs_0_, bf16[3328,128]{1,0:T(8,128)(2,1)} %get-tuple-element.48.refs_1_, ...), custom_call_target="tpu_custom_call" | custom-call | flops 2147483648 | bytes 10485760 | tf_op jit(solution)/shard_map/pallas_call | solution.py:570
  (43 shorter events, 5.7 us)
Async XLA Ops:
  2.2 21.6 %collective-permute-start.1 = (bf16[1568,128]{1,0:T(8,128)(2,1)S(1)}, bf16[1568,128]{1,0:T(8,128)(2,1)}, u32[]{:S(2)}, u32[]{:S(2)}) collective-permute-start(bf16[1568,128]{1,0:T(8,128)(2,1)S(1)} %concatenate.7), channel_id=1, source_target_pairs={{1,0},{2,1},{3,2},{4,3},{5,4},{6,5},{7,6},{8,7},{9,8},{10,9},{11,1... | collective-permute-start | bytes 1204232 | tf_op jit(solution)/shard_map/ppermute | solution.py:602
  7.7 16.2 %collective-permute-start = (bf16[1568,128]{1,0:T(8,128)(2,1)S(1)}, bf16[1568,128]{1,0:T(8,128)(2,1)}, u32[]{:S(2)}, u32[]{:S(2)}) collective-permute-start(bf16[1568,128]{1,0:T(8,128)(2,1)S(1)} %concatenate.6), channel_id=1, source_target_pairs={{0,1},{1,2},{2,3},{3,4},{4,5},{5,6},{6,7},{7,8},{8,9},{9,10},{10,1... | collective-permute-start | bytes 1204232 | tf_op jit(solution)/shard_map/ppermute | solution.py:601
  19.9 15.4 %collective-permute-start.2 = (bf16[1280,128]{1,0:T(8,128)(2,1)}, bf16[1280,128]{1,0:T(8,128)(2,1)}, u32[]{:S(2)}, u32[]{:S(2)}) collective-permute-start(bf16[1280,128]{1,0:T(8,128)(2,1)} %get-tuple-element.38), channel_id=1, source_target_pairs={{0,64},{64,0},{128,192},{192,128},{1,65},{65,1},{129,193},{193,129... | collective-permute-start | bytes 983048 | tf_op jit(solution)/shard_map/ppermute | solution.py:22
  20.7 17.6 %collective-permute-start.3 = (bf16[1280,128]{1,0:T(8,128)(2,1)}, bf16[1280,128]{1,0:T(8,128)(2,1)}, u32[]{:S(2)}, u32[]{:S(2)}) collective-permute-start(bf16[1280,128]{1,0:T(8,128)(2,1)} %get-tuple-element.39), channel_id=1, source_target_pairs={{0,128},{64,192},{128,0},{192,64},{1,129},{65,193},{129,1},{193,65... | collective-permute-start | bytes 983048 | tf_op jit(solution)/shard_map/ppermute | solution.py:22
  23.2 17.2 %collective-permute-start.4 = (bf16[1280,128]{1,0:T(8,128)(2,1)}, bf16[1280,128]{1,0:T(8,128)(2,1)}, u32[]{:S(2)}, u32[]{:S(2)}) collective-permute-start(bf16[1280,128]{1,0:T(8,128)(2,1)} %get-tuple-element.40), channel_id=1, source_target_pairs={{0,192},{64,128},{128,64},{192,0},{1,193},{65,129},{129,65},{193,1... | collective-permute-start | bytes 983048 | tf_op jit(solution)/shard_map/ppermute | solution.py:22
  32.2 8.2 %collective-permute-start.5 = (bf16[768,128]{1,0:T(8,128)(2,1)}, bf16[768,128]{1,0:T(8,128)(2,1)S(1)}, u32[]{:S(2)}, u32[]{:S(2)}) collective-permute-start(bf16[768,128]{1,0:T(8,128)(2,1)} %get-tuple-element.41), channel_id=1, source_target_pairs={{0,64},{64,0},{128,192},{192,128},{1,65},{65,1},{129,193},{193,129... | collective-permute-start | bytes 589832 | tf_op jit(solution)/shard_map/ppermute | solution.py:22
  32.3 14.4 %collective-permute-start.6 = (bf16[768,128]{1,0:T(8,128)(2,1)}, bf16[768,128]{1,0:T(8,128)(2,1)S(1)}, u32[]{:S(2)}, u32[]{:S(2)}) collective-permute-start(bf16[768,128]{1,0:T(8,128)(2,1)} %get-tuple-element.42), channel_id=1, source_target_pairs={{0,128},{64,192},{128,0},{192,64},{1,129},{65,193},{129,1},{193,65... | collective-permute-start | bytes 589832 | tf_op jit(solution)/shard_map/ppermute | solution.py:22
  35.4 13.3 %collective-permute-start.7 = (bf16[768,128]{1,0:T(8,128)(2,1)}, bf16[768,128]{1,0:T(8,128)(2,1)S(1)}, u32[]{:S(2)}, u32[]{:S(2)}) collective-permute-start(bf16[768,128]{1,0:T(8,128)(2,1)} %get-tuple-element.43), channel_id=1, source_target_pairs={{0,192},{64,128},{128,64},{192,0},{1,193},{65,129},{129,65},{193,1... | collective-permute-start | bytes 589832 | tf_op jit(solution)/shard_map/ppermute | solution.py:22
  40.4 8.3 %copy-start.4 = (bf16[768,128]{1,0:T(8,128)(2,1)}, bf16[768,128]{1,0:T(8,128)(2,1)S(1)}, u32[]{:S(2)}) copy-start(bf16[768,128]{1,0:T(8,128)(2,1)S(1)} %collective-permute-done.5.refs_4_.refs_7_) | copy-start | bytes 589828
  46.6 2.0 %copy-start.5 = (bf16[768,128]{1,0:T(8,128)(2,1)}, bf16[768,128]{1,0:T(8,128)(2,1)S(1)}, u32[]{:S(2)}) copy-start(bf16[768,128]{1,0:T(8,128)(2,1)S(1)} %collective-permute-done.6.refs_5_.refs_8_) | copy-start | bytes 589828
  48.7 0.7 copy-start.6
  52.9 38.9 %copy-start.2 = (bf16[2816,128]{1,0:T(8,128)(2,1)S(1)}, bf16[2816,128]{1,0:T(8,128)(2,1)}, u32[]{:S(2)}) copy-start(bf16[2816,128]{1,0:T(8,128)(2,1)} %get-tuple-element.51) | copy-start | bytes 2162692
  52.9 55.7 %copy-start = (bf16[3328,128]{1,0:T(8,128)(2,1)S(1)}, bf16[3328,128]{1,0:T(8,128)(2,1)}, u32[]{:S(2)}) copy-start(bf16[3328,128]{1,0:T(8,128)(2,1)} %get-tuple-element.37.refs_0_) | copy-start | bytes 2555908
  52.9 56.9 %copy-start.1 = (bf16[3328,128]{1,0:T(8,128)(2,1)S(1)}, bf16[3328,128]{1,0:T(8,128)(2,1)}, u32[]{:S(2)}) copy-start(bf16[3328,128]{1,0:T(8,128)(2,1)} %get-tuple-element.48.refs_1_) | copy-start | bytes 2555908
  52.9 3.1 %collective-permute-start.8 = (f32[32,24,128]{2,1,0:T(8,128)}, f32[32,24,128]{2,1,0:T(8,128)S(1)}, u32[]{:S(2)}, u32[]{:S(2)}) collective-permute-start(f32[32,24,128]{2,1,0:T(8,128)} %get-tuple-element.45), channel_id=1, source_target_pairs={{0,1},{1,0},{2,3},{3,2},{4,5},{5,4},{6,7},{7,6},{8,9},{9,8},{10,11... | collective-permute-start | bytes 1179656 | tf_op jit(solution)/shard_map/ppermute | solution.py:26
  81.9 4.1 %collective-permute-start.10 = (f32[24,128]{1,0:T(8,128)S(1)}, f32[24,128]{1,0:T(8,128)S(1)}, u32[]{:S(2)}, u32[]{:S(2)}) collective-permute-start(f32[24,128]{1,0:T(8,128)S(1)} %reduce_sum.9), channel_id=1, source_target_pairs={{0,128},{64,192},{128,0},{192,64},{1,129},{65,193},{129,1},{193,65... | collective-permute-start | bytes 36872 | tf_op jit(solution)/shard_map/ppermute | solution.py:22
  82.0 4.0 %collective-permute-start.11 = (f32[24,128]{1,0:T(8,128)S(1)}, f32[24,128]{1,0:T(8,128)S(1)}, u32[]{:S(2)}, u32[]{:S(2)}) collective-permute-start(f32[24,128]{1,0:T(8,128)S(1)} %reduce_sum.9), channel_id=1, source_target_pairs={{0,192},{64,128},{128,64},{192,0},{1,193},{65,129},{129,65},{193,1... | collective-permute-start | bytes 36872 | tf_op jit(solution)/shard_map/ppermute | solution.py:22
  83.1 2.9 %collective-permute-start.9 = (f32[24,128]{1,0:T(8,128)S(1)}, f32[24,128]{1,0:T(8,128)S(1)}, u32[]{:S(2)}, u32[]{:S(2)}) collective-permute-start(f32[24,128]{1,0:T(8,128)S(1)} %reduce_sum.9), channel_id=1, source_target_pairs={{0,64},{64,0},{128,192},{192,128},{1,65},{65,1},{129,193},{193,129... | collective-permute-start | bytes 36872 | tf_op jit(solution)/shard_map/ppermute | solution.py:22
  86.8 16.4 %all-to-all-start.1 = ((f32[32,24,128]{2,1,0:T(8,128)}), f32[32,24,128]{2,1,0:T(8,128)S(1)}, u32[]{:S(2)}, u32[]{:S(2)}) async-start(f32[32,24,128]{2,1,0:T(8,128)} %broadcast_in_dim.3), calls=%async_computation.1 | async-start | bytes 786432 | tf_op jit(solution)/shard_map/all_to_all | solution.py:30
  91.8 20.6 %collective-permute-start.16 = (bf16[2816,128]{1,0:T(8,128)(2,1)S(1)}, bf16[2816,128]{1,0:T(8,128)(2,1)}, u32[]{:S(2)}, u32[]{:S(2)}) collective-permute-start(bf16[2816,128]{1,0:T(8,128)(2,1)S(1)} %copy-done.2), channel_id=1, source_target_pairs={{0,64},{64,0},{128,192},{192,128},{1,65},{65,1},{129,193},{193,129... | collective-permute-start | bytes 2162696 | tf_op jit(solution)/shard_map/ppermute | solution.py:22
  103.3 9.2 %copy-start.3 = (f32[32,24,128]{2,1,0:T(8,128)}, f32[32,24,128]{2,1,0:T(8,128)S(1)}, u32[]{:S(2)}) copy-start(f32[32,24,128]{2,1,0:T(8,128)S(1)} %all-to-all-done.1.own_hbm) | copy-start | bytes 1179652
  103.3 9.6 %collective-permute-start.12 = (f32[32,24,128]{2,1,0:T(8,128)S(1)}, f32[32,24,128]{2,1,0:T(8,128)S(1)}, u32[]{:S(2)}, u32[]{:S(2)}) collective-permute-start(f32[32,24,128]{2,1,0:T(8,128)S(1)} %all-to-all-done.1.own_hbm), channel_id=1, source_target_pairs={{0,1},{1,0},{2,3},{3,2},{4,5},{5,4},{6,7},{7,6},{8,9},{9,8},{10,11... | collective-permute-start | bytes 1179656 | tf_op jit(solution)/shard_map/ppermute | solution.py:26
  108.6 73.3 %collective-permute-start.13 = (bf16[3328,128]{1,0:T(8,128)(2,1)S(1)}, bf16[3328,128]{1,0:T(8,128)(2,1)}, u32[]{:S(2)}, u32[]{:S(2)}) collective-permute-start(bf16[3328,128]{1,0:T(8,128)(2,1)S(1)} %copy-done), channel_id=1, source_target_pairs={{0,64},{64,0},{128,192},{192,128},{1,65},{65,1},{129,193},{193,129... | collective-permute-start | bytes 2555912 | tf_op jit(solution)/shard_map/ppermute | solution.py:22
  109.8 72.1 %collective-permute-start.14 = (bf16[3328,128]{1,0:T(8,128)(2,1)S(1)}, bf16[3328,128]{1,0:T(8,128)(2,1)}, u32[]{:S(2)}, u32[]{:S(2)}) collective-permute-start(bf16[3328,128]{1,0:T(8,128)(2,1)S(1)} %copy-done.1), channel_id=1, source_target_pairs={{0,128},{64,192},{128,0},{192,64},{1,129},{65,193},{129,1},{193,65... | collective-permute-start | bytes 2555912 | tf_op jit(solution)/shard_map/ppermute | solution.py:22
  111.3 70.5 %collective-permute-start.15 = (bf16[3328,128]{1,0:T(8,128)(2,1)}, bf16[3328,128]{1,0:T(8,128)(2,1)}, u32[]{:S(2)}, u32[]{:S(2)}) collective-permute-start(bf16[3328,128]{1,0:T(8,128)(2,1)} %get-tuple-element.49.refs_2_), channel_id=1, source_target_pairs={{0,192},{64,128},{128,64},{192,0},{1,193},{65,129},{129,65},{193,1... | collective-permute-start | bytes 2555912 | tf_op jit(solution)/shard_map/ppermute | solution.py:22
  112.4 51.7 %collective-permute-start.17 = (bf16[2816,128]{1,0:T(8,128)(2,1)}, bf16[2816,128]{1,0:T(8,128)(2,1)}, u32[]{:S(2)}, u32[]{:S(2)}) collective-permute-start(bf16[2816,128]{1,0:T(8,128)(2,1)} %get-tuple-element.50.refs_3_), channel_id=1, source_target_pairs={{0,128},{64,192},{128,0},{192,64},{1,129},{65,193},{129,1},{193,65... | collective-permute-start | bytes 2162696 | tf_op jit(solution)/shard_map/ppermute | solution.py:22
  112.9 0.8 copy-start.7
  113.6 68.2 %collective-permute-start.18 = (bf16[2816,128]{1,0:T(8,128)(2,1)}, bf16[2816,128]{1,0:T(8,128)(2,1)}, u32[]{:S(2)}, u32[]{:S(2)}) collective-permute-start(bf16[2816,128]{1,0:T(8,128)(2,1)} %get-tuple-element.52), channel_id=1, source_target_pairs={{0,192},{64,128},{128,64},{192,0},{1,193},{65,129},{129,65},{193,1... | collective-permute-start | bytes 2162696 | tf_op jit(solution)/shard_map/ppermute | solution.py:22

commit v5 on v4

--- a/solution.py
+++ b/solution.py
@@ -290,21 +290,24 @@
     return write
 
 
-def send_out(me, snap, singles, moves, sems):
+def send_out(me, snap, singles, stacks, begin, size, sems):
+    one, two, three = stacks
+    moves = [(singles[e - 1], e, 0) for e in (1, 2, 3)]
+    moves += [(one, j ^ 1, PIECE * (j - 1) + begin) for j in (1, 2, 3)]
+    moves += [(two, 2, begin), (two, 1, PIECE + begin), (three, 0, begin)]
     copies = []
-    for e in (1, 2, 3):
-        copies.append(pltpu.make_async_copy(snap.at[me ^ e], singles[e - 1], sems.at[len(copies)]))
-        for stacks, j, begin, size in moves:
-            target = stacks[e - 1].at[pl.ds(begin, size)]
-            copies.append(pltpu.make_async_copy(snap.at[me ^ e ^ j], target, sems.at[len(copies)]))
+    for target, j, at0 in moves:
+        copies.append(
+            pltpu.make_async_copy(snap.at[me ^ j], target.at[pl.ds(at0, size)], sems.at[len(copies)])
+        )
     for copy in copies:
         copy.start()
     return copies
 
 
 def inner_rows(me_ref, scale_ref, own_ref, kp_ref, *refs):
-    singles, near, late, edge_one, edge_two = refs[:3], refs[3:6], refs[6:9], refs[9], refs[10]
-    first, second, east, north, perm_ref, snap, held, sems, edge_sems = refs[11:]
+    singles, stacks, edge_one, edge_two = refs[:3], refs[3:6], refs[6], refs[7]
+    first, second, east, north, perm_ref, snap, held, sems, edge_sems = refs[8:]
     me = me_ref[0]
     load = pltpu.make_async_copy(own_ref, held, sems.at[0])
     load.start()
@@ -330,15 +333,14 @@
     for copy in edges_out:
         copy.start()
     sweep(first, east, north, 3, 3, 10, into_snap(snap, 0, scale_ref))
-    moves = ((near, 1, 0, INNER), (near, 2, PIECE, INNER), (late, 3, 0, INNER))
-    for copy in edges_out + send_out(me, snap, singles, moves, sems):
+    for copy in edges_out + send_out(me, snap, singles, stacks, 0, INNER, sems):
         copy.wait()
 
 
 def outer_rows(me_ref, tile_ref, scale_ref, own_hbm, kp_ref, low_hbm, high_hbm, edge_one, edge_two, *refs):
-    singles, near, late = refs[6:9], refs[9:12], refs[12:15]
-    low0, low1, low2, high0, high1, high2, east, north, perm_ref, snap = refs[15:25]
-    low_ref, high_ref, own_ref, sems, edge_sems = refs[25:]
+    singles, stacks = refs[3:6], refs[6:9]
+    low0, low1, low2, high0, high1, high2, east, north, perm_ref, snap = refs[9:19]
+    low_ref, high_ref, own_ref, sems, edge_sems = refs[19:]
     me, tile = me_ref[0], tile_ref[0]
     loads = [
         pltpu.make_async_copy(low_hbm, low_ref, sems.at[0]),
@@ -410,8 +412,7 @@
 
     sweep(low2, east, north, 1, 3, 3, into_snap(snap, 0, scale_ref))
     sweep(high2, east, north, 1, 8, 3, into_snap(snap, 3, scale_ref))
-    moves = ((near, 1, INNER, OUTER), (late, 3, INNER, OUTER), (late, 2, PIECE, OUTER))
-    for copy in send_out(me, snap, singles, moves, sems):
+    for copy in send_out(me, snap, singles, stacks, INNER, OUTER, sems):
         copy.wait()
 
 
@@ -432,9 +433,9 @@
     edge = jax.ShapeDtypeStruct((4, WIDE, LANES), jnp.float32)
     return pl.pallas_call(
         inner_rows,
-        out_shape=[half(INNER)] * 3 + [half(PIECE + INNER)] * 3 + [half(PIECE + OUTER)] * 3 + [edge] * 2,
+        out_shape=[half(INNER)] * 3 + [half(3 * PIECE), half(2 * PIECE), half(PIECE)] + [edge] * 2,
         in_specs=[SM, SM, ANY, VM],
-        out_specs=[ANY] * 11,
+        out_specs=[ANY] * 8,
         scratch_shapes=[planes(16), planes(16), planes(15), planes(15)]
         + [pltpu.VMEM((WIDE, LANES), jnp.float32), pltpu.VMEM((4, INNER, LANES), jnp.bfloat16)]
         + [pltpu.VMEM((16, NY, LANES), jnp.bfloat16)]
@@ -447,10 +448,10 @@
 def outer_call(me, tile, weights, own, kp, low, high, edge_one, edge_two, stacks):
     return pl.pallas_call(
         outer_rows,
-        out_shape=[half(OUTER)] * 3 + [half(PIECE + INNER)] * 3 + [half(PIECE + OUTER)] * 3,
-        in_specs=[SM, SM, SM, ANY, VM] + [ANY] * 10,
-        out_specs=[ANY] * 9,
-        input_output_aliases={9 + n: 3 + n for n in range(6)},
+        out_shape=[half(OUTER)] * 3 + [half(3 * PIECE), half(2 * PIECE), half(PIECE)],
+        in_specs=[SM, SM, SM, ANY, VM] + [ANY] * 7,
+        out_specs=[ANY] * 6,
+        input_output_aliases={9 + n: 3 + n for n in range(3)},
         scratch_shapes=[planes(5)] * 6
         + [planes(13), planes(13), pltpu.VMEM((WIDE, LANES), jnp.float32)]
         + [pltpu.VMEM((4, OUTER, LANES), jnp.bfloat16)]
@@ -602,30 +603,35 @@
     high = lax.ppermute(packed_edge(own[:STEPS], kp[:STEPS]), "tile", down)
     inner = inner_call(me, merge_weights, own, kp)
     met = [case_swap(inner[e - 1], e) for e in (1, 2, 3)]
-    outer = outer_call(me, tile, merge_weights, own, kp, low, high, inner[9], inner[10], inner[3:9])
-    near, late = outer[3:6], outer[6:9]
+    outer = outer_call(me, tile, merge_weights, own, kp, low, high, inner[6], inner[7], inner[3:6])
+    one, two, three = outer[3:]
     met = met + [case_swap(outer[e - 1], e) for e in (1, 2, 3)]
-    far = [case_swap(near[e - 1], e) for e in (1, 2, 3)]
-    far = far + [case_swap(late[e - 1], e) for e in (1, 2, 3)]
-    own_part, other_part = grams_call(me, core, [near[0]] + met)
+    far_one, far_two, far_three = case_swap(one, 1), case_swap(two, 3), case_swap(three, 3)
+    via_one = [case_swap(met[2], 1), case_swap(met[5], 1), case_swap(far_three, 1)]
+    via_three = [case_swap(met[0], 3), case_swap(met[3], 3)]
+    own_part, other_part = grams_call(me, core, [one] + met)
     part = own_part + core_swap(other_part)
     part = plane_exchange(part).sum(0)
     part = part + case_swap(part, 1) + case_swap(part, 2) + case_swap(part, 3)
     mine = plane_exchange(jnp.broadcast_to(part, (32,) + part.shape))
     yours = core_swap(mine)
     high, low = mixing_call(cells, me, core, mine, yours, start_codes)
+    pieces = [one, two, three] + met + [far_one, far_two, far_three] + via_one + via_three
+    whole = ((0, PIECE),)
+    split = ((0, INNER), (INNER, OUTER))
+    places = {
+        (0, 0): [(0, 0)], (0, 1): [(1, PIECE)], (0, 2): [(0, 2 * PIECE)], (0, 3): [(0, PIECE)],
+        (1, 0): [(3, 0), (6, 0)], (2, 0): [(4, 0), (7, 0)], (3, 0): [(5, 0), (8, 0)],
+        (1, 1): [(9, 0)], (1, 2): [(9, PIECE)], (1, 3): [(9, 2 * PIECE)],
+        (3, 1): [(10, 0)], (3, 2): [(10, PIECE)], (3, 3): [(11, 0)],
+        (2, 1): [(12, 0), (13, 0)], (2, 2): [(14, 0)], (2, 3): [(15, 0), (16, 0)],
+    }
     plan = []
     for j in range(4):
         for e in range(4):
-            if e == 0:
-                plan.append((({0: 0, 3: 1, 2: 2, 1: 3}[j], 0, 0, PIECE),))
-            elif j == 0:
-                plan.append(((3 + e, 0, 0, INNER), (6 + e, 0, INNER, OUTER)))
-            elif j == 2:
-                plan.append(((9 + e, PIECE, 0, INNER), (12 + e, PIECE, INNER, OUTER)))
-            else:
-                plan.append(((9 + e if j == 1 else 12 + e, 0, 0, PIECE),))
-    pieces = [near[0], near[1], near[2], late[1]] + met + far
+            sources = places[e, j]
+            spans = whole if len(sources) == 1 else split
+            plan.append(tuple((i, b, t, n) for (i, b), (t, n) in zip(sources, spans)))
     return finish_call(me, high, low, pieces, tuple(plan)).reshape(1, -1, LANES)
 
 

time: 189 us -> 173 us (0.915)
  the two profiles are of different devices: /device:TPU:1 before, /device:TPU:2 now
where the time goes in v5:
time: 173 us
  waiting for transfers between devices  63.4 us (37%)
  Pallas kernels  44 us (25%)
  starting transfers between devices  32.1 us (19%)
  blocking collectives  27 us (16%)
  local copies, waits for them, and re-layouts  4.06 us (2%)
    ppermute x17, waiting for transfers between devices, case_swap(): lax.ppermute(value, 'case', [(source, source ^ apart) for source in range...  50.8 us
    all_to_all x1, blocking collectives, plane_exchange(): return lax.all_to_all(value, 'tile', 0, 0, axis_index_groups=PLANES)  27 us
    ppermute x17, starting transfers between devices, case_swap(): lax.ppermute(value, 'case', [(source, source ^ apart) for source in range...  23.7 us
    pallas_call x1, Pallas kernels, mixing_call(): pl.pallas_call(functools.partial(mixing, cells), out_shape=(shape, shape)...  16.4 us
    all_to_all x1, waiting for transfers between devices, plane_exchange(): return lax.all_to_all(value, 'tile', 0, 0, axis_index_groups=PLANES)  10.8 us
    pallas_call x1, Pallas kernels, inner_call(): pl.pallas_call(inner_rows, out_shape=[half(INNER)] * 3 + [half(3 * PIECE)...  9.37 us
    pallas_call x1, Pallas kernels, outer_call(): pl.pallas_call(outer_rows, out_shape=[half(OUTER)] * 3 + [half(3 * PIECE)...  8.12 us
    pallas_call x1, Pallas kernels, finish_call(): pl.pallas_call(functools.partial(finish, plan), out_shape=jax.ShapeDtypeS...  6.56 us
  transfers between devices with their start and end apart: 22, of which 10 were waited for; matrix products, arithmetic and copies ran while one was open for 1% of the time, Pallas kernels for 20%

profile of v5, /device:TPU:2, one launch (start us, length us, event | category | flops | bytes accessed | tf_op | source)
XLA Modules:
  0.0 172.7 jit_solution(13949292043114999372)
XLA Ops:
  0.8 1.2 fusion
  2.2 2.5 %collective-permute-start = (bf16[1568,128]{1,0:T(8,128)(2,1)S(1)}, bf16[1568,128]{1,0:T(8,128)(2,1)}, u32[]{:S(2)}, u32[]{:S(2)}) collective-permute-start(bf16[1568,128]{1,0:T(8,128)(2,1)S(1)} %concatenate.6), channel_id=1, source_target_pairs={{0,1},{1,2},{2,3},{3,4},{4,5},{5,6},{6,7},{7,8},{8,9},{9,10},{10,1... | collective-permute-start | bytes 1204232 | tf_op jit(solution)/shard_map/ppermute | solution.py:602
  5.1 1.3 collective-permute-start.1
  7.0 9.4 %shard_map.46 = (bf16[1280,128]{1,0:T(8,128)(2,1)}, bf16[1280,128]{1,0:T(8,128)(2,1)}, bf16[1280,128]{1,0:T(8,128)(2,1)}, bf16[6144,128]{1,0:T(8,128)(2,1)}, bf1...) custom-call(s32[1]{0:T(128)} %bitcast.me_ref, ...), custom_call_target="tpu_custom_call" | custom-call | flops 419430400 | bytes 9437184 | tf_op jit(solution)/shard_map/pallas_call | solution.py:434
  16.4 1.9 %collective-permute-start.2 = (bf16[1280,128]{1,0:T(8,128)(2,1)}, bf16[1280,128]{1,0:T(8,128)(2,1)}, u32[]{:S(2)}, u32[]{:S(2)}) collective-permute-start(bf16[1280,128]{1,0:T(8,128)(2,1)} %get-tuple-element.29), channel_id=1, source_target_pairs={{0,64},{64,0},{128,192},{192,128},{1,65},{65,1},{129,193},{193,129... | collective-permute-start | bytes 983048 | tf_op jit(solution)/shard_map/ppermute | solution.py:22
  18.3 1.2 collective-permute-start.3
  20.0 8.1 %shard_map.47 = (bf16[768,128]{1,0:T(8,128)(2,1)}, bf16[768,128]{1,0:T(8,128)(2,1)}, bf16[768,128]{1,0:T(8,128)(2,1)}, bf16[6144,128]{1,0:T(8,128)(2,1)}, bf16[4...) custom-call(s32[1]{0:T(128)} %bitcast.me_ref, ...), custom_call_target="tpu_custom_call", output_to_operand_aliasing={{3}: (9, {}), {4}: (10, {}), {5}: (11, {})} | custom-call | flops 209715200 | bytes 9437184 | tf_op jit(solution)/shard_map/pallas_call | solution.py:449
  28.1 3.1 %collective-permute-start.5 = (bf16[768,128]{1,0:T(8,128)(2,1)}, bf16[768,128]{1,0:T(8,128)(2,1)}, u32[]{:S(2)}, u32[]{:S(2)}) collective-permute-start(bf16[768,128]{1,0:T(8,128)(2,1)} %get-tuple-element.32), channel_id=1, source_target_pairs={{0,64},{64,0},{128,192},{192,128},{1,65},{65,1},{129,193},{193,129... | collective-permute-start | bytes 589832 | tf_op jit(solution)/shard_map/ppermute | solution.py:22
  31.6 1.1 collective-permute-start.7
  32.8 1.9 %collective-permute-done.3.refs_2_.refs_4_ = bf16[1280,128]{1,0:T(8,128)(2,1)} collective-permute-done((bf16[1280,128]{1,0:T(8,128)(2,1)}, bf16[1280,128]{1,0:T(8,128)(2,1)}, u32[]{:S(2)}, u32[]{:S(2)}) %collective-permute-start.3) | collective-permute-done | bytes 327712 | tf_op jit(solution)/shard_map/ppermute | solution.py:22
  34.7 2.5 %collective-permute-done.4.refs_3_.refs_5_ = bf16[1280,128]{1,0:T(8,128)(2,1)} collective-permute-done((bf16[1280,128]{1,0:T(8,128)(2,1)}, bf16[1280,128]{1,0:T(8,128)(2,1)}, u32[]{:S(2)}, u32[]{:S(2)}) %collective-permute-start.4) | collective-permute-done | bytes 327712 | tf_op jit(solution)/shard_map/ppermute | solution.py:22
  37.1 0.7 collective-permute-done.5.refs_4_.refs_6_
  37.9 5.1 %collective-permute-done.6.refs_5_.refs_7_ = bf16[768,128]{1,0:T(8,128)(2,1)S(1)} collective-permute-done((bf16[768,128]{1,0:T(8,128)(2,1)}, bf16[768,128]{1,0:T(8,128)(2,1)S(1)}, u32[]{:S(2)}, u32[]{:S(2)}) %collective-permute-start.6) | collective-permute-done | bytes 196640 | tf_op jit(solution)/shard_map/ppermute | solution.py:22
  43.0 2.5 %collective-permute-done.7.refs_6_.refs_8_ = bf16[768,128]{1,0:T(8,128)(2,1)} collective-permute-done((bf16[768,128]{1,0:T(8,128)(2,1)}, bf16[768,128]{1,0:T(8,128)(2,1)}, u32[]{:S(2)}, u32[]{:S(2)}) %collective-permute-start.7) | collective-permute-done | bytes 196640 | tf_op jit(solution)/shard_map/ppermute | solution.py:22
  45.6 3.5 %shard_map.48 = (f32[32,24,128]{2,1,0:T(8,128)}, f32[32,24,128]{2,1,0:T(8,128)}) custom-call(s32[1]{0:T(128)} %bitcast.me_ref, s32[1]{0:T(128)S(6)} %and.5.core_ref, bf16[6144,128]{1,0:T(8,128)(2,1)} %get-tuple-element.28.refs_0_, bf16[1280,128]{1,0:T(8,128)(2,1)} %collective-permute-done.2.refs_1_.refs_3_, ...), custom_call_target="tpu_custom_call" | custom-call | flops 1073741824 | bytes 3145728 | tf_op jit(solution)/shard_map/pallas_call | solution.py:505
  49.3 1.8 %collective-permute-done.8 = f32[32,24,128]{2,1,0:T(8,128)S(1)} collective-permute-done((f32[32,24,128]{2,1,0:T(8,128)}, f32[32,24,128]{2,1,0:T(8,128)S(1)}, u32[]{:S(2)}, u32[]{:S(2)}) %collective-permute-start.8) | collective-permute-done | bytes 393248 | tf_op jit(solution)/shard_map/ppermute | solution.py:26
  51.1 1.1 add.12
  52.2 27.0 %all_to_all.10 = f32[32,24,128]{2,1,0:T(8,128)S(1)} all-to-all(f32[32,24,128]{2,1,0:T(8,128)S(1)} %add.12), channel_id=1, replica_groups={{0,2,4,6,8,10,12,14,16,18,20,22,24,26,28,30,32,34,36,38,40,42,44,46,48,..., dimensions={0} | all-to-all | bytes 786432 | tf_op jit(solution)/shard_map/all_to_all | solution.py:30
  79.9 4.5 %collective-permute-start.10 = (f32[24,128]{1,0:T(8,128)S(1)}, f32[24,128]{1,0:T(8,128)S(1)}, u32[]{:S(2)}, u32[]{:S(2)}) collective-permute-start(f32[24,128]{1,0:T(8,128)S(1)} %reduce_sum.9), channel_id=1, source_target_pairs={{0,128},{64,192},{128,0},{192,64},{1,129},{65,193},{129,1},{193,65... | collective-permute-start | bytes 36872 | tf_op jit(solution)/shard_map/ppermute | solution.py:22
  84.5 2.0 %collective-permute-start.13 = (bf16[6144,128]{1,0:T(8,128)(2,1)S(1)}, bf16[6144,128]{1,0:T(8,128)(2,1)}, u32[]{:S(2)}, u32[]{:S(2)}) collective-permute-start(bf16[6144,128]{1,0:T(8,128)(2,1)S(1)} %copy-done), channel_id=1, source_target_pairs={{0,64},{64,0},{128,192},{192,128},{1,65},{65,1},{129,193},{193,129... | collective-permute-start | bytes 4718600 | tf_op jit(solution)/shard_map/ppermute | solution.py:22
  86.5 1.8 %collective-permute-done.9 = f32[24,128]{1,0:T(8,128)S(1)} collective-permute-done((f32[24,128]{1,0:T(8,128)S(1)}, f32[24,128]{1,0:T(8,128)S(1)}, u32[]{:S(2)}, u32[]{:S(2)}) %collective-permute-start.9) | collective-permute-done | bytes 12320 | tf_op jit(solution)/shard_map/ppermute | solution.py:22
  88.3 0.8 broadcast_in_dim.3
  89.1 4.3 %all-to-all-start.1 = ((f32[32,24,128]{2,1,0:T(8,128)}), f32[32,24,128]{2,1,0:T(8,128)S(1)}, u32[]{:S(2)}, u32[]{:S(2)}) async-start(f32[32,24,128]{2,1,0:T(8,128)} %broadcast_in_dim.3), calls=%async_computation.1 | async-start | bytes 786432 | tf_op jit(solution)/shard_map/all_to_all | solution.py:30
  93.5 2.0 %collective-permute-start.14 = (bf16[4096,128]{1,0:T(8,128)(2,1)}, bf16[4096,128]{1,0:T(8,128)(2,1)}, u32[]{:S(2)}, u32[]{:S(2)}) collective-permute-start(bf16[4096,128]{1,0:T(8,128)(2,1)} %get-tuple-element.39.refs_1_), channel_id=1, source_target_pairs={{0,192},{64,128},{128,64},{192,0},{1,193},{65,129},{129,65},{193,1... | collective-permute-start | bytes 3145736 | tf_op jit(solution)/shard_map/ppermute | solution.py:22
  95.6 10.8 %all-to-all-done.1.own_hbm = f32[32,24,128]{2,1,0:T(8,128)S(1)} async-done(((f32[32,24,128]{2,1,0:T(8,128)}), f32[32,24,128]{2,1,0:T(8,128)S(1)}, u32[]{:S(2)}, u32[]{:S(2)}) %all-to-all-start.1) | async-done | bytes 393248 | tf_op jit(solution)/shard_map/all_to_all | solution.py:30
  106.4 27.5 %collective-permute-done.19.refs_15_ = bf16[1280,128]{1,0:T(8,128)(2,1)S(1)} collective-permute-done((bf16[1280,128]{1,0:T(8,128)(2,1)}, bf16[1280,128]{1,0:T(8,128)(2,1)S(1)}, u32[]{:S(2)}, u32[]{:S(2)}) %collective-permute-start.19) | collective-permute-done | bytes 327712 | tf_op jit(solution)/shard_map/ppermute | solution.py:22
  133.9 1.8 %collective-permute-start.16 = (bf16[1280,128]{1,0:T(8,128)(2,1)}, bf16[1280,128]{1,0:T(8,128)(2,1)S(1)}, u32[]{:S(2)}, u32[]{:S(2)}) collective-permute-start(bf16[1280,128]{1,0:T(8,128)(2,1)} %collective-permute-done.4.refs_3_.refs_5_), channel_id=1, source_target_pairs={{0,64},{64,0},{128,192},{192,128},{1,65},{65,1},{129,193},{193,129... | collective-permute-start | bytes 983048 | tf_op jit(solution)/shard_map/ppermute | solution.py:22
  135.9 8.8 %collective-permute-done.16.refs_12_ = bf16[1280,128]{1,0:T(8,128)(2,1)S(1)} collective-permute-done((bf16[1280,128]{1,0:T(8,128)(2,1)}, bf16[1280,128]{1,0:T(8,128)(2,1)S(1)}, u32[]{:S(2)}, u32[]{:S(2)}) %collective-permute-start.16) | collective-permute-done | bytes 327712 | tf_op jit(solution)/shard_map/ppermute | solution.py:22
  144.7 1.5 collective-permute-start.20
  146.9 2.6 %collective-permute-start.17 = (bf16[768,128]{1,0:T(8,128)(2,1)}, bf16[768,128]{1,0:T(8,128)(2,1)}, u32[]{:S(2)}, u32[]{:S(2)}) collective-permute-start(bf16[768,128]{1,0:T(8,128)(2,1)} %collective-permute-done.7.refs_6_.refs_8_), channel_id=1, source_target_pairs={{0,64},{64,0},{128,192},{192,128},{1,65},{65,1},{129,193},{193,129... | collective-permute-start | bytes 589832 | tf_op jit(solution)/shard_map/ppermute | solution.py:22
  149.5 16.4 %shard_map.49 = (bf16[512,128]{1,0:T(8,128)(2,1)}, bf16[512,128]{1,0:T(8,128)(2,1)}) custom-call(s32[1]{0:T(128)} %bitcast.me_ref, s32[1]{0:T(128)S(6)} %and.5.core_ref, f32[32,24,128]{2,1,0:T(8,128)} %copy-done.2, f32[32,24,128]{2,1,0:T(8,128)} %copy-done.6, s32[2,256,128]{2,1,0:T(8,128)} %start_ref.1), custom_call_target="tpu_custom_call" | custom-call | flops 1073741824 | bytes 1048576 | tf_op jit(solution)/shard_map/pallas_call | solution.py:520
  166.0 6.6 %shard_map.50 = bf16[16,512,128]{2,1,0:T(8,128)(2,1)} custom-call(s32[1]{0:T(128)} %bitcast.me_ref, bf16[512,128]{1,0:T(8,128)(2,1)} %get-tuple-element.37.high_ref, bf16[512,128]{1,0:T(8,128)(2,1)} %get-tuple-element.38.low_ref, bf16[6144,128]{1,0:T(8,128)(2,1)} %get-tuple-element.28.refs_0_, bf16[4096,128]{1,0:T(8,128)(2,1)} %get-tuple-element.39.refs_1_, ...), custom_call_target="tpu_custom_call" | custom-call | flops 2147483648 | bytes 10485760 | tf_op jit(solution)/shard_map/pallas_call | solution.py:571
  (45 shorter events, 4.4 us)
Async XLA Ops:
  2.2 17.7 %collective-permute-start = (bf16[1568,128]{1,0:T(8,128)(2,1)S(1)}, bf16[1568,128]{1,0:T(8,128)(2,1)}, u32[]{:S(2)}, u32[]{:S(2)}) collective-permute-start(bf16[1568,128]{1,0:T(8,128)(2,1)S(1)} %concatenate.6), channel_id=1, source_target_pairs={{0,1},{1,2},{2,3},{3,4},{4,5},{5,6},{6,7},{7,8},{8,9},{9,10},{10,1... | collective-permute-start | bytes 1204232 | tf_op jit(solution)/shard_map/ppermute | solution.py:602
  5.1 14.9 %collective-permute-start.1 = (bf16[1568,128]{1,0:T(8,128)(2,1)S(1)}, bf16[1568,128]{1,0:T(8,128)(2,1)}, u32[]{:S(2)}, u32[]{:S(2)}) collective-permute-start(bf16[1568,128]{1,0:T(8,128)(2,1)S(1)} %concatenate.7), channel_id=1, source_target_pairs={{1,0},{2,1},{3,2},{4,3},{5,4},{6,5},{7,6},{8,7},{9,8},{10,9},{11,1... | collective-permute-start | bytes 1204232 | tf_op jit(solution)/shard_map/ppermute | solution.py:603
  16.4 15.2 %collective-permute-start.2 = (bf16[1280,128]{1,0:T(8,128)(2,1)}, bf16[1280,128]{1,0:T(8,128)(2,1)}, u32[]{:S(2)}, u32[]{:S(2)}) collective-permute-start(bf16[1280,128]{1,0:T(8,128)(2,1)} %get-tuple-element.29), channel_id=1, source_target_pairs={{0,64},{64,0},{128,192},{192,128},{1,65},{65,1},{129,193},{193,129... | collective-permute-start | bytes 983048 | tf_op jit(solution)/shard_map/ppermute | solution.py:22
  18.3 16.4 %collective-permute-start.3 = (bf16[1280,128]{1,0:T(8,128)(2,1)}, bf16[1280,128]{1,0:T(8,128)(2,1)}, u32[]{:S(2)}, u32[]{:S(2)}) collective-permute-start(bf16[1280,128]{1,0:T(8,128)(2,1)} %get-tuple-element.30), channel_id=1, source_target_pairs={{0,128},{64,192},{128,0},{192,64},{1,129},{65,193},{129,1},{193,65... | collective-permute-start | bytes 983048 | tf_op jit(solution)/shard_map/ppermute | solution.py:22
  19.4 17.7 %collective-permute-start.4 = (bf16[1280,128]{1,0:T(8,128)(2,1)}, bf16[1280,128]{1,0:T(8,128)(2,1)}, u32[]{:S(2)}, u32[]{:S(2)}) collective-permute-start(bf16[1280,128]{1,0:T(8,128)(2,1)} %get-tuple-element.31), channel_id=1, source_target_pairs={{0,192},{64,128},{128,64},{192,0},{1,193},{65,129},{129,65},{193,1... | collective-permute-start | bytes 983048 | tf_op jit(solution)/shard_map/ppermute | solution.py:22
  28.1 9.8 %collective-permute-start.5 = (bf16[768,128]{1,0:T(8,128)(2,1)}, bf16[768,128]{1,0:T(8,128)(2,1)}, u32[]{:S(2)}, u32[]{:S(2)}) collective-permute-start(bf16[768,128]{1,0:T(8,128)(2,1)} %get-tuple-element.32), channel_id=1, source_target_pairs={{0,64},{64,0},{128,192},{192,128},{1,65},{65,1},{129,193},{193,129... | collective-permute-start | bytes 589832 | tf_op jit(solution)/shard_map/ppermute | solution.py:22
  31.2 11.8 %collective-permute-start.6 = (bf16[768,128]{1,0:T(8,128)(2,1)}, bf16[768,128]{1,0:T(8,128)(2,1)S(1)}, u32[]{:S(2)}, u32[]{:S(2)}) collective-permute-start(bf16[768,128]{1,0:T(8,128)(2,1)} %get-tuple-element.33), channel_id=1, source_target_pairs={{0,128},{64,192},{128,0},{192,64},{1,129},{65,193},{129,1},{193,65... | collective-permute-start | bytes 589832 | tf_op jit(solution)/shard_map/ppermute | solution.py:22
  31.6 13.9 %collective-permute-start.7 = (bf16[768,128]{1,0:T(8,128)(2,1)}, bf16[768,128]{1,0:T(8,128)(2,1)}, u32[]{:S(2)}, u32[]{:S(2)}) collective-permute-start(bf16[768,128]{1,0:T(8,128)(2,1)} %get-tuple-element.34), channel_id=1, source_target_pairs={{0,192},{64,128},{128,64},{192,0},{1,193},{65,129},{129,65},{193,1... | collective-permute-start | bytes 589832 | tf_op jit(solution)/shard_map/ppermute | solution.py:22
  43.0 2.5 %copy-start.5 = (bf16[768,128]{1,0:T(8,128)(2,1)}, bf16[768,128]{1,0:T(8,128)(2,1)S(1)}, u32[]{:S(2)}) copy-start(bf16[768,128]{1,0:T(8,128)(2,1)S(1)} %collective-permute-done.6.refs_5_.refs_7_) | copy-start | bytes 589828
  49.1 35.4 %copy-start = (bf16[6144,128]{1,0:T(8,128)(2,1)S(1)}, bf16[6144,128]{1,0:T(8,128)(2,1)}, u32[]{:S(2)}) copy-start(bf16[6144,128]{1,0:T(8,128)(2,1)} %get-tuple-element.28.refs_0_) | copy-start | bytes 4718596
  49.1 2.0 %collective-permute-start.8 = (f32[32,24,128]{2,1,0:T(8,128)}, f32[32,24,128]{2,1,0:T(8,128)S(1)}, u32[]{:S(2)}, u32[]{:S(2)}) collective-permute-start(f32[32,24,128]{2,1,0:T(8,128)} %get-tuple-element.36), channel_id=1, source_target_pairs={{0,1},{1,0},{2,3},{3,2},{4,5},{5,4},{6,7},{7,6},{8,9},{9,8},{10,11... | collective-permute-start | bytes 1179656 | tf_op jit(solution)/shard_map/ppermute | solution.py:26
  51.1 42.3 %copy-start.1 = (bf16[2048,128]{1,0:T(8,128)(2,1)S(1)}, bf16[2048,128]{1,0:T(8,128)(2,1)}, u32[]{:S(2)}) copy-start(bf16[2048,128]{1,0:T(8,128)(2,1)} %get-tuple-element.40.refs_2_) | copy-start | bytes 1572868
  79.3 7.2 %collective-permute-start.11 = (f32[24,128]{1,0:T(8,128)S(1)}, f32[24,128]{1,0:T(8,128)S(1)}, u32[]{:S(2)}, u32[]{:S(2)}) collective-permute-start(f32[24,128]{1,0:T(8,128)S(1)} %reduce_sum.9), channel_id=1, source_target_pairs={{0,192},{64,128},{128,64},{192,0},{1,193},{65,129},{129,65},{193,1... | collective-permute-start | bytes 36872 | tf_op jit(solution)/shard_map/ppermute | solution.py:22
  79.9 6.6 %collective-permute-start.10 = (f32[24,128]{1,0:T(8,128)S(1)}, f32[24,128]{1,0:T(8,128)S(1)}, u32[]{:S(2)}, u32[]{:S(2)}) collective-permute-start(f32[24,128]{1,0:T(8,128)S(1)} %reduce_sum.9), channel_id=1, source_target_pairs={{0,128},{64,192},{128,0},{192,64},{1,129},{65,193},{129,1},{193,65... | collective-permute-start | bytes 36872 | tf_op jit(solution)/shard_map/ppermute | solution.py:22
  84.5 3.8 %collective-permute-start.9 = (f32[24,128]{1,0:T(8,128)S(1)}, f32[24,128]{1,0:T(8,128)S(1)}, u32[]{:S(2)}, u32[]{:S(2)}) collective-permute-start(f32[24,128]{1,0:T(8,128)S(1)} %reduce_sum.9), channel_id=1, source_target_pairs={{0,64},{64,0},{128,192},{192,128},{1,65},{65,1},{129,193},{193,129... | collective-permute-start | bytes 36872 | tf_op jit(solution)/shard_map/ppermute | solution.py:22
  84.5 81.5 %collective-permute-start.13 = (bf16[6144,128]{1,0:T(8,128)(2,1)S(1)}, bf16[6144,128]{1,0:T(8,128)(2,1)}, u32[]{:S(2)}, u32[]{:S(2)}) collective-permute-start(bf16[6144,128]{1,0:T(8,128)(2,1)S(1)} %copy-done), channel_id=1, source_target_pairs={{0,64},{64,0},{128,192},{192,128},{1,65},{65,1},{129,193},{193,129... | collective-permute-start | bytes 4718600 | tf_op jit(solution)/shard_map/ppermute | solution.py:22
  89.1 17.3 %all-to-all-start.1 = ((f32[32,24,128]{2,1,0:T(8,128)}), f32[32,24,128]{2,1,0:T(8,128)S(1)}, u32[]{:S(2)}, u32[]{:S(2)}) async-start(f32[32,24,128]{2,1,0:T(8,128)} %broadcast_in_dim.3), calls=%async_computation.1 | async-start | bytes 786432 | tf_op jit(solution)/shard_map/all_to_all | solution.py:30
  93.4 42.3 %collective-permute-start.15 = (bf16[2048,128]{1,0:T(8,128)(2,1)S(1)}, bf16[2048,128]{1,0:T(8,128)(2,1)}, u32[]{:S(2)}, u32[]{:S(2)}) collective-permute-start(bf16[2048,128]{1,0:T(8,128)(2,1)S(1)} %copy-done.1), channel_id=1, source_target_pairs={{0,192},{64,128},{128,64},{192,0},{1,193},{65,129},{129,65},{193,1... | collective-permute-start | bytes 1572872 | tf_op jit(solution)/shard_map/ppermute | solution.py:22
  93.5 72.5 %collective-permute-start.14 = (bf16[4096,128]{1,0:T(8,128)(2,1)}, bf16[4096,128]{1,0:T(8,128)(2,1)}, u32[]{:S(2)}, u32[]{:S(2)}) collective-permute-start(bf16[4096,128]{1,0:T(8,128)(2,1)} %get-tuple-element.39.refs_1_), channel_id=1, source_target_pairs={{0,192},{64,128},{128,64},{192,0},{1,193},{65,129},{129,65},{193,1... | collective-permute-start | bytes 3145736 | tf_op jit(solution)/shard_map/ppermute | solution.py:22
  95.5 38.4 %collective-permute-start.19 = (bf16[1280,128]{1,0:T(8,128)(2,1)}, bf16[1280,128]{1,0:T(8,128)(2,1)S(1)}, u32[]{:S(2)}, u32[]{:S(2)}) collective-permute-start(bf16[1280,128]{1,0:T(8,128)(2,1)} %collective-permute-done.2.refs_1_.refs_3_), channel_id=1, source_target_pairs={{0,192},{64,128},{128,64},{192,0},{1,193},{65,129},{129,65},{193,1... | collective-permute-start | bytes 983048 | tf_op jit(solution)/shard_map/ppermute | solution.py:22
  106.4 43.1 %copy-start.2 = (f32[32,24,128]{2,1,0:T(8,128)}, f32[32,24,128]{2,1,0:T(8,128)S(1)}, u32[]{:S(2)}) copy-start(f32[32,24,128]{2,1,0:T(8,128)S(1)} %all-to-all-done.1.own_hbm) | copy-start | bytes 1179652
  106.4 39.7 %collective-permute-start.12 = (f32[32,24,128]{2,1,0:T(8,128)S(1)}, f32[32,24,128]{2,1,0:T(8,128)S(1)}, u32[]{:S(2)}, u32[]{:S(2)}) collective-permute-start(f32[32,24,128]{2,1,0:T(8,128)S(1)} %all-to-all-done.1.own_hbm), channel_id=1, source_target_pairs={{0,1},{1,0},{2,3},{3,2},{4,5},{5,4},{6,7},{7,6},{8,9},{9,8},{10,11... | collective-permute-start | bytes 1179656 | tf_op jit(solution)/shard_map/ppermute | solution.py:26
  133.9 12.3 %copy-start.3 = (bf16[1280,128]{1,0:T(8,128)(2,1)}, bf16[1280,128]{1,0:T(8,128)(2,1)S(1)}, u32[]{:S(2)}) copy-start(bf16[1280,128]{1,0:T(8,128)(2,1)S(1)} %collective-permute-done.19.refs_15_) | copy-start | bytes 983044
  133.9 10.8 %collective-permute-start.16 = (bf16[1280,128]{1,0:T(8,128)(2,1)}, bf16[1280,128]{1,0:T(8,128)(2,1)S(1)}, u32[]{:S(2)}, u32[]{:S(2)}) collective-permute-start(bf16[1280,128]{1,0:T(8,128)(2,1)} %collective-permute-done.4.refs_3_.refs_5_), channel_id=1, source_target_pairs={{0,64},{64,0},{128,192},{192,128},{1,65},{65,1},{129,193},{193,129... | collective-permute-start | bytes 983048 | tf_op jit(solution)/shard_map/ppermute | solution.py:22
  135.7 30.2 %collective-permute-start.18 = (bf16[2048,128]{1,0:T(8,128)(2,1)}, bf16[2048,128]{1,0:T(8,128)(2,1)}, u32[]{:S(2)}, u32[]{:S(2)}) collective-permute-start(bf16[2048,128]{1,0:T(8,128)(2,1)} %collective-permute-done.15.refs_11_), channel_id=1, source_target_pairs={{0,64},{64,0},{128,192},{192,128},{1,65},{65,1},{129,193},{193,129... | collective-permute-start | bytes 1572872 | tf_op jit(solution)/shard_map/ppermute | solution.py:22
  144.7 1.5 copy-start.4
  144.7 21.3 %collective-permute-start.20 = (bf16[768,128]{1,0:T(8,128)(2,1)}, bf16[768,128]{1,0:T(8,128)(2,1)}, u32[]{:S(2)}, u32[]{:S(2)}) collective-permute-start(bf16[768,128]{1,0:T(8,128)(2,1)} %collective-permute-done.5.refs_4_.refs_6_), channel_id=1, source_target_pairs={{0,192},{64,128},{128,64},{192,0},{1,193},{65,129},{129,65},{193,1... | collective-permute-start | bytes 589832 | tf_op jit(solution)/shard_map/ppermute | solution.py:22
  146.1 0.7 copy-start.6
  146.9 19.1 %collective-permute-start.17 = (bf16[768,128]{1,0:T(8,128)(2,1)}, bf16[768,128]{1,0:T(8,128)(2,1)}, u32[]{:S(2)}, u32[]{:S(2)}) collective-permute-start(bf16[768,128]{1,0:T(8,128)(2,1)} %collective-permute-done.7.refs_6_.refs_8_), channel_id=1, source_target_pairs={{0,64},{64,0},{128,192},{192,128},{1,65},{65,1},{129,193},{193,129... | collective-permute-start | bytes 589832 | tf_op jit(solution)/shard_map/ppermute | solution.py:22

commit v6 on v5

--- a/solution.py
+++ b/solution.py
@@ -15,7 +15,7 @@
     return (z * 4 + y) * 2 + core
 
 
-PLANES = [[at(z, y, core) for z in range(8) for y in range(4)] for core in range(2)]
+LINES = [[at(z, y, core) for z in range(8)] for y in range(4) for core in range(2)]
 
 
 def case_swap(value, apart):
@@ -26,8 +26,13 @@
     return lax.ppermute(value, "tile", [(source, source ^ 1) for source in range(64)])
 
 
-def plane_exchange(value):
-    return lax.all_to_all(value, "tile", 0, 0, axis_index_groups=PLANES)
+def row_swap(value, apart):
+    pairs = [(at(z, y, c), at(z, y ^ apart, c)) for z in range(8) for y in range(4) for c in range(2)]
+    return lax.ppermute(value, "tile", pairs)
+
+
+def line_exchange(value):
+    return lax.all_to_all(value, "tile", 0, 0, axis_index_groups=LINES)
 
 
 AB = (((1,), (0,)), ((), ()))
@@ -122,7 +127,7 @@
     return [jnp.concatenate(a, 0) for a in tiles]
 
 
-def mixing(cells, me_ref, core_ref, own_hbm, other_hbm, start_ref, high_ref, low_ref, *scratch):
+def mixing(cells, me_ref, core_ref, y_ref, own_hbm, other_hbm, start_ref, high_ref, low_ref, *scratch):
     gram_ref, own_ref, other_ref, sems = scratch
     me, core = me_ref[0], core_ref[0]
     loads = [
@@ -138,11 +143,13 @@
         @pl.when(core == side)
         def _(side=side):
             for half, ref in enumerate((own_ref, other_ref) if side == 0 else (other_ref, own_ref)):
-                rows = ref[:, 0:16].reshape(4, 128, 128)
-                for i in range(4):
-                    gram_ref[5 * half + i] = rows[i]
-                for k in range(32):
-                    gram_ref[5 * half + 4, 4 * k : 4 * k + 4] = ref[k, 16:20]
+                for y in range(4):
+                    slot = y_ref[0] ^ y
+                    for z in range(8):
+                        k = 4 * z + y
+                        row = 16 * (k % 8)
+                        gram_ref[5 * half + k // 8, row : row + 16] = ref[slot, z, 0:16]
+                        gram_ref[5 * half + 4, 4 * k : 4 * k + 4] = ref[slot, z, 16:20]
 
     odd = lax.rem(me, 2) == 1
     upper = me // 2
@@ -463,7 +470,7 @@
     )(me, tile, weights, own, kp, low, high, edge_one, edge_two, *stacks)
 
 
-def grams(me_ref, core_ref, *refs):
+def grams(me_ref, core_ref, y_ref, *refs):
     pieces, own_ref, other_ref, wide, sems = refs[:7], refs[7], refs[8], refs[9], refs[10]
     me, core = me_ref[0], core_ref[0]
     copies = []
@@ -494,40 +501,44 @@
         def _(side=side):
             for half, ref in enumerate((own_ref, other_ref) if side == 0 else (other_ref, own_ref)):
                 mine = blocks[5 * half : 5 * half + 5]
-                ref[:, 0:16] = jnp.concatenate(mine[:4], 0).reshape(32, 16, 128)
-                ref[:, 16:24] = jnp.zeros((32, 8, 128), jnp.float32)
-                for k in range(32):
-                    ref[k, 16:20] = mine[4][4 * k : 4 * k + 4]
-
-
-def grams_call(me, core, pieces):
-    shape = jax.ShapeDtypeStruct((32, 24, 128), jnp.float32)
+                big = jnp.concatenate(mine[:4], 0)
+                for y in range(4):
+                    slot = y_ref[0] ^ y
+                    for z in range(8):
+                        k = 4 * z + y
+                        ref[slot, z, 0:16] = big[16 * k : 16 * k + 16]
+                        ref[slot, z, 16:24] = jnp.zeros((8, 128), jnp.float32)
+                        ref[slot, z, 16:20] = mine[4][4 * k : 4 * k + 4]
+
+
+def grams_call(me, core, row, pieces):
+    shape = jax.ShapeDtypeStruct((4, 8, 24, 128), jnp.float32)
     return pl.pallas_call(
         grams,
         out_shape=(shape, shape),
-        in_specs=[SM, SM] + [ANY] * 7,
+        in_specs=[SM, SM, SM] + [ANY] * 7,
         out_specs=(VM, VM),
         scratch_shapes=[pltpu.VMEM((PIECE, 512), jnp.bfloat16), pltpu.SemaphoreType.DMA((7,))],
         compiler_params=pltpu.CompilerParams(vmem_limit_bytes=63 << 20),
         cost_estimate=pl.CostEstimate(flops=2 * 2048 * 512 * 512, bytes_accessed=3 << 20, transcendentals=0),
-    )(me, core, *pieces)
-
-
-def mixing_call(cells, me, core, own, other, start_codes):
+    )(me, core, row, *pieces)
+
+
+def mixing_call(cells, me, core, row, own, other, start_codes):
     shape = jax.ShapeDtypeStruct((512, 128), jnp.bfloat16)
     vmem = pl.BlockSpec(memory_space=pltpu.VMEM)
     smem = pl.BlockSpec(memory_space=pltpu.SMEM)
     return pl.pallas_call(
         functools.partial(mixing, cells),
         out_shape=(shape, shape),
-        in_specs=[smem, smem, ANY, ANY, vmem],
+        in_specs=[smem, smem, smem, ANY, ANY, vmem],
         out_specs=(vmem, vmem),
         scratch_shapes=[pltpu.VMEM((10, 128, 128), jnp.float32)]
-        + [pltpu.VMEM((32, 24, 128), jnp.float32)] * 2
+        + [pltpu.VMEM((4, 8, 24, 128), jnp.float32)] * 2
         + [pltpu.SemaphoreType.DMA((2,))],
         compiler_params=pltpu.CompilerParams(vmem_limit_bytes=62 << 20),
         cost_estimate=pl.CostEstimate(flops=1 << 30, bytes_accessed=1 << 20, transcendentals=0),
-    )(me, core, own, other, start_codes)
+    )(me, core, row, own, other, start_codes)
 
 
 def finish(plan, me_ref, high_ref, low_ref, *refs):
@@ -595,6 +606,7 @@
     me = lax.axis_index("case").astype(jnp.int32).reshape(1)
     tile = lax.axis_index("tile").astype(jnp.int32).reshape(1)
     core = tile & 1
+    row = (tile >> 1) & 3
     cells = forcing.shape[1] * lax.axis_size("tile") * forcing.shape[2]
     own, kp = forcing[0], permeability[0]
     up = [(i, i + 1) for i in range(63)]
@@ -609,13 +621,15 @@
     far_one, far_two, far_three = case_swap(one, 1), case_swap(two, 3), case_swap(three, 3)
     via_one = [case_swap(met[2], 1), case_swap(met[5], 1), case_swap(far_three, 1)]
     via_three = [case_swap(met[0], 3), case_swap(met[3], 3)]
-    own_part, other_part = grams_call(me, core, [one] + met)
+    own_part, other_part = grams_call(me, core, row, [one] + met)
     part = own_part + core_swap(other_part)
-    part = plane_exchange(part).sum(0)
+    part = part[0] + row_swap(part[1], 1) + row_swap(part[2], 2) + row_swap(part[3], 3)
+    part = line_exchange(part).sum(0)
     part = part + case_swap(part, 1) + case_swap(part, 2) + case_swap(part, 3)
-    mine = plane_exchange(jnp.broadcast_to(part, (32,) + part.shape))
+    mine = line_exchange(jnp.broadcast_to(part, (8,) + part.shape))
+    mine = jnp.stack([mine, row_swap(mine, 1), row_swap(mine, 2), row_swap(mine, 3)])
     yours = core_swap(mine)
-    high, low = mixing_call(cells, me, core, mine, yours, start_codes)
+    high, low = mixing_call(cells, me, core, row, mine, yours, start_codes)
     pieces = [one, two, three] + met + [far_one, far_two, far_three] + via_one + via_three
     whole = ((0, PIECE),)
     split = ((0, INNER), (INNER, OUTER))

time: 173 us -> 185 us (1.069)
  the two profiles are of different devices: /device:TPU:2 before, /device:TPU:10 now
where the time goes in v6:
time: 185 us
  waiting for transfers between devices  70.7 us (38%)
  starting transfers between devices  47.9 us (26%)
  Pallas kernels  43.9 us (24%)
  blocking collectives  16.1 us (9%)
  local copies, waits for them, and re-layouts  3.98 us (2%)
    ppermute x17, waiting for transfers between devices, case_swap(): lax.ppermute(value, 'case', [(source, source ^ apart) for source in range...  52.2 us
    ppermute x17, starting transfers between devices, case_swap(): lax.ppermute(value, 'case', [(source, source ^ apart) for source in range...  25.9 us
    pallas_call x1, Pallas kernels, mixing_call(): pl.pallas_call(functools.partial(mixing, cells), out_shape=(shape, shape)...  16.4 us
    all_to_all x1, blocking collectives, line_exchange(): return lax.all_to_all(value, 'tile', 0, 0, axis_index_groups=LINES)  16.1 us
    ppermute x6, waiting for transfers between devices, row_swap(): return lax.ppermute(value, 'tile', pairs)  9.93 us
    pallas_call x1, Pallas kernels, inner_call(): pl.pallas_call(inner_rows, out_shape=[half(INNER)] * 3 + [half(3 * PIECE)...  9.37 us
    all_to_all x1, starting transfers between devices, line_exchange(): return lax.all_to_all(value, 'tile', 0, 0, axis_index_groups=LINES)  8.47 us
    pallas_call x1, Pallas kernels, outer_call(): pl.pallas_call(outer_rows, out_shape=[half(OUTER)] * 3 + [half(3 * PIECE)...  8.05 us
  transfers between devices with their start and end apart: 28, of which 15 were waited for; matrix products, arithmetic and copies ran while one was open for 1% of the time, Pallas kernels for 18%

profile of v6, /device:TPU:10, one launch (start us, length us, event | category | flops | bytes accessed | tf_op | source)
XLA Modules:
  0.0 184.8 jit_solution(3397404234187783801)
XLA Ops:
  2.2 1.9 %collective-permute-start = (bf16[1568,128]{1,0:T(8,128)(2,1)S(1)}, bf16[1568,128]{1,0:T(8,128)(2,1)}, u32[]{:S(2)}, u32[]{:S(2)}) collective-permute-start(bf16[1568,128]{1,0:T(8,128)(2,1)S(1)} %concatenate.6), channel_id=1, source_target_pairs={{0,1},{1,2},{2,3},{3,4},{4,5},{5,6},{6,7},{7,8},{8,9},{9,10},{10,1... | collective-permute-start | bytes 1204232 | tf_op jit(solution)/shard_map/ppermute | solution.py:614
  4.5 3.6 %collective-permute-start.1 = (bf16[1568,128]{1,0:T(8,128)(2,1)S(1)}, bf16[1568,128]{1,0:T(8,128)(2,1)}, u32[]{:S(2)}, u32[]{:S(2)}) collective-permute-start(bf16[1568,128]{1,0:T(8,128)(2,1)S(1)} %concatenate.7), channel_id=1, source_target_pairs={{1,0},{2,1},{3,2},{4,3},{5,4},{6,5},{7,6},{8,7},{9,8},{10,9},{11,1... | collective-permute-start | bytes 1204232 | tf_op jit(solution)/shard_map/ppermute | solution.py:615
  8.8 9.4 %shard_map.46 = (bf16[1280,128]{1,0:T(8,128)(2,1)}, bf16[1280,128]{1,0:T(8,128)(2,1)}, bf16[1280,128]{1,0:T(8,128)(2,1)}, bf16[6144,128]{1,0:T(8,128)(2,1)}, bf1...) custom-call(s32[1]{0:T(128)} %bitcast.me_ref, ...), custom_call_target="tpu_custom_call" | custom-call | flops 419430400 | bytes 9437184 | tf_op jit(solution)/shard_map/pallas_call | solution.py:441
  18.8 2.4 %collective-permute-start.3 = (bf16[1280,128]{1,0:T(8,128)(2,1)}, bf16[1280,128]{1,0:T(8,128)(2,1)}, u32[]{:S(2)}, u32[]{:S(2)}) collective-permute-start(bf16[1280,128]{1,0:T(8,128)(2,1)} %get-tuple-element.30), channel_id=1, source_target_pairs={{0,128},{64,192},{128,0},{192,64},{1,129},{65,193},{129,1},{193,65... | collective-permute-start | bytes 983048 | tf_op jit(solution)/shard_map/ppermute | solution.py:22
  21.8 8.1 %shard_map.47 = (bf16[768,128]{1,0:T(8,128)(2,1)}, bf16[768,128]{1,0:T(8,128)(2,1)}, bf16[768,128]{1,0:T(8,128)(2,1)}, bf16[6144,128]{1,0:T(8,128)(2,1)}, bf16[4...) custom-call(s32[1]{0:T(128)} %bitcast.me_ref, ...), custom_call_target="tpu_custom_call", output_to_operand_aliasing={{3}: (9, {}), {4}: (10, {}), {5}: (11, {})} | custom-call | flops 209715200 | bytes 9437184 | tf_op jit(solution)/shard_map/pallas_call | solution.py:456
  29.8 1.8 collective-permute-start.5
  31.7 1.7 collective-permute-start.6
  33.8 3.3 %collective-permute-done.3.refs_2_.refs_4_ = bf16[1280,128]{1,0:T(8,128)(2,1)} collective-permute-done((bf16[1280,128]{1,0:T(8,128)(2,1)}, bf16[1280,128]{1,0:T(8,128)(2,1)}, u32[]{:S(2)}, u32[]{:S(2)}) %collective-permute-start.3) | collective-permute-done | bytes 327712 | tf_op jit(solution)/shard_map/ppermute | solution.py:22
  37.2 1.8 collective-permute-done.4.refs_3_.refs_5_
  39.0 1.5 collective-permute-done.5.refs_4_.refs_6_
  40.5 4.1 %collective-permute-done.6.refs_5_.refs_7_ = bf16[768,128]{1,0:T(8,128)(2,1)S(1)} collective-permute-done((bf16[768,128]{1,0:T(8,128)(2,1)}, bf16[768,128]{1,0:T(8,128)(2,1)S(1)}, u32[]{:S(2)}, u32[]{:S(2)}) %collective-permute-start.6) | collective-permute-done | bytes 196640 | tf_op jit(solution)/shard_map/ppermute | solution.py:22
  44.6 1.4 collective-permute-done.7.refs_6_.refs_8_
  46.0 3.5 %shard_map.48 = (f32[4,8,24,128]{3,2,1,0:T(8,128)}, f32[4,8,24,128]{3,2,1,0:T(8,128)}) custom-call(s32[1]{0:T(128)} %bitcast.me_ref, s32[1]{0:T(128)S(6)} %and.8.core_ref, s32[1]{0:T(128)S(6)} %and.9.y_ref, bf16[6144,128]{1,0:T(8,128)(2,1)} %get-tuple-element.28.refs_0_, bf16[1280,128]{1,0:T(8,128)(2,1)} %collective-permute-done.2.refs_1_.refs_3_, ...), custom_call_target="tpu_custom_call" | custom-call | flops 1073741824 | bytes 3145728 | tf_op jit(solution)/shard_map/pallas_call | solution.py:516
  49.7 1.9 %collective-permute-done.8 = f32[4,8,24,128]{3,2,1,0:T(8,128)S(1)} collective-permute-done((f32[4,8,24,128]{3,2,1,0:T(8,128)}, f32[4,8,24,128]{3,2,1,0:T(8,128)S(1)}, u32[]{:S(2)}, u32[]{:S(2)}) %collective-permute-start.8) | collective-permute-done | bytes 393248 | tf_op jit(solution)/shard_map/ppermute | solution.py:26
  52.8 2.8 %collective-permute-start.11 = (f32[8,24,128]{2,1,0:T(8,128)S(1)}, f32[8,24,128]{2,1,0:T(8,128)S(1)}, u32[]{:S(2)}, u32[]{:S(2)}) collective-permute-start(f32[8,24,128]{2,1,0:T(8,128)S(1)} %get-tuple-element.48), channel_id=1, source_target_pairs={{0,6},{1,7},{2,4},{3,5},{4,2},{5,3},{6,0},{7,1},{8,14},{9,15},{10,... | collective-permute-start | bytes 294920 | tf_op jit(solution)/shard_map/ppermute | solution.py:31
  56.8 3.0 %collective-permute-start.19 = (bf16[6144,128]{1,0:T(8,128)(2,1)S(1)}, bf16[6144,128]{1,0:T(8,128)(2,1)}, u32[]{:S(2)}, u32[]{:S(2)}) collective-permute-start(bf16[6144,128]{1,0:T(8,128)(2,1)S(1)} %copy-done), channel_id=1, source_target_pairs={{0,64},{64,0},{128,192},{192,128},{1,65},{65,1},{129,193},{193,129... | collective-permute-start | bytes 4718600 | tf_op jit(solution)/shard_map/ppermute | solution.py:22
  59.9 1.8 collective-permute-done.10
  61.7 16.1 %all_to_all.10 = f32[8,24,128]{2,1,0:T(8,128)S(1)} all-to-all(f32[8,24,128]{2,1,0:T(8,128)S(1)} %fusion.2), channel_id=1, replica_groups={{0,8,16,24,32,40,48,56},{1,9,17,25,33,41,49,57},{2,10,18,26,34,42,50,58..., dimensions={0} | all-to-all | bytes 196608 | tf_op jit(solution)/shard_map/all_to_all | solution.py:35
  78.5 4.5 %collective-permute-start.13 = (f32[24,128]{1,0:T(8,128)S(1)}, f32[24,128]{1,0:T(8,128)S(1)}, u32[]{:S(2)}, u32[]{:S(2)}) collective-permute-start(f32[24,128]{1,0:T(8,128)S(1)} %reduce_sum.9), channel_id=1, source_target_pairs={{0,128},{64,192},{128,0},{192,64},{1,129},{65,193},{129,1},{193,65... | collective-permute-start | bytes 36872 | tf_op jit(solution)/shard_map/ppermute | solution.py:22
  83.0 10.4 %collective-permute-done.13 = f32[24,128]{1,0:T(8,128)S(1)} collective-permute-done((f32[24,128]{1,0:T(8,128)S(1)}, f32[24,128]{1,0:T(8,128)S(1)}, u32[]{:S(2)}, u32[]{:S(2)}) %collective-permute-start.13) | collective-permute-done | bytes 12320 | tf_op jit(solution)/shard_map/ppermute | solution.py:22
  94.9 8.5 %all-to-all-start.1 = ((f32[8,24,128]{2,1,0:T(8,128)}), f32[8,24,128]{2,1,0:T(8,128)S(1)}, u32[]{:S(2)}, u32[]{:S(2)}) async-start(f32[8,24,128]{2,1,0:T(8,128)} %broadcast_in_dim.3), calls=%async_computation.1 | async-start | bytes 196608 | tf_op jit(solution)/shard_map/all_to_all | solution.py:35
  103.4 1.4 collective-permute-start.21
  105.5 6.6 %all-to-all-done.1 = f32[8,24,128]{2,1,0:T(8,128)S(1)} async-done(((f32[8,24,128]{2,1,0:T(8,128)}), f32[8,24,128]{2,1,0:T(8,128)S(1)}, u32[]{:S(2)}, u32[]{:S(2)}) %all-to-all-start.1) | async-done | bytes 98336 | tf_op jit(solution)/shard_map/all_to_all | solution.py:35
  114.6 2.2 %collective-permute-done.17 = f32[8,24,128]{2,1,0:T(8,128)S(1)} collective-permute-done((f32[8,24,128]{2,1,0:T(8,128)S(1)}, f32[8,24,128]{2,1,0:T(8,128)S(1)}, u32[]{:S(2)}, u32[]{:S(2)}) %collective-permute-start.17) | collective-permute-done | bytes 98336 | tf_op jit(solution)/shard_map/ppermute | solution.py:31
  118.0 2.4 %collective-permute-done.16 = f32[8,24,128]{2,1,0:T(8,128)S(1)} collective-permute-done((f32[8,24,128]{2,1,0:T(8,128)S(1)}, f32[8,24,128]{2,1,0:T(8,128)S(1)}, u32[]{:S(2)}, u32[]{:S(2)}) %collective-permute-start.16) | collective-permute-done | bytes 98336 | tf_op jit(solution)/shard_map/ppermute | solution.py:31
  121.6 3.5 %collective-permute-done.15 = f32[8,24,128]{2,1,0:T(8,128)S(1)} collective-permute-done((f32[8,24,128]{2,1,0:T(8,128)S(1)}, f32[8,24,128]{2,1,0:T(8,128)S(1)}, u32[]{:S(2)}, u32[]{:S(2)}) %collective-permute-start.15) | collective-permute-done | bytes 98336 | tf_op jit(solution)/shard_map/ppermute | solution.py:31
  125.2 20.1 %collective-permute-done.25.refs_15_ = bf16[1280,128]{1,0:T(8,128)(2,1)S(1)} collective-permute-done((bf16[1280,128]{1,0:T(8,128)(2,1)}, bf16[1280,128]{1,0:T(8,128)(2,1)S(1)}, u32[]{:S(2)}, u32[]{:S(2)}) %collective-permute-start.25) | collective-permute-done | bytes 327712 | tf_op jit(solution)/shard_map/ppermute | solution.py:22
  145.3 2.7 %collective-permute-start.22 = (bf16[1280,128]{1,0:T(8,128)(2,1)}, bf16[1280,128]{1,0:T(8,128)(2,1)S(1)}, u32[]{:S(2)}, u32[]{:S(2)}) collective-permute-start(bf16[1280,128]{1,0:T(8,128)(2,1)} %collective-permute-done.4.refs_3_.refs_5_), channel_id=1, source_target_pairs={{0,64},{64,0},{128,192},{192,128},{1,65},{65,1},{129,193},{193,129... | collective-permute-start | bytes 983048 | tf_op jit(solution)/shard_map/ppermute | solution.py:22
  148.1 8.7 %collective-permute-done.22.refs_12_ = bf16[1280,128]{1,0:T(8,128)(2,1)S(1)} collective-permute-done((bf16[1280,128]{1,0:T(8,128)(2,1)}, bf16[1280,128]{1,0:T(8,128)(2,1)S(1)}, u32[]{:S(2)}, u32[]{:S(2)}) %collective-permute-start.22) | collective-permute-done | bytes 327712 | tf_op jit(solution)/shard_map/ppermute | solution.py:22
  158.9 2.6 %collective-permute-start.23 = (bf16[768,128]{1,0:T(8,128)(2,1)}, bf16[768,128]{1,0:T(8,128)(2,1)}, u32[]{:S(2)}, u32[]{:S(2)}) collective-permute-start(bf16[768,128]{1,0:T(8,128)(2,1)} %collective-permute-done.7.refs_6_.refs_8_), channel_id=1, source_target_pairs={{0,64},{64,0},{128,192},{192,128},{1,65},{65,1},{129,193},{193,129... | collective-permute-start | bytes 589832 | tf_op jit(solution)/shard_map/ppermute | solution.py:22
  161.6 16.4 %shard_map.49 = (bf16[512,128]{1,0:T(8,128)(2,1)}, bf16[512,128]{1,0:T(8,128)(2,1)}) custom-call(s32[1]{0:T(128)} %bitcast.me_ref, s32[1]{0:T(128)S(6)} %and.8.core_ref, s32[1]{0:T(128)S(6)} %and.9.y_ref, f32[4,8,24,128]{3,2,1,0:T(8,128)} %copy-done.2, f32[4,8,24,128]{3,2,1,0:T(8,128)} %copy-done.6, s32[2,256,128]{2,1,0:T(8,128)} %start_ref.1), custom_call_target="tpu_custom_call" | custom-call | flops 1073741824 | bytes 1048576 | tf_op jit(solution)/shard_map/pallas_call | solution.py:531
  178.0 6.6 %shard_map.50 = bf16[16,512,128]{2,1,0:T(8,128)(2,1)} custom-call(s32[1]{0:T(128)} %bitcast.me_ref, bf16[512,128]{1,0:T(8,128)(2,1)} %get-tuple-element.37.high_ref, bf16[512,128]{1,0:T(8,128)(2,1)} %get-tuple-element.38.low_ref, bf16[6144,128]{1,0:T(8,128)(2,1)} %get-tuple-element.28.refs_0_, bf16[4096,128]{1,0:T(8,128)(2,1)} %get-tuple-element.39.refs_1_, ...), custom_call_target="tpu_custom_call" | custom-call | flops 2147483648 | bytes 10485760 | tf_op jit(solution)/shard_map/pallas_call | solution.py:582
  (60 shorter events, 16.8 us)
Async XLA Ops:
  2.2 19.5 %collective-permute-start = (bf16[1568,128]{1,0:T(8,128)(2,1)S(1)}, bf16[1568,128]{1,0:T(8,128)(2,1)}, u32[]{:S(2)}, u32[]{:S(2)}) collective-permute-start(bf16[1568,128]{1,0:T(8,128)(2,1)S(1)} %concatenate.6), channel_id=1, source_target_pairs={{0,1},{1,2},{2,3},{3,4},{4,5},{5,6},{6,7},{7,8},{8,9},{9,10},{10,1... | collective-permute-start | bytes 1204232 | tf_op jit(solution)/shard_map/ppermute | solution.py:614
  4.5 17.3 %collective-permute-start.1 = (bf16[1568,128]{1,0:T(8,128)(2,1)S(1)}, bf16[1568,128]{1,0:T(8,128)(2,1)}, u32[]{:S(2)}, u32[]{:S(2)}) collective-permute-start(bf16[1568,128]{1,0:T(8,128)(2,1)S(1)} %concatenate.7), channel_id=1, source_target_pairs={{1,0},{2,1},{3,2},{4,3},{5,4},{6,5},{7,6},{8,7},{9,8},{10,9},{11,1... | collective-permute-start | bytes 1204232 | tf_op jit(solution)/shard_map/ppermute | solution.py:615
  18.2 15.2 %collective-permute-start.2 = (bf16[1280,128]{1,0:T(8,128)(2,1)}, bf16[1280,128]{1,0:T(8,128)(2,1)}, u32[]{:S(2)}, u32[]{:S(2)}) collective-permute-start(bf16[1280,128]{1,0:T(8,128)(2,1)} %get-tuple-element.29), channel_id=1, source_target_pairs={{0,64},{64,0},{128,192},{192,128},{1,65},{65,1},{129,193},{193,129... | collective-permute-start | bytes 983048 | tf_op jit(solution)/shard_map/ppermute | solution.py:22
  18.8 18.4 %collective-permute-start.3 = (bf16[1280,128]{1,0:T(8,128)(2,1)}, bf16[1280,128]{1,0:T(8,128)(2,1)}, u32[]{:S(2)}, u32[]{:S(2)}) collective-permute-start(bf16[1280,128]{1,0:T(8,128)(2,1)} %get-tuple-element.30), channel_id=1, source_target_pairs={{0,128},{64,192},{128,0},{192,64},{1,129},{65,193},{129,1},{193,65... | collective-permute-start | bytes 983048 | tf_op jit(solution)/shard_map/ppermute | solution.py:22
  21.2 17.7 %collective-permute-start.4 = (bf16[1280,128]{1,0:T(8,128)(2,1)}, bf16[1280,128]{1,0:T(8,128)(2,1)}, u32[]{:S(2)}, u32[]{:S(2)}) collective-permute-start(bf16[1280,128]{1,0:T(8,128)(2,1)} %get-tuple-element.31), channel_id=1, source_target_pairs={{0,192},{64,128},{128,64},{192,0},{1,193},{65,129},{129,65},{193,1... | collective-permute-start | bytes 983048 | tf_op jit(solution)/shard_map/ppermute | solution.py:22
  29.8 10.6 %collective-permute-start.5 = (bf16[768,128]{1,0:T(8,128)(2,1)}, bf16[768,128]{1,0:T(8,128)(2,1)}, u32[]{:S(2)}, u32[]{:S(2)}) collective-permute-start(bf16[768,128]{1,0:T(8,128)(2,1)} %get-tuple-element.32), channel_id=1, source_target_pairs={{0,64},{64,0},{128,192},{192,128},{1,65},{65,1},{129,193},{193,129... | collective-permute-start | bytes 589832 | tf_op jit(solution)/shard_map/ppermute | solution.py:22
  31.7 12.9 %collective-permute-start.6 = (bf16[768,128]{1,0:T(8,128)(2,1)}, bf16[768,128]{1,0:T(8,128)(2,1)S(1)}, u32[]{:S(2)}, u32[]{:S(2)}) collective-permute-start(bf16[768,128]{1,0:T(8,128)(2,1)} %get-tuple-element.33), channel_id=1, source_target_pairs={{0,128},{64,192},{128,0},{192,64},{1,129},{65,193},{129,1},{193,65... | collective-permute-start | bytes 589832 | tf_op jit(solution)/shard_map/ppermute | solution.py:22
  33.4 12.6 %collective-permute-start.7 = (bf16[768,128]{1,0:T(8,128)(2,1)}, bf16[768,128]{1,0:T(8,128)(2,1)}, u32[]{:S(2)}, u32[]{:S(2)}) collective-permute-start(bf16[768,128]{1,0:T(8,128)(2,1)} %get-tuple-element.34), channel_id=1, source_target_pairs={{0,192},{64,128},{128,64},{192,0},{1,193},{65,129},{129,65},{193,1... | collective-permute-start | bytes 589832 | tf_op jit(solution)/shard_map/ppermute | solution.py:22
  49.5 7.3 %copy-start = (bf16[6144,128]{1,0:T(8,128)(2,1)S(1)}, bf16[6144,128]{1,0:T(8,128)(2,1)}, u32[]{:S(2)}) copy-start(bf16[6144,128]{1,0:T(8,128)(2,1)} %get-tuple-element.28.refs_0_) | copy-start | bytes 4718596
  49.6 53.8 %copy-start.1 = (bf16[2048,128]{1,0:T(8,128)(2,1)S(1)}, bf16[2048,128]{1,0:T(8,128)(2,1)}, u32[]{:S(2)}) copy-start(bf16[2048,128]{1,0:T(8,128)(2,1)} %get-tuple-element.40.refs_2_) | copy-start | bytes 1572868
  49.6 2.0 %collective-permute-start.8 = (f32[4,8,24,128]{3,2,1,0:T(8,128)}, f32[4,8,24,128]{3,2,1,0:T(8,128)S(1)}, u32[]{:S(2)}, u32[]{:S(2)}) collective-permute-start(f32[4,8,24,128]{3,2,1,0:T(8,128)} %get-tuple-element.36), channel_id=1, source_target_pairs={{0,1},{1,0},{2,3},{3,2},{4,5},{5,4},{6,7},{7,6},{8,9},{9,8},{10,11... | collective-permute-start | bytes 1179656 | tf_op jit(solution)/shard_map/ppermute | solution.py:26
  52.7 7.2 %collective-permute-start.9 = (f32[8,24,128]{2,1,0:T(8,128)S(1)}, f32[8,24,128]{2,1,0:T(8,128)S(1)}, u32[]{:S(2)}, u32[]{:S(2)}) collective-permute-start(f32[8,24,128]{2,1,0:T(8,128)S(1)} %get-tuple-element.47), channel_id=1, source_target_pairs={{0,2},{1,3},{2,0},{3,1},{4,6},{5,7},{6,4},{7,5},{8,10},{9,11},{10,... | collective-permute-start | bytes 294920 | tf_op jit(solution)/shard_map/ppermute | solution.py:31
  52.8 7.1 %collective-permute-start.11 = (f32[8,24,128]{2,1,0:T(8,128)S(1)}, f32[8,24,128]{2,1,0:T(8,128)S(1)}, u32[]{:S(2)}, u32[]{:S(2)}) collective-permute-start(f32[8,24,128]{2,1,0:T(8,128)S(1)} %get-tuple-element.48), channel_id=1, source_target_pairs={{0,6},{1,7},{2,4},{3,5},{4,2},{5,3},{6,0},{7,1},{8,14},{9,15},{10,... | collective-permute-start | bytes 294920 | tf_op jit(solution)/shard_map/ppermute | solution.py:31
  55.6 6.1 %collective-permute-start.10 = (f32[8,24,128]{2,1,0:T(8,128)S(1)}, f32[8,24,128]{2,1,0:T(8,128)S(1)}, u32[]{:S(2)}, u32[]{:S(2)}) collective-permute-start(f32[8,24,128]{2,1,0:T(8,128)S(1)} %get-tuple-element.49), channel_id=1, source_target_pairs={{0,4},{1,5},{2,6},{3,7},{4,0},{5,1},{6,2},{7,3},{8,12},{9,13},{10,... | collective-permute-start | bytes 294920 | tf_op jit(solution)/shard_map/ppermute | solution.py:31
  56.8 121.2 %collective-permute-start.19 = (bf16[6144,128]{1,0:T(8,128)(2,1)S(1)}, bf16[6144,128]{1,0:T(8,128)(2,1)}, u32[]{:S(2)}, u32[]{:S(2)}) collective-permute-start(bf16[6144,128]{1,0:T(8,128)(2,1)S(1)} %copy-done), channel_id=1, source_target_pairs={{0,64},{64,0},{128,192},{192,128},{1,65},{65,1},{129,193},{193,129... | collective-permute-start | bytes 4718600 | tf_op jit(solution)/shard_map/ppermute | solution.py:22
  77.9 5.2 %collective-permute-start.14 = (f32[24,128]{1,0:T(8,128)S(1)}, f32[24,128]{1,0:T(8,128)S(1)}, u32[]{:S(2)}, u32[]{:S(2)}) collective-permute-start(f32[24,128]{1,0:T(8,128)S(1)} %reduce_sum.9), channel_id=1, source_target_pairs={{0,192},{64,128},{128,64},{192,0},{1,193},{65,129},{129,65},{193,1... | collective-permute-start | bytes 36872 | tf_op jit(solution)/shard_map/ppermute | solution.py:22
  78.5 14.9 %collective-permute-start.13 = (f32[24,128]{1,0:T(8,128)S(1)}, f32[24,128]{1,0:T(8,128)S(1)}, u32[]{:S(2)}, u32[]{:S(2)}) collective-permute-start(f32[24,128]{1,0:T(8,128)S(1)} %reduce_sum.9), channel_id=1, source_target_pairs={{0,128},{64,192},{128,0},{192,64},{1,129},{65,193},{129,1},{193,65... | collective-permute-start | bytes 36872 | tf_op jit(solution)/shard_map/ppermute | solution.py:22
  83.0 11.2 %collective-permute-start.12 = (f32[24,128]{1,0:T(8,128)S(1)}, f32[24,128]{1,0:T(8,128)S(1)}, u32[]{:S(2)}, u32[]{:S(2)}) collective-permute-start(f32[24,128]{1,0:T(8,128)S(1)} %reduce_sum.9), channel_id=1, source_target_pairs={{0,64},{64,0},{128,192},{192,128},{1,65},{65,1},{129,193},{193,129... | collective-permute-start | bytes 36872 | tf_op jit(solution)/shard_map/ppermute | solution.py:22
  94.9 17.2 %all-to-all-start.1 = ((f32[8,24,128]{2,1,0:T(8,128)}), f32[8,24,128]{2,1,0:T(8,128)S(1)}, u32[]{:S(2)}, u32[]{:S(2)}) async-start(f32[8,24,128]{2,1,0:T(8,128)} %broadcast_in_dim.3), calls=%async_computation.1 | async-start | bytes 196608 | tf_op jit(solution)/shard_map/all_to_all | solution.py:35
  103.4 44.6 %collective-permute-start.21 = (bf16[2048,128]{1,0:T(8,128)(2,1)S(1)}, bf16[2048,128]{1,0:T(8,128)(2,1)}, u32[]{:S(2)}, u32[]{:S(2)}) collective-permute-start(bf16[2048,128]{1,0:T(8,128)(2,1)S(1)} %copy-done.1), channel_id=1, source_target_pairs={{0,192},{64,128},{128,64},{192,0},{1,193},{65,129},{129,65},{193,1... | collective-permute-start | bytes 1572872 | tf_op jit(solution)/shard_map/ppermute | solution.py:22
  104.8 73.2 %collective-permute-start.20 = (bf16[4096,128]{1,0:T(8,128)(2,1)}, bf16[4096,128]{1,0:T(8,128)(2,1)}, u32[]{:S(2)}, u32[]{:S(2)}) collective-permute-start(bf16[4096,128]{1,0:T(8,128)(2,1)} %get-tuple-element.39.refs_1_), channel_id=1, source_target_pairs={{0,192},{64,128},{128,64},{192,0},{1,193},{65,129},{129,65},{193,1... | collective-permute-start | bytes 3145736 | tf_op jit(solution)/shard_map/ppermute | solution.py:22
  112.1 4.7 %collective-permute-start.17 = (f32[8,24,128]{2,1,0:T(8,128)S(1)}, f32[8,24,128]{2,1,0:T(8,128)S(1)}, u32[]{:S(2)}, u32[]{:S(2)}) collective-permute-start(f32[8,24,128]{2,1,0:T(8,128)S(1)} %all-to-all-done.1), channel_id=1, source_target_pairs={{0,6},{1,7},{2,4},{3,5},{4,2},{5,3},{6,0},{7,1},{8,14},{9,15},{10,... | collective-permute-start | bytes 294920 | tf_op jit(solution)/shard_map/ppermute | solution.py:31
  113.4 7.1 %collective-permute-start.16 = (f32[8,24,128]{2,1,0:T(8,128)S(1)}, f32[8,24,128]{2,1,0:T(8,128)S(1)}, u32[]{:S(2)}, u32[]{:S(2)}) collective-permute-start(f32[8,24,128]{2,1,0:T(8,128)S(1)} %all-to-all-done.1), channel_id=1, source_target_pairs={{0,4},{1,5},{2,6},{3,7},{4,0},{5,1},{6,2},{7,3},{8,12},{9,13},{10,... | collective-permute-start | bytes 294920 | tf_op jit(solution)/shard_map/ppermute | solution.py:31
  116.8 28.5 %collective-permute-start.25 = (bf16[1280,128]{1,0:T(8,128)(2,1)}, bf16[1280,128]{1,0:T(8,128)(2,1)S(1)}, u32[]{:S(2)}, u32[]{:S(2)}) collective-permute-start(bf16[1280,128]{1,0:T(8,128)(2,1)} %collective-permute-done.2.refs_1_.refs_3_), channel_id=1, source_target_pairs={{0,192},{64,128},{128,64},{192,0},{1,193},{65,129},{129,65},{193,1... | collective-permute-start | bytes 983048 | tf_op jit(solution)/shard_map/ppermute | solution.py:22
  120.4 4.6 %collective-permute-start.15 = (f32[8,24,128]{2,1,0:T(8,128)S(1)}, f32[8,24,128]{2,1,0:T(8,128)S(1)}, u32[]{:S(2)}, u32[]{:S(2)}) collective-permute-start(f32[8,24,128]{2,1,0:T(8,128)S(1)} %all-to-all-done.1), channel_id=1, source_target_pairs={{0,2},{1,3},{2,0},{3,1},{4,6},{5,7},{6,4},{7,5},{8,10},{9,11},{10,... | collective-permute-start | bytes 294920 | tf_op jit(solution)/shard_map/ppermute | solution.py:31
  125.1 36.5 %copy-start.2 = (f32[4,8,24,128]{3,2,1,0:T(8,128)}, f32[4,8,24,128]{3,2,1,0:T(8,128)S(1)}, u32[]{:S(2)}) copy-start(f32[4,8,24,128]{3,2,1,0:T(8,128)S(1)} %pad_maximum_fusion.own_hbm) | copy-start | bytes 1179652
  125.1 33.1 %collective-permute-start.18 = (f32[4,8,24,128]{3,2,1,0:T(8,128)S(1)}, f32[4,8,24,128]{3,2,1,0:T(8,128)S(1)}, u32[]{:S(2)}, u32[]{:S(2)}) collective-permute-start(f32[4,8,24,128]{3,2,1,0:T(8,128)S(1)} %pad_maximum_fusion.own_hbm), channel_id=1, source_target_pairs={{0,1},{1,0},{2,3},{3,2},{4,5},{5,4},{6,7},{7,6},{8,9},{9,8},{10,11... | collective-permute-start | bytes 1179656 | tf_op jit(solution)/shard_map/ppermute | solution.py:26
  145.3 12.9 %copy-start.3 = (bf16[1280,128]{1,0:T(8,128)(2,1)}, bf16[1280,128]{1,0:T(8,128)(2,1)S(1)}, u32[]{:S(2)}) copy-start(bf16[1280,128]{1,0:T(8,128)(2,1)S(1)} %collective-permute-done.25.refs_15_) | copy-start | bytes 983044
  145.3 11.4 %collective-permute-start.22 = (bf16[1280,128]{1,0:T(8,128)(2,1)}, bf16[1280,128]{1,0:T(8,128)(2,1)S(1)}, u32[]{:S(2)}, u32[]{:S(2)}) collective-permute-start(bf16[1280,128]{1,0:T(8,128)(2,1)} %collective-permute-done.4.refs_3_.refs_5_), channel_id=1, source_target_pairs={{0,64},{64,0},{128,192},{192,128},{1,65},{65,1},{129,193},{193,129... | collective-permute-start | bytes 983048 | tf_op jit(solution)/shard_map/ppermute | solution.py:22
  148.0 30.0 %collective-permute-start.24 = (bf16[2048,128]{1,0:T(8,128)(2,1)}, bf16[2048,128]{1,0:T(8,128)(2,1)}, u32[]{:S(2)}, u32[]{:S(2)}) collective-permute-start(bf16[2048,128]{1,0:T(8,128)(2,1)} %collective-permute-done.21.refs_11_), channel_id=1, source_target_pairs={{0,64},{64,0},{128,192},{192,128},{1,65},{65,1},{129,193},{193,129... | collective-permute-start | bytes 1572872 | tf_op jit(solution)/shard_map/ppermute | solution.py:22
  156.8 21.2 %collective-permute-start.26 = (bf16[768,128]{1,0:T(8,128)(2,1)}, bf16[768,128]{1,0:T(8,128)(2,1)}, u32[]{:S(2)}, u32[]{:S(2)}) collective-permute-start(bf16[768,128]{1,0:T(8,128)(2,1)} %collective-permute-done.5.refs_4_.refs_6_), channel_id=1, source_target_pairs={{0,192},{64,128},{128,64},{192,0},{1,193},{65,129},{129,65},{193,1... | collective-permute-start | bytes 589832 | tf_op jit(solution)/shard_map/ppermute | solution.py:22
  158.9 19.1 %collective-permute-start.23 = (bf16[768,128]{1,0:T(8,128)(2,1)}, bf16[768,128]{1,0:T(8,128)(2,1)}, u32[]{:S(2)}, u32[]{:S(2)}) collective-permute-start(bf16[768,128]{1,0:T(8,128)(2,1)} %collective-permute-done.7.refs_6_.refs_8_), channel_id=1, source_target_pairs={{0,64},{64,0},{128,192},{192,128},{1,65},{65,1},{129,193},{193,129... | collective-permute-start | bytes 589832 | tf_op jit(solution)/shard_map/ppermute | solution.py:22
  (3 other events, 3.6 us)

commit v7 on v5

--- a/solution.py
+++ b/solution.py
@@ -553,9 +553,9 @@
     for j in range(4):
         for copy in loads[j]:
             copy.wait()
-        for r in range(16):
-            both = jnp.dot(wide[j, 128 * r : 128 * r + 128], mix, preferred_element_type=jnp.float32)
-            done[j, r] = (both[:, :128] + both[:, 128:]).astype(jnp.bfloat16)
+        for r in range(0, 16, 4):
+            both = jnp.dot(wide[j, 128 * r : 128 * r + 512], mix, preferred_element_type=jnp.float32)
+            done[j, r : r + 4] = (both[:, :128] + both[:, 128:]).astype(jnp.bfloat16).reshape(4, GROUP, LANES)
         columns = pl.ds(pl.multiple_of((me ^ j) * GROUP, GROUP), GROUP)
         for n, (source, target, size) in enumerate(((0, 3, 10), (10, 0, 3), (13, 13, 3))):
             copy = pltpu.make_async_copy(

time: 173 us -> 173 us (level)
  no operation moved by 1% of the time
where the time goes in v7:
time: 173 us
  waiting for transfers between devices  63.4 us (37%)
  Pallas kernels  44 us (25%)
  starting transfers between devices  32.1 us (19%)
  blocking collectives  27 us (16%)
  local copies, waits for them, and re-layouts  4.06 us (2%)
    ppermute x17, waiting for transfers between devices, case_swap(): lax.ppermute(value, 'case', [(source, source ^ apart) for source in range...  50.8 us
    all_to_all x1, blocking collectives, plane_exchange(): return lax.all_to_all(value, 'tile', 0, 0, axis_index_groups=PLANES)  27 us
    ppermute x17, starting transfers between devices, case_swap(): lax.ppermute(value, 'case', [(source, source ^ apart) for source in range...  23.7 us
    pallas_call x1, Pallas kernels, mixing_call(): pl.pallas_call(functools.partial(mixing, cells), out_shape=(shape, shape)...  16.4 us
    all_to_all x1, waiting for transfers between devices, plane_exchange(): return lax.all_to_all(value, 'tile', 0, 0, axis_index_groups=PLANES)  10.8 us
    pallas_call x1, Pallas kernels, inner_call(): pl.pallas_call(inner_rows, out_shape=[half(INNER)] * 3 + [half(3 * PIECE)...  9.37 us
    pallas_call x1, Pallas kernels, outer_call(): pl.pallas_call(outer_rows, out_shape=[half(OUTER)] * 3 + [half(3 * PIECE)...  8.12 us
    pallas_call x1, Pallas kernels, finish_call(): pl.pallas_call(functools.partial(finish, plan), out_shape=jax.ShapeDtypeS...  6.53 us
  transfers between devices with their start and end apart: 22, of which 10 were waited for; matrix products, arithmetic and copies ran while one was open for 1% of the time, Pallas kernels for 20%

profile of v7, /device:TPU:2, one launch (start us, length us, event | category | flops | bytes accessed | tf_op | source)
XLA Modules:
  0.0 172.7 jit_solution(13341998199633317541)
XLA Ops:
  0.8 1.2 fusion
  2.2 2.5 %collective-permute-start = (bf16[1568,128]{1,0:T(8,128)(2,1)S(1)}, bf16[1568,128]{1,0:T(8,128)(2,1)}, u32[]{:S(2)}, u32[]{:S(2)}) collective-permute-start(bf16[1568,128]{1,0:T(8,128)(2,1)S(1)} %concatenate.6), channel_id=1, source_target_pairs={{0,1},{1,2},{2,3},{3,4},{4,5},{5,6},{6,7},{7,8},{8,9},{9,10},{10,1... | collective-permute-start | bytes 1204232 | tf_op jit(solution)/shard_map/ppermute | solution.py:602
  5.1 1.3 collective-permute-start.1
  7.0 9.4 %shard_map.46 = (bf16[1280,128]{1,0:T(8,128)(2,1)}, bf16[1280,128]{1,0:T(8,128)(2,1)}, bf16[1280,128]{1,0:T(8,128)(2,1)}, bf16[6144,128]{1,0:T(8,128)(2,1)}, bf1...) custom-call(s32[1]{0:T(128)} %bitcast.me_ref, ...), custom_call_target="tpu_custom_call" | custom-call | flops 419430400 | bytes 9437184 | tf_op jit(solution)/shard_map/pallas_call | solution.py:434
  16.4 1.9 %collective-permute-start.2 = (bf16[1280,128]{1,0:T(8,128)(2,1)}, bf16[1280,128]{1,0:T(8,128)(2,1)}, u32[]{:S(2)}, u32[]{:S(2)}) collective-permute-start(bf16[1280,128]{1,0:T(8,128)(2,1)} %get-tuple-element.29), channel_id=1, source_target_pairs={{0,64},{64,0},{128,192},{192,128},{1,65},{65,1},{129,193},{193,129... | collective-permute-start | bytes 983048 | tf_op jit(solution)/shard_map/ppermute | solution.py:22
  18.3 1.2 collective-permute-start.3
  20.0 8.1 %shard_map.47 = (bf16[768,128]{1,0:T(8,128)(2,1)}, bf16[768,128]{1,0:T(8,128)(2,1)}, bf16[768,128]{1,0:T(8,128)(2,1)}, bf16[6144,128]{1,0:T(8,128)(2,1)}, bf16[4...) custom-call(s32[1]{0:T(128)} %bitcast.me_ref, ...), custom_call_target="tpu_custom_call", output_to_operand_aliasing={{3}: (9, {}), {4}: (10, {}), {5}: (11, {})} | custom-call | flops 209715200 | bytes 9437184 | tf_op jit(solution)/shard_map/pallas_call | solution.py:449
  28.1 3.1 %collective-permute-start.5 = (bf16[768,128]{1,0:T(8,128)(2,1)}, bf16[768,128]{1,0:T(8,128)(2,1)}, u32[]{:S(2)}, u32[]{:S(2)}) collective-permute-start(bf16[768,128]{1,0:T(8,128)(2,1)} %get-tuple-element.32), channel_id=1, source_target_pairs={{0,64},{64,0},{128,192},{192,128},{1,65},{65,1},{129,193},{193,129... | collective-permute-start | bytes 589832 | tf_op jit(solution)/shard_map/ppermute | solution.py:22
  31.6 1.1 collective-permute-start.7
  32.8 1.9 %collective-permute-done.3.refs_2_.refs_4_ = bf16[1280,128]{1,0:T(8,128)(2,1)} collective-permute-done((bf16[1280,128]{1,0:T(8,128)(2,1)}, bf16[1280,128]{1,0:T(8,128)(2,1)}, u32[]{:S(2)}, u32[]{:S(2)}) %collective-permute-start.3) | collective-permute-done | bytes 327712 | tf_op jit(solution)/shard_map/ppermute | solution.py:22
  34.7 2.5 %collective-permute-done.4.refs_3_.refs_5_ = bf16[1280,128]{1,0:T(8,128)(2,1)} collective-permute-done((bf16[1280,128]{1,0:T(8,128)(2,1)}, bf16[1280,128]{1,0:T(8,128)(2,1)}, u32[]{:S(2)}, u32[]{:S(2)}) %collective-permute-start.4) | collective-permute-done | bytes 327712 | tf_op jit(solution)/shard_map/ppermute | solution.py:22
  37.1 0.7 collective-permute-done.5.refs_4_.refs_6_
  37.9 5.1 %collective-permute-done.6.refs_5_.refs_7_ = bf16[768,128]{1,0:T(8,128)(2,1)S(1)} collective-permute-done((bf16[768,128]{1,0:T(8,128)(2,1)}, bf16[768,128]{1,0:T(8,128)(2,1)S(1)}, u32[]{:S(2)}, u32[]{:S(2)}) %collective-permute-start.6) | collective-permute-done | bytes 196640 | tf_op jit(solution)/shard_map/ppermute | solution.py:22
  43.0 2.5 %collective-permute-done.7.refs_6_.refs_8_ = bf16[768,128]{1,0:T(8,128)(2,1)} collective-permute-done((bf16[768,128]{1,0:T(8,128)(2,1)}, bf16[768,128]{1,0:T(8,128)(2,1)}, u32[]{:S(2)}, u32[]{:S(2)}) %collective-permute-start.7) | collective-permute-done | bytes 196640 | tf_op jit(solution)/shard_map/ppermute | solution.py:22
  45.6 3.5 %shard_map.48 = (f32[32,24,128]{2,1,0:T(8,128)}, f32[32,24,128]{2,1,0:T(8,128)}) custom-call(s32[1]{0:T(128)} %bitcast.me_ref, s32[1]{0:T(128)S(6)} %and.5.core_ref, bf16[6144,128]{1,0:T(8,128)(2,1)} %get-tuple-element.28.refs_0_, bf16[1280,128]{1,0:T(8,128)(2,1)} %collective-permute-done.2.refs_1_.refs_3_, ...), custom_call_target="tpu_custom_call" | custom-call | flops 1073741824 | bytes 3145728 | tf_op jit(solution)/shard_map/pallas_call | solution.py:505
  49.3 1.8 %collective-permute-done.8 = f32[32,24,128]{2,1,0:T(8,128)S(1)} collective-permute-done((f32[32,24,128]{2,1,0:T(8,128)}, f32[32,24,128]{2,1,0:T(8,128)S(1)}, u32[]{:S(2)}, u32[]{:S(2)}) %collective-permute-start.8) | collective-permute-done | bytes 393248 | tf_op jit(solution)/shard_map/ppermute | solution.py:26
  51.1 1.1 add.12
  52.2 27.0 %all_to_all.10 = f32[32,24,128]{2,1,0:T(8,128)S(1)} all-to-all(f32[32,24,128]{2,1,0:T(8,128)S(1)} %add.12), channel_id=1, replica_groups={{0,2,4,6,8,10,12,14,16,18,20,22,24,26,28,30,32,34,36,38,40,42,44,46,48,..., dimensions={0} | all-to-all | bytes 786432 | tf_op jit(solution)/shard_map/all_to_all | solution.py:30
  79.9 4.5 %collective-permute-start.10 = (f32[24,128]{1,0:T(8,128)S(1)}, f32[24,128]{1,0:T(8,128)S(1)}, u32[]{:S(2)}, u32[]{:S(2)}) collective-permute-start(f32[24,128]{1,0:T(8,128)S(1)} %reduce_sum.9), channel_id=1, source_target_pairs={{0,128},{64,192},{128,0},{192,64},{1,129},{65,193},{129,1},{193,65... | collective-permute-start | bytes 36872 | tf_op jit(solution)/shard_map/ppermute | solution.py:22
  84.5 2.0 %collective-permute-start.13 = (bf16[6144,128]{1,0:T(8,128)(2,1)S(1)}, bf16[6144,128]{1,0:T(8,128)(2,1)}, u32[]{:S(2)}, u32[]{:S(2)}) collective-permute-start(bf16[6144,128]{1,0:T(8,128)(2,1)S(1)} %copy-done), channel_id=1, source_target_pairs={{0,64},{64,0},{128,192},{192,128},{1,65},{65,1},{129,193},{193,129... | collective-permute-start | bytes 4718600 | tf_op jit(solution)/shard_map/ppermute | solution.py:22
  86.5 1.8 %collective-permute-done.9 = f32[24,128]{1,0:T(8,128)S(1)} collective-permute-done((f32[24,128]{1,0:T(8,128)S(1)}, f32[24,128]{1,0:T(8,128)S(1)}, u32[]{:S(2)}, u32[]{:S(2)}) %collective-permute-start.9) | collective-permute-done | bytes 12320 | tf_op jit(solution)/shard_map/ppermute | solution.py:22
  88.3 0.8 broadcast_in_dim.3
  89.1 4.3 %all-to-all-start.1 = ((f32[32,24,128]{2,1,0:T(8,128)}), f32[32,24,128]{2,1,0:T(8,128)S(1)}, u32[]{:S(2)}, u32[]{:S(2)}) async-start(f32[32,24,128]{2,1,0:T(8,128)} %broadcast_in_dim.3), calls=%async_computation.1 | async-start | bytes 786432 | tf_op jit(solution)/shard_map/all_to_all | solution.py:30
  93.5 2.0 %collective-permute-start.14 = (bf16[4096,128]{1,0:T(8,128)(2,1)}, bf16[4096,128]{1,0:T(8,128)(2,1)}, u32[]{:S(2)}, u32[]{:S(2)}) collective-permute-start(bf16[4096,128]{1,0:T(8,128)(2,1)} %get-tuple-element.39.refs_1_), channel_id=1, source_target_pairs={{0,192},{64,128},{128,64},{192,0},{1,193},{65,129},{129,65},{193,1... | collective-permute-start | bytes 3145736 | tf_op jit(solution)/shard_map/ppermute | solution.py:22
  95.6 10.8 %all-to-all-done.1.own_hbm = f32[32,24,128]{2,1,0:T(8,128)S(1)} async-done(((f32[32,24,128]{2,1,0:T(8,128)}), f32[32,24,128]{2,1,0:T(8,128)S(1)}, u32[]{:S(2)}, u32[]{:S(2)}) %all-to-all-start.1) | async-done | bytes 393248 | tf_op jit(solution)/shard_map/all_to_all | solution.py:30
  106.4 27.5 %collective-permute-done.19.refs_15_ = bf16[1280,128]{1,0:T(8,128)(2,1)S(1)} collective-permute-done((bf16[1280,128]{1,0:T(8,128)(2,1)}, bf16[1280,128]{1,0:T(8,128)(2,1)S(1)}, u32[]{:S(2)}, u32[]{:S(2)}) %collective-permute-start.19) | collective-permute-done | bytes 327712 | tf_op jit(solution)/shard_map/ppermute | solution.py:22
  133.9 1.8 %collective-permute-start.16 = (bf16[1280,128]{1,0:T(8,128)(2,1)}, bf16[1280,128]{1,0:T(8,128)(2,1)S(1)}, u32[]{:S(2)}, u32[]{:S(2)}) collective-permute-start(bf16[1280,128]{1,0:T(8,128)(2,1)} %collective-permute-done.4.refs_3_.refs_5_), channel_id=1, source_target_pairs={{0,64},{64,0},{128,192},{192,128},{1,65},{65,1},{129,193},{193,129... | collective-permute-start | bytes 983048 | tf_op jit(solution)/shard_map/ppermute | solution.py:22
  135.9 8.8 %collective-permute-done.16.refs_12_ = bf16[1280,128]{1,0:T(8,128)(2,1)S(1)} collective-permute-done((bf16[1280,128]{1,0:T(8,128)(2,1)}, bf16[1280,128]{1,0:T(8,128)(2,1)S(1)}, u32[]{:S(2)}, u32[]{:S(2)}) %collective-permute-start.16) | collective-permute-done | bytes 327712 | tf_op jit(solution)/shard_map/ppermute | solution.py:22
  144.7 1.5 collective-permute-start.20
  146.9 2.6 %collective-permute-start.17 = (bf16[768,128]{1,0:T(8,128)(2,1)}, bf16[768,128]{1,0:T(8,128)(2,1)}, u32[]{:S(2)}, u32[]{:S(2)}) collective-permute-start(bf16[768,128]{1,0:T(8,128)(2,1)} %collective-permute-done.7.refs_6_.refs_8_), channel_id=1, source_target_pairs={{0,64},{64,0},{128,192},{192,128},{1,65},{65,1},{129,193},{193,129... | collective-permute-start | bytes 589832 | tf_op jit(solution)/shard_map/ppermute | solution.py:22
  149.5 16.4 %shard_map.49 = (bf16[512,128]{1,0:T(8,128)(2,1)}, bf16[512,128]{1,0:T(8,128)(2,1)}) custom-call(s32[1]{0:T(128)} %bitcast.me_ref, s32[1]{0:T(128)S(6)} %and.5.core_ref, f32[32,24,128]{2,1,0:T(8,128)} %copy-done.2, f32[32,24,128]{2,1,0:T(8,128)} %copy-done.6, s32[2,256,128]{2,1,0:T(8,128)} %start_ref.1), custom_call_target="tpu_custom_call" | custom-call | flops 1073741824 | bytes 1048576 | tf_op jit(solution)/shard_map/pallas_call | solution.py:520
  166.0 6.5 %shard_map.50 = bf16[16,512,128]{2,1,0:T(8,128)(2,1)} custom-call(s32[1]{0:T(128)} %bitcast.me_ref, bf16[512,128]{1,0:T(8,128)(2,1)} %get-tuple-element.37.high_ref, bf16[512,128]{1,0:T(8,128)(2,1)} %get-tuple-element.38.low_ref, bf16[6144,128]{1,0:T(8,128)(2,1)} %get-tuple-element.28.refs_0_, bf16[4096,128]{1,0:T(8,128)(2,1)} %get-tuple-element.39.refs_1_, ...), custom_call_target="tpu_custom_call" | custom-call | flops 2147483648 | bytes 10485760 | tf_op jit(solution)/shard_map/pallas_call | solution.py:571
  (45 shorter events, 4.4 us)
Async XLA Ops:
  2.2 17.7 %collective-permute-start = (bf16[1568,128]{1,0:T(8,128)(2,1)S(1)}, bf16[1568,128]{1,0:T(8,128)(2,1)}, u32[]{:S(2)}, u32[]{:S(2)}) collective-permute-start(bf16[1568,128]{1,0:T(8,128)(2,1)S(1)} %concatenate.6), channel_id=1, source_target_pairs={{0,1},{1,2},{2,3},{3,4},{4,5},{5,6},{6,7},{7,8},{8,9},{9,10},{10,1... | collective-permute-start | bytes 1204232 | tf_op jit(solution)/shard_map/ppermute | solution.py:602
  5.1 14.9 %collective-permute-start.1 = (bf16[1568,128]{1,0:T(8,128)(2,1)S(1)}, bf16[1568,128]{1,0:T(8,128)(2,1)}, u32[]{:S(2)}, u32[]{:S(2)}) collective-permute-start(bf16[1568,128]{1,0:T(8,128)(2,1)S(1)} %concatenate.7), channel_id=1, source_target_pairs={{1,0},{2,1},{3,2},{4,3},{5,4},{6,5},{7,6},{8,7},{9,8},{10,9},{11,1... | collective-permute-start | bytes 1204232 | tf_op jit(solution)/shard_map/ppermute | solution.py:603
  16.4 15.2 %collective-permute-start.2 = (bf16[1280,128]{1,0:T(8,128)(2,1)}, bf16[1280,128]{1,0:T(8,128)(2,1)}, u32[]{:S(2)}, u32[]{:S(2)}) collective-permute-start(bf16[1280,128]{1,0:T(8,128)(2,1)} %get-tuple-element.29), channel_id=1, source_target_pairs={{0,64},{64,0},{128,192},{192,128},{1,65},{65,1},{129,193},{193,129... | collective-permute-start | bytes 983048 | tf_op jit(solution)/shard_map/ppermute | solution.py:22
  18.3 16.4 %collective-permute-start.3 = (bf16[1280,128]{1,0:T(8,128)(2,1)}, bf16[1280,128]{1,0:T(8,128)(2,1)}, u32[]{:S(2)}, u32[]{:S(2)}) collective-permute-start(bf16[1280,128]{1,0:T(8,128)(2,1)} %get-tuple-element.30), channel_id=1, source_target_pairs={{0,128},{64,192},{128,0},{192,64},{1,129},{65,193},{129,1},{193,65... | collective-permute-start | bytes 983048 | tf_op jit(solution)/shard_map/ppermute | solution.py:22
  19.4 17.7 %collective-permute-start.4 = (bf16[1280,128]{1,0:T(8,128)(2,1)}, bf16[1280,128]{1,0:T(8,128)(2,1)}, u32[]{:S(2)}, u32[]{:S(2)}) collective-permute-start(bf16[1280,128]{1,0:T(8,128)(2,1)} %get-tuple-element.31), channel_id=1, source_target_pairs={{0,192},{64,128},{128,64},{192,0},{1,193},{65,129},{129,65},{193,1... | collective-permute-start | bytes 983048 | tf_op jit(solution)/shard_map/ppermute | solution.py:22
  28.1 9.8 %collective-permute-start.5 = (bf16[768,128]{1,0:T(8,128)(2,1)}, bf16[768,128]{1,0:T(8,128)(2,1)}, u32[]{:S(2)}, u32[]{:S(2)}) collective-permute-start(bf16[768,128]{1,0:T(8,128)(2,1)} %get-tuple-element.32), channel_id=1, source_target_pairs={{0,64},{64,0},{128,192},{192,128},{1,65},{65,1},{129,193},{193,129... | collective-permute-start | bytes 589832 | tf_op jit(solution)/shard_map/ppermute | solution.py:22
  31.2 11.8 %collective-permute-start.6 = (bf16[768,128]{1,0:T(8,128)(2,1)}, bf16[768,128]{1,0:T(8,128)(2,1)S(1)}, u32[]{:S(2)}, u32[]{:S(2)}) collective-permute-start(bf16[768,128]{1,0:T(8,128)(2,1)} %get-tuple-element.33), channel_id=1, source_target_pairs={{0,128},{64,192},{128,0},{192,64},{1,129},{65,193},{129,1},{193,65... | collective-permute-start | bytes 589832 | tf_op jit(solution)/shard_map/ppermute | solution.py:22
  31.6 13.9 %collective-permute-start.7 = (bf16[768,128]{1,0:T(8,128)(2,1)}, bf16[768,128]{1,0:T(8,128)(2,1)}, u32[]{:S(2)}, u32[]{:S(2)}) collective-permute-start(bf16[768,128]{1,0:T(8,128)(2,1)} %get-tuple-element.34), channel_id=1, source_target_pairs={{0,192},{64,128},{128,64},{192,0},{1,193},{65,129},{129,65},{193,1... | collective-permute-start | bytes 589832 | tf_op jit(solution)/shard_map/ppermute | solution.py:22
  43.0 2.5 %copy-start.5 = (bf16[768,128]{1,0:T(8,128)(2,1)}, bf16[768,128]{1,0:T(8,128)(2,1)S(1)}, u32[]{:S(2)}) copy-start(bf16[768,128]{1,0:T(8,128)(2,1)S(1)} %collective-permute-done.6.refs_5_.refs_7_) | copy-start | bytes 589828
  49.1 35.4 %copy-start = (bf16[6144,128]{1,0:T(8,128)(2,1)S(1)}, bf16[6144,128]{1,0:T(8,128)(2,1)}, u32[]{:S(2)}) copy-start(bf16[6144,128]{1,0:T(8,128)(2,1)} %get-tuple-element.28.refs_0_) | copy-start | bytes 4718596
  49.1 2.0 %collective-permute-start.8 = (f32[32,24,128]{2,1,0:T(8,128)}, f32[32,24,128]{2,1,0:T(8,128)S(1)}, u32[]{:S(2)}, u32[]{:S(2)}) collective-permute-start(f32[32,24,128]{2,1,0:T(8,128)} %get-tuple-element.36), channel_id=1, source_target_pairs={{0,1},{1,0},{2,3},{3,2},{4,5},{5,4},{6,7},{7,6},{8,9},{9,8},{10,11... | collective-permute-start | bytes 1179656 | tf_op jit(solution)/shard_map/ppermute | solution.py:26
  51.1 42.3 %copy-start.1 = (bf16[2048,128]{1,0:T(8,128)(2,1)S(1)}, bf16[2048,128]{1,0:T(8,128)(2,1)}, u32[]{:S(2)}) copy-start(bf16[2048,128]{1,0:T(8,128)(2,1)} %get-tuple-element.40.refs_2_) | copy-start | bytes 1572868
  79.3 7.2 %collective-permute-start.11 = (f32[24,128]{1,0:T(8,128)S(1)}, f32[24,128]{1,0:T(8,128)S(1)}, u32[]{:S(2)}, u32[]{:S(2)}) collective-permute-start(f32[24,128]{1,0:T(8,128)S(1)} %reduce_sum.9), channel_id=1, source_target_pairs={{0,192},{64,128},{128,64},{192,0},{1,193},{65,129},{129,65},{193,1... | collective-permute-start | bytes 36872 | tf_op jit(solution)/shard_map/ppermute | solution.py:22
  79.9 6.6 %collective-permute-start.10 = (f32[24,128]{1,0:T(8,128)S(1)}, f32[24,128]{1,0:T(8,128)S(1)}, u32[]{:S(2)}, u32[]{:S(2)}) collective-permute-start(f32[24,128]{1,0:T(8,128)S(1)} %reduce_sum.9), channel_id=1, source_target_pairs={{0,128},{64,192},{128,0},{192,64},{1,129},{65,193},{129,1},{193,65... | collective-permute-start | bytes 36872 | tf_op jit(solution)/shard_map/ppermute | solution.py:22
  84.5 3.8 %collective-permute-start.9 = (f32[24,128]{1,0:T(8,128)S(1)}, f32[24,128]{1,0:T(8,128)S(1)}, u32[]{:S(2)}, u32[]{:S(2)}) collective-permute-start(f32[24,128]{1,0:T(8,128)S(1)} %reduce_sum.9), channel_id=1, source_target_pairs={{0,64},{64,0},{128,192},{192,128},{1,65},{65,1},{129,193},{193,129... | collective-permute-start | bytes 36872 | tf_op jit(solution)/shard_map/ppermute | solution.py:22
  84.5 81.5 %collective-permute-start.13 = (bf16[6144,128]{1,0:T(8,128)(2,1)S(1)}, bf16[6144,128]{1,0:T(8,128)(2,1)}, u32[]{:S(2)}, u32[]{:S(2)}) collective-permute-start(bf16[6144,128]{1,0:T(8,128)(2,1)S(1)} %copy-done), channel_id=1, source_target_pairs={{0,64},{64,0},{128,192},{192,128},{1,65},{65,1},{129,193},{193,129... | collective-permute-start | bytes 4718600 | tf_op jit(solution)/shard_map/ppermute | solution.py:22
  89.1 17.3 %all-to-all-start.1 = ((f32[32,24,128]{2,1,0:T(8,128)}), f32[32,24,128]{2,1,0:T(8,128)S(1)}, u32[]{:S(2)}, u32[]{:S(2)}) async-start(f32[32,24,128]{2,1,0:T(8,128)} %broadcast_in_dim.3), calls=%async_computation.1 | async-start | bytes 786432 | tf_op jit(solution)/shard_map/all_to_all | solution.py:30
  93.4 42.3 %collective-permute-start.15 = (bf16[2048,128]{1,0:T(8,128)(2,1)S(1)}, bf16[2048,128]{1,0:T(8,128)(2,1)}, u32[]{:S(2)}, u32[]{:S(2)}) collective-permute-start(bf16[2048,128]{1,0:T(8,128)(2,1)S(1)} %copy-done.1), channel_id=1, source_target_pairs={{0,192},{64,128},{128,64},{192,0},{1,193},{65,129},{129,65},{193,1... | collective-permute-start | bytes 1572872 | tf_op jit(solution)/shard_map/ppermute | solution.py:22
  93.5 72.5 %collective-permute-start.14 = (bf16[4096,128]{1,0:T(8,128)(2,1)}, bf16[4096,128]{1,0:T(8,128)(2,1)}, u32[]{:S(2)}, u32[]{:S(2)}) collective-permute-start(bf16[4096,128]{1,0:T(8,128)(2,1)} %get-tuple-element.39.refs_1_), channel_id=1, source_target_pairs={{0,192},{64,128},{128,64},{192,0},{1,193},{65,129},{129,65},{193,1... | collective-permute-start | bytes 3145736 | tf_op jit(solution)/shard_map/ppermute | solution.py:22
  95.5 38.4 %collective-permute-start.19 = (bf16[1280,128]{1,0:T(8,128)(2,1)}, bf16[1280,128]{1,0:T(8,128)(2,1)S(1)}, u32[]{:S(2)}, u32[]{:S(2)}) collective-permute-start(bf16[1280,128]{1,0:T(8,128)(2,1)} %collective-permute-done.2.refs_1_.refs_3_), channel_id=1, source_target_pairs={{0,192},{64,128},{128,64},{192,0},{1,193},{65,129},{129,65},{193,1... | collective-permute-start | bytes 983048 | tf_op jit(solution)/shard_map/ppermute | solution.py:22
  106.4 43.1 %copy-start.2 = (f32[32,24,128]{2,1,0:T(8,128)}, f32[32,24,128]{2,1,0:T(8,128)S(1)}, u32[]{:S(2)}) copy-start(f32[32,24,128]{2,1,0:T(8,128)S(1)} %all-to-all-done.1.own_hbm) | copy-start | bytes 1179652
  106.4 39.7 %collective-permute-start.12 = (f32[32,24,128]{2,1,0:T(8,128)S(1)}, f32[32,24,128]{2,1,0:T(8,128)S(1)}, u32[]{:S(2)}, u32[]{:S(2)}) collective-permute-start(f32[32,24,128]{2,1,0:T(8,128)S(1)} %all-to-all-done.1.own_hbm), channel_id=1, source_target_pairs={{0,1},{1,0},{2,3},{3,2},{4,5},{5,4},{6,7},{7,6},{8,9},{9,8},{10,11... | collective-permute-start | bytes 1179656 | tf_op jit(solution)/shard_map/ppermute | solution.py:26
  133.9 12.3 %copy-start.3 = (bf16[1280,128]{1,0:T(8,128)(2,1)}, bf16[1280,128]{1,0:T(8,128)(2,1)S(1)}, u32[]{:S(2)}) copy-start(bf16[1280,128]{1,0:T(8,128)(2,1)S(1)} %collective-permute-done.19.refs_15_) | copy-start | bytes 983044
  133.9 10.8 %collective-permute-start.16 = (bf16[1280,128]{1,0:T(8,128)(2,1)}, bf16[1280,128]{1,0:T(8,128)(2,1)S(1)}, u32[]{:S(2)}, u32[]{:S(2)}) collective-permute-start(bf16[1280,128]{1,0:T(8,128)(2,1)} %collective-permute-done.4.refs_3_.refs_5_), channel_id=1, source_target_pairs={{0,64},{64,0},{128,192},{192,128},{1,65},{65,1},{129,193},{193,129... | collective-permute-start | bytes 983048 | tf_op jit(solution)/shard_map/ppermute | solution.py:22
  135.7 30.2 %collective-permute-start.18 = (bf16[2048,128]{1,0:T(8,128)(2,1)}, bf16[2048,128]{1,0:T(8,128)(2,1)}, u32[]{:S(2)}, u32[]{:S(2)}) collective-permute-start(bf16[2048,128]{1,0:T(8,128)(2,1)} %collective-permute-done.15.refs_11_), channel_id=1, source_target_pairs={{0,64},{64,0},{128,192},{192,128},{1,65},{65,1},{129,193},{193,129... | collective-permute-start | bytes 1572872 | tf_op jit(solution)/shard_map/ppermute | solution.py:22
  144.7 1.5 copy-start.4
  144.7 21.3 %collective-permute-start.20 = (bf16[768,128]{1,0:T(8,128)(2,1)}, bf16[768,128]{1,0:T(8,128)(2,1)}, u32[]{:S(2)}, u32[]{:S(2)}) collective-permute-start(bf16[768,128]{1,0:T(8,128)(2,1)} %collective-permute-done.5.refs_4_.refs_6_), channel_id=1, source_target_pairs={{0,192},{64,128},{128,64},{192,0},{1,193},{65,129},{129,65},{193,1... | collective-permute-start | bytes 589832 | tf_op jit(solution)/shard_map/ppermute | solution.py:22
  146.1 0.7 copy-start.6
  146.9 19.1 %collective-permute-start.17 = (bf16[768,128]{1,0:T(8,128)(2,1)}, bf16[768,128]{1,0:T(8,128)(2,1)}, u32[]{:S(2)}, u32[]{:S(2)}) collective-permute-start(bf16[768,128]{1,0:T(8,128)(2,1)} %collective-permute-done.7.refs_6_.refs_8_), channel_id=1, source_target_pairs={{0,64},{64,0},{128,192},{192,128},{1,65},{65,1},{129,193},{193,129... | collective-permute-start | bytes 589832 | tf_op jit(solution)/shard_map/ppermute | solution.py:22
